TPU v7x, 128 devices: a whole 4x4x4 slice. The times are simulated.
128 devices in a mesh: row: 16 (over z_lo, y, core), col: 8 (over x, z_hi).
Axes of the slice: x: 4, y: 4, z: 4 (z_hi: 2, z_lo: 2; z = z_hi * 2 + z_lo), core: 2. Of those that a mesh axis runs over, the one named last changes fastest.
Arguments:
- pair: bfloat16 [1024, 1024, 128], P('row', 'col'), may hold values from -6 to 6
- ln_gain: float32 [128], replicated, may hold values from 0.1 to 1.9
- ln_bias: float32 [128], replicated, may hold values from -3 to 3
- gate_weight: bfloat16 [128, 512], replicated, may hold values from -0.5 to 0.5
- up_weight: bfloat16 [128, 512], replicated, may hold values from -0.5 to 0.5
- out_weight: bfloat16 [512, 128], replicated, may hold values from -0.25 to 0.25
- head_weight: bfloat16 [128, 64], replicated, may hold values from -1 to 1
- targets: int32 [1024, 1024], P(('row', 'col')), may hold values from 0 to 63
- pair_mask: int32 [1024, 1024], P(('row', 'col')), may hold values 0 or 1
Outputs:
- pair_out: bfloat16 [1024, 1024, 128], P('row', 'col')
- loss: float32 [], replicated
- grad_gain: float32 [128], replicated
- grad_bias: float32 [128], replicated
- grad_gate: float32 [128, 512], replicated
- grad_up: float32 [128, 512], replicated
- grad_out: float32 [512, 128], replicated
- grad_head: float32 [128, 64], replicated
All inputs are finite; a program needn't handle non-finite values. No bound on the sum of `pair_mask` on one device may be relied on, other than what follows from the above.
Results may differ from a plain program's by a relative error of at most 0.001.
The roundings to bfloat16 on the way count: a program that leaves them out, or rounds other values in their place, can miss the bound.
Values may be sent and summed in bfloat16 or wider, within the bound.
No kernel may reach another device: no remote copies, remote signals or barrier semaphores. Data moves between devices by JAX's collectives and lax.ppermute only.
A program may use at most 64 MiB of HBM per device.

v0:
```python
import math

import jax
import jax.numpy as jnp
from jax import lax
from jax.sharding import PartitionSpec as P

EPSILON = 1e-05


def normalize(rows_in, ln_gain, ln_bias):
    values = rows_in.astype(jnp.float32)
    centered = values - jnp.mean(values, axis=-1, keepdims=True)
    variance = jnp.mean(centered * centered, axis=-1, keepdims=True)
    unit_rows = centered * lax.rsqrt(variance + EPSILON)
    normed = (unit_rows * ln_gain + ln_bias).astype(jnp.bfloat16)
    return (unit_rows, normed)


def inner(left, right):
    return lax.dot_general(
        left, right, (((0,), (0,)), ((), ())), preferred_element_type=jnp.float32
    )


def advance(rows_in, ln_gain, ln_bias, gate_weight, up_weight, out_weight):
    unit_rows, normed = normalize(rows_in, ln_gain, ln_bias)
    gate_pre = jnp.dot(normed, gate_weight, preferred_element_type=jnp.float32)
    up_pre = jnp.dot(normed, up_weight, preferred_element_type=jnp.float32)
    hidden = (jax.nn.silu(gate_pre) * up_pre).astype(jnp.bfloat16)
    update = jnp.dot(hidden, out_weight, preferred_element_type=jnp.float32)
    return (rows_in.astype(jnp.float32) + update).astype(jnp.bfloat16)


def retreat(totals, rows_in, grad_rows, ln_gain, ln_bias, gate_weight, up_weight, out_weight):
    unit_rows, normed = normalize(rows_in, ln_gain, ln_bias)
    gate_pre = jnp.dot(normed, gate_weight, preferred_element_type=jnp.float32)
    up_pre = jnp.dot(normed, up_weight, preferred_element_type=jnp.float32)
    squashed = jax.nn.sigmoid(gate_pre)
    silu_val = gate_pre * squashed
    hidden = (silu_val * up_pre).astype(jnp.bfloat16)
    grad_hidden = jnp.dot(grad_rows, out_weight.T, preferred_element_type=jnp.float32)
    grad_gate_pre = (grad_hidden * up_pre * squashed * (1.0 + gate_pre * (1.0 - squashed))).astype(
        jnp.bfloat16
    )
    grad_up_pre = (grad_hidden * silu_val).astype(jnp.bfloat16)
    grad_normed = jnp.dot(
        grad_gate_pre, gate_weight.T, preferred_element_type=jnp.float32
    ) + jnp.dot(grad_up_pre, up_weight.T, preferred_element_type=jnp.float32)
    sum_gain, sum_bias, sum_gate, sum_up, sum_out = totals
    return (
        sum_gain + jnp.sum(grad_normed * unit_rows, axis=0),
        sum_bias + jnp.sum(grad_normed, axis=0),
        sum_gate + inner(normed, grad_gate_pre),
        sum_up + inner(normed, grad_up_pre),
        sum_out + inner(hidden, grad_rows),
    )


def loss_terms(logits, targets, pair_mask):
    bins = logits.shape[-1]
    one_hot = (targets[..., None] == jnp.arange(bins, dtype=jnp.int32)).astype(jnp.float32)
    log_total = jnp.log(jnp.sum(jnp.exp(logits), axis=-1))
    weights_mask = pair_mask.astype(jnp.float32)
    loss_part = jnp.sum(weights_mask * (log_total - jnp.sum(logits * one_hot, axis=-1)))
    soft_probs = jnp.exp(logits - log_total[..., None])
    return (loss_part, soft_probs)


def grad_from(soft_probs, targets, pair_mask, tokens):
    bins = soft_probs.shape[-1]
    one_hot = (targets[..., None] == jnp.arange(bins, dtype=jnp.int32)).astype(jnp.float32)
    weights_mask = pair_mask.astype(jnp.float32)
    return (weights_mask[..., None] * (soft_probs - one_hot) / tokens).astype(jnp.bfloat16)


def shards(
    pair, ln_gain, ln_bias, gate_weight, up_weight, out_weight, head_weight, targets, pair_mask
):
    rows_tile, cols_tile, width = pair.shape
    tokens = cols_tile * lax.axis_size("col")
    block_rows = math.gcd(rows_tile, max(1, 2048 // cols_tile))
    count = rows_tile // block_rows
    blocks = pair.reshape(count, block_rows * cols_tile, width)

    def forward_one(rows_in):
        return advance(rows_in, ln_gain, ln_bias, gate_weight, up_weight, out_weight)

    pair_out = lax.map(forward_one, blocks).reshape(pair.shape)
    rows_pair = lax.all_to_all(pair_out, "col", split_axis=0, concat_axis=1, tiled=True)
    flip_pair = lax.all_to_all(
        jnp.swapaxes(rows_pair, 0, 1), ("row", "col"), split_axis=0, concat_axis=1, tiled=True
    )
    half_rows = jnp.dot(rows_pair, head_weight, preferred_element_type=jnp.float32).astype(
        jnp.bfloat16
    )
    half_flip = jnp.dot(flip_pair, head_weight, preferred_element_type=jnp.float32).astype(
        jnp.bfloat16
    )
    logits = half_rows.astype(jnp.float32) + half_flip.astype(jnp.float32)
    loss_part, soft_probs = loss_terms(logits, targets, pair_mask)
    grad_logits = grad_from(soft_probs, targets, pair_mask, tokens)
    grad_flip = lax.all_to_all(
        jnp.swapaxes(grad_logits, 0, 1), ("row", "col"), split_axis=0, concat_axis=1, tiled=True
    )
    tile_grad, tile_flip = (
        lax.all_to_all(grad_logits, "col", split_axis=1, concat_axis=0, tiled=True),
        lax.all_to_all(grad_flip, "col", split_axis=1, concat_axis=0, tiled=True),
    )
    bins = head_weight.shape[1]
    flat_out = pair_out.reshape(-1, width)
    grad_head = inner(flat_out, tile_grad.reshape(-1, bins)) + inner(
        flat_out, tile_flip.reshape(-1, bins)
    )
    head_back = head_weight.T
    grad_pair = (
        jnp.dot(tile_grad, head_back, preferred_element_type=jnp.float32)
        + jnp.dot(tile_flip, head_back, preferred_element_type=jnp.float32)
    ).astype(jnp.bfloat16)
    grad_blocks = grad_pair.reshape(count, block_rows * cols_tile, width)
    hidden_width = gate_weight.shape[1]
    start = (
        jnp.zeros((width,), jnp.float32),
        jnp.zeros((width,), jnp.float32),
        jnp.zeros((width, hidden_width), jnp.float32),
        jnp.zeros((width, hidden_width), jnp.float32),
        jnp.zeros((hidden_width, width), jnp.float32),
    )

    def backward_one(totals, inputs):
        return (
            retreat(
                totals, inputs[0], inputs[1], ln_gain, ln_bias, gate_weight, up_weight, out_weight
            ),
            None,
        )

    totals, unused = lax.scan(backward_one, start, (blocks, grad_blocks))
    summed = lax.psum(
        (loss_part, totals[0], totals[1], totals[2], totals[3], totals[4], grad_head),
        ("row", "col"),
    )
    loss = summed[0] / (tokens * tokens)
    return (pair_out, loss, summed[1], summed[2], summed[3], summed[4], summed[5], summed[6])


def solution(mesh):
    placed = (
        P("row", "col", None),
        P(),
        P(),
        P(),
        P(),
        P(),
        P(),
        P(("row", "col"), None),
        P(("row", "col"), None),
    )
    return jax.shard_map(
        shards,
        mesh=mesh,
        in_specs=placed,
        out_specs=(P("row", "col", None), P(), P(), P(), P(), P(), P(), P()),
        check_vma=False,
    )
```

profile of v0, /device:TPU:1, one launch (start us, length us, event | category | flops | bytes accessed | tf_op | source)
XLA Modules:
  0.0 416.3 jit_solution(17993143803311774811)
XLA Ops:
  7.2 47.0 %while.29 = (s32[]{:T(128)}, bf16[4,2048,128]{2,1,0:T(8,128)(2,1)}, bf16[4,2048,128]{2,1,0:T(8,128)(2,1)}, f32[128]{0:T(128)}, f32[128]{0:T(128)}, /*index=5*/bf...) while((s32[]{:T(128)}, bf16[4,2048,128]{2,1,0:T(8,128)(2,1)}, ...), condition=%wide.region_3.4_spmd, body=%wide.region_0.3_spmd.sunk | while | flops 817104896 | bytes 21462268 | solution.py:89
  10.2 4.0 fusion.137
  14.2 4.7 %fusion.138 = bf16[4,2048,128]{2,1,0:T(8,128)(2,1)} fusion(bf16[4,2048,128]{2,1,0:T(8,128)(2,1)} %get-tuple-element.382, s32[]{:T(128)S(6)} %copy.70, bf16[512,128]{1,0:T(8,128)(2,1)S(1)} %copy-done.22, f32[2048,512]{1,0:T(8,128)} %fusion.137, bf16[128,512]{1,0:T(8,128)(2,1)S(1)} %copy-done.12, f32[128]{0:T(128)S(1)} %copy-done.17, ...), kind=kOutput, calls=%fused_computation.4.clone.1 | convolution fusion | flops 545521664 | bytes 6047744 | tf_op jit(solution)/shard_map/while/body/eval_jaxpr/dot_general | solution.py:31
  22.0 4.0 fusion.137
  26.0 4.7 %fusion.138 = bf16[4,2048,128]{2,1,0:T(8,128)(2,1)} fusion(bf16[4,2048,128]{2,1,0:T(8,128)(2,1)} %get-tuple-element.382, s32[]{:T(128)S(6)} %copy.70, bf16[512,128]{1,0:T(8,128)(2,1)S(1)} %copy-done.22, f32[2048,512]{1,0:T(8,128)} %fusion.137, bf16[128,512]{1,0:T(8,128)(2,1)S(1)} %copy-done.12, f32[128]{0:T(128)S(1)} %copy-done.17, ...), kind=kOutput, calls=%fused_computation.4.clone.1 | convolution fusion | flops 545521664 | bytes 6047744 | tf_op jit(solution)/shard_map/while/body/eval_jaxpr/dot_general | solution.py:31
  33.7 4.0 fusion.137
  37.7 4.7 %fusion.138 = bf16[4,2048,128]{2,1,0:T(8,128)(2,1)} fusion(bf16[4,2048,128]{2,1,0:T(8,128)(2,1)} %get-tuple-element.382, s32[]{:T(128)S(6)} %copy.70, bf16[512,128]{1,0:T(8,128)(2,1)S(1)} %copy-done.22, f32[2048,512]{1,0:T(8,128)} %fusion.137, bf16[128,512]{1,0:T(8,128)(2,1)S(1)} %copy-done.12, f32[128]{0:T(128)S(1)} %copy-done.17, ...), kind=kOutput, calls=%fused_computation.4.clone.1 | convolution fusion | flops 545521664 | bytes 6047744 | tf_op jit(solution)/shard_map/while/body/eval_jaxpr/dot_general | solution.py:31
  45.4 4.0 fusion.137
  49.4 4.7 %fusion.138 = bf16[4,2048,128]{2,1,0:T(8,128)(2,1)} fusion(bf16[4,2048,128]{2,1,0:T(8,128)(2,1)} %get-tuple-element.382, s32[]{:T(128)S(6)} %copy.70, bf16[512,128]{1,0:T(8,128)(2,1)S(1)} %copy-done.22, f32[2048,512]{1,0:T(8,128)} %fusion.137, bf16[128,512]{1,0:T(8,128)(2,1)S(1)} %copy-done.12, f32[128]{0:T(128)S(1)} %copy-done.17, ...), kind=kOutput, calls=%fused_computation.4.clone.1 | convolution fusion | flops 545521664 | bytes 6047744 | tf_op jit(solution)/shard_map/while/body/eval_jaxpr/dot_general | solution.py:31
  54.2 34.8 %all_to_all.90 = bf16[64,128,128]{2,1,0:T(8,128)(2,1)S(1)} all-to-all(bf16[64,128,128]{2,1,0:T(8,128)(2,1)} %bitcast.213), channel_id=1, replica_groups=mesh['row'=16,'col'=8] {'col'}, dimensions={0} | all-to-all | bytes 4194304 | tf_op jit(solution)/shard_map/all_to_all | solution.py:90
  91.8 8.6 %all-to-all-start.1 = ((bf16[1024,8,128]{2,1,0:T(8,128)(2,1)}), bf16[1024,8,128]{2,1,0:T(8,128)(2,1)}, u32[]{:S(2)}, u32[]{:S(2)}) async-start(bf16[1024,8,128]{2,1,0:T(8,128)(2,1)} %copy.30), calls=%async_computation.1 | async-start | bytes 4194304 | tf_op jit(solution)/shard_map/all_to_all | solution.py:91
  101.2 27.3 %all-to-all-done.1 = bf16[1024,8,128]{2,1,0:T(8,128)(2,1)} async-done(((bf16[1024,8,128]{2,1,0:T(8,128)(2,1)}), bf16[1024,8,128]{2,1,0:T(8,128)(2,1)}, u32[]{:S(2)}, u32[]{:S(2)}) %all-to-all-start.1) | async-done | bytes 2097184 | tf_op jit(solution)/shard_map/all_to_all | solution.py:91
  128.5 2.8 exponential_reduce_fusion
  139.1 6.3 %all-to-all-start.3 = ((bf16[128,2,2048]{2,1,0:T(2,128)(2,1)}), bf16[128,2,2048]{2,1,0:T(2,128)(2,1)}, u32[]{:S(2)}, u32[]{:S(2)}) async-start(bf16[128,2,2048]{2,1,0:T(2,128)(2,1)} %reshape.76), calls=%async_computation.3 | async-start | bytes 2097152 | tf_op jit(solution)/shard_map/all_to_all | solution.py:103
  147.9 2.7 reshape.74
  150.6 12.1 %all-to-all-done.3 = bf16[128,2,2048]{2,1,0:T(2,128)(2,1)} async-done(((bf16[128,2,2048]{2,1,0:T(2,128)(2,1)}), bf16[128,2,2048]{2,1,0:T(2,128)(2,1)}, u32[]{:S(2)}, u32[]{:S(2)}) %all-to-all-start.3) | async-done | bytes 1048608 | tf_op jit(solution)/shard_map/all_to_all | solution.py:103
  162.7 4.6 %all-to-all-start.2 = ((bf16[8,2,32768]{2,1,0:T(2,128)(2,1)}), bf16[8,2,32768]{2,1,0:T(2,128)(2,1)S(1)}, u32[]{:S(2)}, u32[]{:S(2)}) async-start(bf16[8,2,32768]{2,1,0:T(2,128)(2,1)} %reshape.74), calls=%async_computation.2 | async-start | bytes 2097152 | tf_op jit(solution)/shard_map/all_to_all | solution.py:107
  167.3 3.8 reshape.77
  175.5 7.5 %all-to-all-done.2 = bf16[8,2,32768]{2,1,0:T(2,128)(2,1)S(1)} async-done(((bf16[8,2,32768]{2,1,0:T(2,128)(2,1)}), bf16[8,2,32768]{2,1,0:T(2,128)(2,1)S(1)}, u32[]{:S(2)}, u32[]{:S(2)}) %all-to-all-start.2) | async-done | bytes 1048608 | tf_op jit(solution)/shard_map/all_to_all | solution.py:107
  183.0 4.2 %all-to-all-start.4 = ((bf16[8,2,32768]{2,1,0:T(2,128)(2,1)}), bf16[8,2,32768]{2,1,0:T(2,128)(2,1)}, u32[]{:S(2)}, u32[]{:S(2)}) async-start(bf16[8,2,32768]{2,1,0:T(2,128)(2,1)} %reshape.78), calls=%async_computation.4 | async-start | bytes 2097152 | tf_op jit(solution)/shard_map/all_to_all | solution.py:108
  187.4 3.1 reshape.75
  190.5 3.1 copy.33
  195.5 3.9 fusion.79
  199.4 3.5 all-to-all-done.4
  203.0 3.1 reshape.79
  208.0 4.8 %add_convert_fusion = bf16[64,128,128]{2,1,0:T(8,128)(2,1)} fusion(f32[64,128,128]{2,1,0:T(8,128)} %fusion.79, bf16[64,128,64]{1,2,0:T(8,128)(2,1)} %bitcast.225, bf16[128,64]{0,1:T(8,128)(2,1)S(1)} %copy-done), kind=kOutput, calls=%fused_computation.67 | convolution fusion | flops 136314880 | bytes 7356416 | tf_op jit(solution)/shard_map/dot_general | solution.py:118
  212.9 43.0 %while.30 = (s32[]{:T(128)}, f32[128]{0:T(128)S(1)}, f32[128]{0:T(128)S(1)}, f32[128,512]{1,0:T(8,128)S(1)}, f32[128,512]{1,0:T(8,128)S(1)}, /*index=5*/f32[512,...) while((s32[]{:T(128)}, f32[128]{0:T(128)S(1)}, ...), condition=%wide.region_13.14_spmd.clone, body=%wide.region_8.13_spmd.clone.sunk | while | flops 2177501440 | bytes 55328988 | solution.py:138
  256.8 2.7 fusion.75
  259.6 3.1 copy.40
  262.7 2.8 convolution_add_fusion.4
  265.5 64.7 %all-reduce = (f32[]{:T(128)}, f32[128]{0:T(128)}, f32[128]{0:T(128)}, f32[128,64]{0,1:T(8,128)}) all-reduce(f32[]{:T(128)} %get-tuple-element.229, f32[128]{0:T(128)S(1)} %get-tuple-element.122, f32[128]{0:T(128)S(1)} %get-tuple-element.123, f32[128,64]{0,1:T(8,128)S(1)} %convolution_add_fusion.4), channel_id=1, replica_groups=mesh['row'=16,'col'=8] {'row','col'}, use_global_device_ids=true, to_apply=%region_7.8 | all-reduce | flops 8449 | bytes 67592 | tf_op jit(solution)/shard_map/psum | solution.py:139
  330.8 72.6 %all-reduce.4.cloned.1.call-done = (f32[128,512]{1,0:T(8,128)}, f32[128,512]{1,0:T(8,128)}, f32[512,128]{1,0:T(8,128)}) async-done(((f32[128,512]{1,0:T(8,128)}, f32[128,512]{1,0:T(8,128)}, f32[512,128]{1,0:T(8,128)}), (f32[128,512]{1,0:T(8,128)}, f32[128,512]{1,0:T(8,128)}, f32[512,128]{1,0:T(8,128)})) %all-reduce.4.cloned.1.call-update) | async-done | bytes 786448 | tf_op jit(solution)/shard_map/psum | solution.py:139
  (178 shorter events, 82.5 us)
Async XLA Ops:
  7.2 93.2 %copy-start = (bf16[128,64]{0,1:T(8,128)(2,1)S(1)}, bf16[128,64]{0,1:T(8,128)(2,1)}, u32[]{:S(2)}) copy-start(bf16[128,64]{0,1:T(8,128)(2,1)} %param.19) | copy-start | bytes 49156
  10.2 4.0 copy-start.2
  10.2 4.0 copy-start.12
  10.2 4.0 copy-start.15
  10.2 4.0 copy-start.17
  21.9 4.0 copy-start.2
  21.9 4.0 copy-start.12
  21.9 4.0 copy-start.15
  33.6 4.0 copy-start.2
  33.7 4.0 copy-start.12
  33.7 4.0 copy-start.15
  33.7 4.0 copy-start.17
  33.7 4.0 copy-start.22
  45.4 4.0 copy-start.2
  45.4 4.0 copy-start.12
  45.4 4.0 copy-start.15
  91.8 8.6 %copy-start.21 = (s32[8,1024]{1,0:T(8,128)S(1)}, s32[8,1024]{1,0:T(8,128)}, u32[]{:S(2)}) copy-start(s32[8,1024]{1,0:T(8,128)} %param.21) | copy-start | bytes 98308
  91.8 36.7 %all-to-all-start.1 = ((bf16[1024,8,128]{2,1,0:T(8,128)(2,1)}), bf16[1024,8,128]{2,1,0:T(8,128)(2,1)}, u32[]{:S(2)}, u32[]{:S(2)}) async-start(bf16[1024,8,128]{2,1,0:T(8,128)(2,1)} %copy.30), calls=%async_computation.1 | async-start | bytes 4194304 | tf_op jit(solution)/shard_map/all_to_all | solution.py:91
  100.4 28.1 %copy-start.20 = (s32[8,1024]{1,0:T(8,128)S(1)}, s32[8,1024]{1,0:T(8,128)}, u32[]{:S(2)}) copy-start(s32[8,1024]{1,0:T(8,128)} %param.20) | copy-start | bytes 98308
  139.0 6.3 %copy-start.10 = (bf16[8,1024,64]{1,2,0:T(8,128)(2,1)S(1)}, bf16[8,1024,64]{1,2,0:T(8,128)(2,1)}, u32[]{:S(2)}) copy-start(bf16[8,1024,64]{1,2,0:T(8,128)(2,1)} %copy-done.9) | copy-start | bytes 3145732
  139.1 23.7 %all-to-all-start.3 = ((bf16[128,2,2048]{2,1,0:T(2,128)(2,1)}), bf16[128,2,2048]{2,1,0:T(2,128)(2,1)}, u32[]{:S(2)}, u32[]{:S(2)}) async-start(bf16[128,2,2048]{2,1,0:T(2,128)(2,1)} %reshape.76), calls=%async_computation.3 | async-start | bytes 2097152 | tf_op jit(solution)/shard_map/all_to_all | solution.py:103
  162.7 20.3 %all-to-all-start.2 = ((bf16[8,2,32768]{2,1,0:T(2,128)(2,1)}), bf16[8,2,32768]{2,1,0:T(2,128)(2,1)S(1)}, u32[]{:S(2)}, u32[]{:S(2)}) async-start(bf16[8,2,32768]{2,1,0:T(2,128)(2,1)} %reshape.74), calls=%async_computation.2 | async-start | bytes 2097152 | tf_op jit(solution)/shard_map/all_to_all | solution.py:107
  183.0 4.3 %copy-start.11 = (bf16[8,2,32768]{2,1,0:T(2,128)(2,1)}, bf16[8,2,32768]{2,1,0:T(2,128)(2,1)S(1)}, u32[]{:S(2)}) copy-start(bf16[8,2,32768]{2,1,0:T(2,128)(2,1)S(1)} %all-to-all-done.2) | copy-start | bytes 3145732
  183.0 19.9 %all-to-all-start.4 = ((bf16[8,2,32768]{2,1,0:T(2,128)(2,1)}), bf16[8,2,32768]{2,1,0:T(2,128)(2,1)}, u32[]{:S(2)}, u32[]{:S(2)}) async-start(bf16[8,2,32768]{2,1,0:T(2,128)(2,1)} %reshape.78), calls=%async_computation.4 | async-start | bytes 2097152 | tf_op jit(solution)/shard_map/all_to_all | solution.py:108
  187.3 216.1 %all-reduce.4.cloned.1.call-start = ((), (), s32[]{:S(2)}) async-start(), calls=%async_computation.5 | async-start | bytes 1572864 | tf_op jit(solution)/shard_map/psum | solution.py:139
  208.0 4.8 %copy-start.3 = (bf16[4,2048,128]{2,1,0:T(8,128)(2,1)S(1)}, bf16[4,2048,128]{2,1,0:T(8,128)(2,1)}, u32[]{:S(2)}) copy-start(bf16[4,2048,128]{2,1,0:T(8,128)(2,1)} %get-tuple-element.458) | copy-start | bytes 6291460
  208.0 4.8 %copy-start.4 = (bf16[128,512]{1,0:T(8,128)(2,1)S(1)}, bf16[128,512]{1,0:T(8,128)(2,1)}, u32[]{:S(2)}) copy-start(bf16[128,512]{1,0:T(8,128)(2,1)} %get-tuple-element.459) | copy-start | bytes 393220
  208.0 4.8 %copy-start.13 = (bf16[128,512]{1,0:T(8,128)(2,1)S(1)}, bf16[128,512]{1,0:T(8,128)(2,1)}, u32[]{:S(2)}) copy-start(bf16[128,512]{1,0:T(8,128)(2,1)} %get-tuple-element.472) | copy-start | bytes 393220
  208.0 4.8 %copy-start.16 = (f32[128]{0:T(128)S(1)}, f32[128]{0:T(128)}, u32[]{:S(2)}) copy-start(f32[128]{0:T(128)} %get-tuple-element.473) | copy-start | bytes 1540
  208.0 4.8 %copy-start.18 = (f32[128]{0:T(128)S(1)}, f32[128]{0:T(128)}, u32[]{:S(2)}) copy-start(f32[128]{0:T(128)} %get-tuple-element.474) | copy-start | bytes 1540
  208.0 4.8 %copy-start.23 = (bf16[512,128]{1,0:T(8,128)(2,1)S(1)}, bf16[512,128]{1,0:T(8,128)(2,1)}, u32[]{:S(2)}) copy-start(bf16[512,128]{1,0:T(8,128)(2,1)} %get-tuple-element.480) | copy-start | bytes 393220
  262.7 145.7 %copy-start.1 = (bf16[128,64]{0,1:T(8,128)(2,1)S(1)}, bf16[128,64]{0,1:T(8,128)(2,1)}, u32[]{:S(2)}) copy-start(bf16[128,64]{0,1:T(8,128)(2,1)} %param.19) | copy-start | bytes 49156
  (15 other events, 35.2 us)
Sparse Core Ops, SparseCore 0:
  256.9 146.3 all-reduce.3
where the time goes:
time: 418 us; the launch traced here: 416 us
  waiting for transfers between devices  123 us (29%)
  blocking collectives  99.5 us (24%)
  matrix products  88.2 us (21%)
  local copies, waits for them, and re-layouts  46 us (11%)
  starting transfers between devices  23.7 us (6%)
  other arithmetic  18.7 us (4%)
  between operations  16.2 us (4%)
    psum x1, waiting for transfers between devices, shards(): lax.psum((loss_part, totals[0], totals[1], totals[2], totals[3], totals[4...  72.6 us
    psum x1, blocking collectives, shards(): lax.psum((loss_part, totals[0], totals[1], totals[2], totals[3], totals[4...  64.7 us
    all_to_all x1, blocking collectives, shards(): lax.all_to_all(pair_out, 'col', split_axis=0, concat_axis=1, tiled=True)  34.8 us
    all_to_all x1, waiting for transfers between devices, shards(): lax.all_to_all(jnp.swapaxes(rows_pair, 0, 1), ('row', 'col'), split_axis=...  27.3 us
    unnamed x45, local copies, waits for them, and re-layouts  23.8 us
    dot_general x14, matrix products, inner(): lax.dot_general(left, right, (((0,), (0,)), ((), ())), preferred_element_...  19.9 us
    dot_general x4, matrix products, advance(): update = jnp.dot(hidden, out_weight, preferred_element_type=jnp.float32)  18.9 us
    dot_general x4, matrix products, advance(): gate_pre = jnp.dot(normed, gate_weight, preferred_element_type=jnp.float32)  15.9 us
  transfers between devices with their start and end apart: 5, of which 5 were waited for; matrix products, arithmetic and copies ran while one was open for 8% of the time, Pallas kernels for 0%

commit v1 on v0

v1 whole, which is shorter than its diff:
```python
import functools

import jax
import jax.numpy as jnp
from jax import lax
from jax.experimental import pallas as pl
from jax.experimental.pallas import tpu as pltpu
from jax.sharding import PartitionSpec as P

EPSILON = 1e-05
F32 = jnp.float32
BF16 = jnp.bfloat16
AXES = ("row", "col")

SIDE = 64
GROUP = 8
F_COLS = 16
B_GROUPS = 2


def dot(left, right, dims=((1,), (0,))):
    return lax.dot_general(left, right, (dims, ((), ())), preferred_element_type=F32)


def normalize(rows_in, gain, bias):
    values = rows_in.astype(F32)
    centered = values - jnp.mean(values, axis=-1, keepdims=True)
    variance = jnp.mean(centered * centered, axis=-1, keepdims=True)
    unit_rows = centered * lax.rsqrt(variance + EPSILON)
    return unit_rows, (unit_rows * gain + bias).astype(BF16)


def sigmoid(values):
    return 0.5 * jnp.tanh(0.5 * values) + 0.5


def forward_body(which, pair, gain, bias, w_in, w_out, head_two, *rest):
    pair_out, send, wide = rest[-3:]
    hid = w_out.shape[0]
    rows_in = pair[...].reshape(SIDE * F_COLS, 128)
    count = 4
    size = SIDE * F_COLS // count
    for k in range(count):
        part = rows_in[k * size : (k + 1) * size]
        _, normed = normalize(part, gain[...], bias[...])
        gate_pre = dot(normed, w_in[:, :hid])
        up_pre = dot(normed, w_in[:, hid:])
        hidden = (gate_pre * sigmoid(gate_pre) * up_pre).astype(BF16)
        result = (part.astype(F32) + dot(hidden, w_out[...])).astype(BF16)
        pair_out[k * size // F_COLS : (k + 1) * size // F_COLS] = result.reshape(
            size // F_COLS, 1, F_COLS, 128
        )
        wide[k * size : (k + 1) * size, :] = result.astype(F32)
    for grp in range(F_COLS // GROUP):
        left, right = [
            jnp.concatenate(
                [
                    wide[pl.ds(grp * GROUP + shift + a, SIDE, stride=F_COLS), :]
                    for a in range(GROUP // 2)
                ],
                axis=0,
            )
            for shift in (0, GROUP // 2)
        ]
        both = jnp.concatenate([left, right], axis=1).astype(BF16)
        rows = SIDE * GROUP // 2
        send[grp * rows : (grp + 1) * rows, :] = dot(both, head_two[...]).astype(BF16)


def forward_call(which, pair4, gain, bias, w_in, w_out, head_two, partial=None):
    block = pl.BlockSpec((SIDE, 1, F_COLS, 128), lambda g, w: (0, w[0], g, 0))
    whole = lambda a: pl.BlockSpec(a.shape, lambda g, w: (0,) * a.ndim)
    in_specs = [block] + [whole(a) for a in (gain, bias, w_in, w_out, head_two)]
    args = [pair4, gain, bias, w_in, w_out, head_two]
    alias = {}
    if partial is not None:
        in_specs.append(pl.BlockSpec(memory_space=pl.ANY))
        args.append(partial)
        alias = {7: 0}
    steps = SIDE // F_COLS
    rows = SIDE * F_COLS // 2
    return pl.pallas_call(
        forward_body,
        out_shape=(
            jax.ShapeDtypeStruct(pair4.shape, BF16),
            jax.ShapeDtypeStruct((rows * steps, 128), BF16),
        ),
        grid_spec=pltpu.PrefetchScalarGridSpec(
            num_scalar_prefetch=1,
            grid=(steps,),
            in_specs=in_specs,
            out_specs=(block, pl.BlockSpec((rows, 128), lambda g, w: (g, 0))),
            scratch_shapes=[pltpu.VMEM((SIDE * F_COLS, 128), F32)],
        ),
        input_output_aliases=alias,
        compiler_params=pltpu.CompilerParams(dimension_semantics=("arbitrary",)),
        name="forward",
    )(which, *args)


def code_of(word):
    return (jnp.bitwise_and(word, 65535) + 64 * jnp.right_shift(word, 16)).astype(F32).astype(BF16)


def backward_body(
    which, pair, pair_out, mirror, own_code, mirror_code, gain, bias, w_in, w_out, head_two, *rest
):
    if len(rest) > 8:
        earlier, rest = rest[:4], rest[4:]
    else:
        earlier = None
    g_in, g_out, g_head, g_small, s_normed, s_grad_in, s_hidden, s_pair = rest
    hid = w_out.shape[0]
    step = pl.program_id(0)
    rows = SIDE * GROUP // 2

    @pl.when(step == 0)
    def _():
        if earlier is None:
            for ref in (g_in, g_out, g_head, g_small):
                ref[...] = jnp.zeros_like(ref)
        else:
            for ref, old in zip((g_in, g_out, g_head, g_small), earlier):
                ref[...] = old[...]

    lane = lax.broadcasted_iota(jnp.int32, (rows, 128), 1)
    wanted = (jnp.bitwise_and(lane, 63) + 64).astype(F32)
    lane_row = lax.broadcasted_iota(jnp.int32, (128, 128), 0)
    lane_col = lax.broadcasted_iota(jnp.int32, (128, 128), 1)
    same = (lane_row // 64 == lane_col // 64).astype(F32).astype(BF16)
    sum_bins = jnp.concatenate([same, same], axis=0)
    own = code_of(own_code[...])
    other = code_of(mirror_code[...])
    pick_n = lax.broadcasted_iota(jnp.int32, (SIDE, 512), 1)
    pick_k = lax.broadcasted_iota(jnp.int32, (SIDE, 512), 0)
    pick_base = pick_n // 128 + (GROUP // 2) * (jnp.bitwise_and(pick_n, 127) // 64)

    for grp in range(B_GROUPS):
        at = grp * 2 * rows
        x_out = pair_out[grp * GROUP : (grp + 1) * GROUP].reshape(2 * rows, 128)
        both = jnp.concatenate([x_out[:rows], x_out[rows:]], axis=1)
        half = dot(both, head_two[...]).astype(BF16)
        logits = half.astype(F32) + mirror[grp * rows : (grp + 1) * rows, :].astype(F32)
        expo = 0.5 * jnp.exp(logits)
        high = expo.astype(BF16)
        low = (expo - high.astype(F32)).astype(BF16)
        total = dot(jnp.concatenate([high, low], axis=1), sum_bins)
        log_total = jnp.log(total) + 0.6931471805599453
        soft = jnp.exp(logits - log_total)
        pick = (pick_k == pick_base + GROUP * (step * B_GROUPS + grp)).astype(F32).astype(BF16)
        codes = []
        for spread in (dot(own, pick, ((0,), (0,))), dot(other, pick)):
            codes.append(
                jnp.concatenate([spread[:, 128 * a : 128 * (a + 1)] for a in range(4)], axis=0)
            )
        scale = 1.0 / 1024.0
        hit = codes[0] == wanted
        grads = [
            (scale * (jnp.where(c >= 63.5, soft, 0.0) - jnp.where(c == wanted, 1.0, 0.0))).astype(
                BF16
            )
            for c in codes
        ]
        loss_part = jnp.where(hit, log_total - logits, 0.0)
        grad_both = jnp.concatenate(grads, axis=1)
        g_head[...] += dot(both, grad_both, ((0,), (0,)))
        head_rows = jnp.concatenate([head_two[...], head_two[...]], axis=1)
        grad_pair = dot(grad_both, head_rows, ((1,), (1,))).astype(BF16)
        grad_pair = jnp.concatenate([grad_pair[:, :128], grad_pair[:, 128:]], axis=0)
        s_pair[at : at + 2 * rows, :] = grad_pair

        x_in = pair[grp * GROUP : (grp + 1) * GROUP].reshape(2 * rows, 128)
        unit_rows, normed = normalize(x_in, gain[...], bias[...])
        s_normed[at : at + 2 * rows, :] = normed
        gate_pre = dot(normed, w_in[:, :hid])
        up_pre = dot(normed, w_in[:, hid:])
        grad_hidden = dot(grad_pair, w_out[...], ((1,), (1,)))
        squashed = sigmoid(gate_pre)
        silu_val = gate_pre * squashed
        s_hidden[at : at + 2 * rows, :] = (silu_val * up_pre).astype(BF16)
        slope = squashed * (1.0 + gate_pre * (1.0 - squashed))
        s_grad_in[at : at + 2 * rows, :hid] = (grad_hidden * up_pre * slope).astype(BF16)
        s_grad_in[at : at + 2 * rows, hid:] = (grad_hidden * silu_val).astype(BF16)
        grad_normed = dot(s_grad_in[at : at + 2 * rows, :], w_in[...], ((1,), (1,)))
        fold = lambda v: jnp.sum(v.reshape(-1, 8, 128), axis=0)
        g_small[0:8, :] += fold(grad_normed * unit_rows)
        g_small[8:16, :] += fold(grad_normed)
        g_small[16:24, :] += fold(loss_part)
    g_in[...] += dot(s_normed[...], s_grad_in[...], ((0,), (0,)))
    g_out[...] += dot(s_pair[...], s_hidden[...], ((0,), (0,)))


def backward_call(
    which, pair4, pair_out4, mirror, own_code, mirror_code, gain, bias, w_in, w_out, head_two,
    earlier=None,
):
    wide, hid = w_in.shape[1], w_out.shape[0]
    block = pl.BlockSpec((GROUP * B_GROUPS, 1, SIDE, 128), lambda g, w: (g, w[0], 0, 0))
    whole = lambda a: pl.BlockSpec(a.shape, lambda g, w: (0,) * len(a.shape))
    rows = SIDE * GROUP // 2 * B_GROUPS
    fixed = (own_code, mirror_code, gain, bias, w_in, w_out, head_two)
    in_specs = [block, block, pl.BlockSpec((rows, 128), lambda g, w: (g, 0))]
    in_specs += [whole(a) for a in fixed]
    args = [pair4, pair_out4, mirror, *fixed]
    outs = (
        jax.ShapeDtypeStruct((128, wide), F32),
        jax.ShapeDtypeStruct((128, hid), F32),
        jax.ShapeDtypeStruct((256, 256), F32),
        jax.ShapeDtypeStruct((24, 128), F32),
    )
    if earlier is not None:
        in_specs += [whole(a) for a in outs]
        args += list(earlier)
    return pl.pallas_call(
        backward_body,
        out_shape=outs,
        grid_spec=pltpu.PrefetchScalarGridSpec(
            num_scalar_prefetch=1,
            grid=(SIDE // (GROUP * B_GROUPS),),
            in_specs=in_specs,
            out_specs=tuple(whole(a) for a in outs),
            scratch_shapes=[
                pltpu.VMEM((2 * rows, 128), BF16),
                pltpu.VMEM((2 * rows, wide), BF16),
                pltpu.VMEM((2 * rows, hid), BF16),
                pltpu.VMEM((2 * rows, 128), BF16),
            ],
        ),
        compiler_params=pltpu.CompilerParams(dimension_semantics=("arbitrary",)),
        name="backward",
    )(which, *args)


def shards(
    pair, ln_gain, ln_bias, gate_weight, up_weight, out_weight, head_weight, targets, pair_mask
):
    rows_tile, cols_tile, width = pair.shape
    row_count, col_count = lax.axis_size("row"), lax.axis_size("col")
    tokens = rows_tile * row_count
    hid = gate_weight.shape[1]
    bins = head_weight.shape[1]
    row = lax.axis_index("row")
    parity = lax.rem(row, 2)
    swap = [[], []]
    for r in range(row_count):
        for c in range(col_count):
            for turn in range(2):
                h = (r + turn) % 2
                swap[turn].append((r * col_count + c, (2 * c + h) * col_count + r // 2))

    words = targets + 65536 * pair_mask
    tile_words = lax.all_to_all(words, "col", split_axis=1, concat_axis=0, tiled=True)
    tile_words = tile_words.reshape(rows_tile, 2, SIDE)

    gain, bias = ln_gain.reshape(1, width), ln_bias.reshape(1, width)
    w_in = jnp.concatenate([gate_weight, up_weight], axis=1)
    blank = jnp.zeros_like(head_weight)
    head_two = jnp.concatenate(
        [
            jnp.concatenate([head_weight, blank], axis=1),
            jnp.concatenate([blank, head_weight], axis=1),
        ],
        axis=0,
    )
    pair4 = pair.reshape(rows_tile, 2, SIDE, width)
    which = [(parity + turn) % 2 for turn in range(2)]
    which = [w.astype(jnp.int32).reshape(1) for w in which]
    weights = (gain, bias, w_in, out_weight, head_two)

    out4, sent0 = forward_call(which[0], pair4, *weights)
    mirror0 = lax.ppermute(sent0, AXES, swap[0])
    own = [
        lax.dynamic_index_in_dim(tile_words, which[turn][0], 1, keepdims=False)
        for turn in range(2)
    ]
    theirs = [lax.ppermute(own[turn], AXES, swap[turn]) for turn in range(2)]
    out4, sent1 = forward_call(which[1], pair4, *weights, partial=out4)
    mirror1 = lax.ppermute(sent1, AXES, swap[1])
    part = backward_call(which[0], pair4, out4, mirror0, own[0], theirs[0], *weights)
    part = backward_call(which[1], pair4, out4, mirror1, own[1], theirs[1], *weights, earlier=part)
    g_in, g_out, g_head, g_small = part
    head_sum = (
        g_head[:128, :bins]
        + g_head[:128, 128 : 128 + bins]
        + g_head[128:, bins:128]
        + g_head[128:, 128 + bins :]
    )
    flat = jnp.concatenate(
        [
            g_in.reshape(-1),
            g_out.reshape(-1),
            head_sum.reshape(-1),
            g_small.reshape(-1),
        ]
    )
    devices = row_count * col_count
    unit = devices * 1024
    length = flat.shape[0]
    padded = -(-length // unit) * unit
    flat = jnp.pad(flat, (0, padded - length)).reshape(devices, -1, 128)
    pieces = lax.all_to_all(flat, AXES, split_axis=0, concat_axis=0, tiled=True)
    mine = jnp.sum(pieces, axis=0, keepdims=True)
    mine = jnp.broadcast_to(mine, pieces.shape)
    summed = lax.all_to_all(mine, AXES, split_axis=0, concat_axis=0, tiled=True).reshape(-1)
    cut = [0]
    for size in (g_in.size, g_out.size, head_sum.size, g_small.size):
        cut.append(cut[-1] + size)
    s_in = summed[cut[0] : cut[1]].reshape(g_in.shape)
    s_out = summed[cut[1] : cut[2]].reshape(g_out.shape).T
    s_head = summed[cut[2] : cut[3]].reshape(head_sum.shape)
    small = jnp.sum(summed[cut[3] : cut[4]].reshape(3, 8, 128), axis=1)
    loss = jnp.sum(small[2]) / (tokens * tokens)
    pair_out = out4.reshape(pair.shape)
    return (pair_out, loss, small[0], small[1], s_in[:, :hid], s_in[:, hid:], s_out, s_head)


def solution(mesh):
    placed = (
        P("row", "col", None),
        P(),
        P(),
        P(),
        P(),
        P(),
        P(),
        P(AXES, None),
        P(AXES, None),
    )
    return jax.shard_map(
        shards,
        mesh=mesh,
        in_specs=placed,
        out_specs=(P("row", "col", None), P(), P(), P(), P(), P(), P(), P()),
        check_vma=False,
    )
```

time: 418 us -> 213 us (0.51)
  matrix products: 88.2 us -> 0 us
  waiting for transfers between devices: 123 us -> 69.1 us
  Pallas kernels: 0 us -> 48.3 us
  blocking collectives: 99.5 us -> 58.3 us
  local copies, waits for them, and re-layouts: 46 us -> 10 us
  other arithmetic: 18.7 us -> 4.43 us
  between operations: 16.2 us -> 2.6 us
  starting transfers between devices: 23.7 us -> 19 us
    dot_general x46 -> x0, matrix products: 88.2 us -> none  [the longest x14 19.9 us: inner(): lax.dot_general(left, right, (((0,), (0,)), ((), ())), preferred_element_...]
    psum x1 -> x0, waiting for transfers between devices: 72.6 us -> none  [shards(): lax.psum((loss_part, totals[0], totals[1], totals[2], totals[3], totals[4...]
    psum x1 -> x0, blocking collectives: 64.7 us -> none  [shards(): lax.psum((loss_part, totals[0], totals[1], totals[2], totals[3], totals[4...]
    pallas_call x0 -> x4, Pallas kernels: none -> 48.3 us  [the longest x2 29.9 us: backward_call(): pl.pallas_call(backward_body, out_shape=outs, grid_spec=pltpu.PrefetchSca...]
    all_to_all x1 -> x2, blocking collectives: 34.8 us -> 58.3 us  [the longest x1 35.3 us: shards(): pieces = lax.all_to_all(flat, AXES, split_axis=0, concat_axis=0, tiled=True)]
    all_to_all x4 -> x1, waiting for transfers between devices: 50.5 us -> 69.1 us  [shards(): lax.all_to_all(words, 'col', split_axis=1, concat_axis=0, tiled=True)]
    unnamed x45 -> x24, local copies, waits for them, and re-layouts: 23.8 us -> 7.73 us
    reduce_sum x16 -> x2, other arithmetic: 15.1 us -> 0.15 us  [the longest x1 0.14 us: shards(): mine = jnp.sum(pieces, axis=0, keepdims=True)]
  transfers between devices with their start and end apart: 5 -> 5, of which waited for: 5 -> 1; matrix products, arithmetic and copies ran while one was open for 8% -> 0% of each run, Pallas kernels for 0% -> 11%
where the time goes in v1:
time: 213 us; the launch traced here: 212 us
  waiting for transfers between devices  69.1 us (32%)
  blocking collectives  58.3 us (27%)
  Pallas kernels  48.3 us (23%)
  starting transfers between devices  19 us (9%)
  local copies, waits for them, and re-layouts  10 us (5%)
  other arithmetic  4.43 us (2%)
  between operations  2.6 us (1%)
    all_to_all x1, waiting for transfers between devices, shards(): lax.all_to_all(words, 'col', split_axis=1, concat_axis=0, tiled=True)  69.1 us
    all_to_all x1, blocking collectives, shards(): pieces = lax.all_to_all(flat, AXES, split_axis=0, concat_axis=0, tiled=True)  35.3 us
    pallas_call x2, Pallas kernels, backward_call(): pl.pallas_call(backward_body, out_shape=outs, grid_spec=pltpu.PrefetchSca...  29.9 us
    all_to_all x1, blocking collectives, shards(): lax.all_to_all(mine, AXES, split_axis=0, concat_axis=0, tiled=True)  22.9 us
    pallas_call x2, Pallas kernels, forward_call(): pl.pallas_call(forward_body, out_shape=(jax.ShapeDtypeStruct(pair4.shape,...  18.4 us
    all_to_all x1, starting transfers between devices, shards(): lax.all_to_all(words, 'col', split_axis=1, concat_axis=0, tiled=True)  13.3 us
    unnamed x24, local copies, waits for them, and re-layouts  7.73 us
  transfers between devices with their start and end apart: 5, of which 1 were waited for; matrix products, arithmetic and copies ran while one was open for 0% of the time, Pallas kernels for 11%

profile of v1, /device:TPU:1, one launch (start us, length us, event | category | flops | bytes accessed | tf_op | source)
XLA Modules:
  0.0 211.8 jit_solution(5100422942864213136)
XLA Ops:
  0.7 0.9 constant_dynamic-update-slice_fusion.1
  1.6 0.8 copy.24
  2.4 0.7 fusion.2.head_two
  3.1 0.9 constant_dynamic-update-slice_fusion.w_in
  4.0 0.7 copy-done
  4.7 9.2 %forward.2 = (bf16[64,2,64,128]{3,2,1,0:T(8,128)(2,1)}, bf16[2048,128]{1,0:T(8,128)(2,1)}) custom-call(s32[1]{0:T(128)} %bitcast.4.which, bf16[64,2,64,128]{3,2,1,0:T(8,128)(2,1)} %bitcast.23, f32[1,128]{1,0:T(1,128)} %bitcast.41, f32[1,128]{1,0:T(1,128)} %bitcast.45, bf16[128,1024]{1,0:T(8,128)(2,1)} %copy-done, bf16[512,128]{1,0:T(8,128)(2,1)} %w_out.7, ...), custom_call_target="tpu_custom_call" | custom-call | tf_op jit(solution)/shard_map/forward/pallas_call | solution.py:82
  13.9 1.7 collective-permute-start.2
  15.6 9.2 %forward.3 = (bf16[64,2,64,128]{3,2,1,0:T(8,128)(2,1)}, bf16[2048,128]{1,0:T(8,128)(2,1)}) custom-call(s32[1]{0:T(128)} %bitcast.which, bf16[64,2,64,128]{3,2,1,0:T(8,128)(2,1)} %bitcast.24, f32[1,128]{1,0:T(1,128)} %bitcast.42, f32[1,128]{1,0:T(1,128)} %bitcast.46, bf16[128,1024]{1,0:T(8,128)(2,1)} %copy-done, ...), custom_call_target="tpu_custom_call", output_to_operand_aliasing={{0}: (7, {})} | custom-call | tf_op jit(solution)/shard_map/forward/pallas_call | solution.py:82
  24.9 1.4 collective-permute-start
  26.3 0.6 add_bitcast_fusion
  26.9 13.3 %all-to-all-start = ((s32[8,8,128]{2,0,1:T(8,128)}), s32[8,8,128]{2,0,1:T(8,128)S(1)}, u32[]{:S(2)}, u32[]{:S(2)}) async-start(s32[8,8,128]{2,0,1:T(8,128)} %add_bitcast_fusion), calls=%async_computation | async-start | bytes 65536 | tf_op jit(solution)/shard_map/all_to_all | solution.py:252
  40.2 69.1 %all-to-all-done = s32[8,8,128]{2,0,1:T(8,128)S(1)} async-done(((s32[8,8,128]{2,0,1:T(8,128)}), s32[8,8,128]{2,0,1:T(8,128)S(1)}, u32[]{:S(2)}, u32[]{:S(2)}) %all-to-all-start) | async-done | bytes 32800 | tf_op jit(solution)/shard_map/all_to_all | solution.py:252
  109.3 0.1 reshape.82
  109.5 0.7 collective-permute-start.3
  110.2 2.0 collective-permute-start.1
  112.2 0.6 copy-done.6
  112.8 0.2 copy-done.1
  113.0 14.7 %backward.2 = (f32[128,1024]{1,0:T(8,128)}, f32[128,512]{1,0:T(8,128)}, f32[256,256]{1,0:T(8,128)}, f32[24,128]{1,0:T(8,128)}) custom-call(s32[1]{0:T(128)} %bitcast.4.which, bf16[64,2,64,128]{3,2,1,0:T(8,128)(2,1)} %bitcast.25, bf16[64,2,64,128]{3,2,1,0:T(8,128)(2,1)} %get-tuple-element.21.pair_out, bf16[2048,128]{1,0:T(8,128)(2,1)} %copy-done.1, ...), custom_call_target="tpu_custom_call" | custom-call | tf_op jit(solution)/shard_map/backward/pallas_call | solution.py:214
  127.8 0.6 copy-done.5
  128.4 0.2 copy-done.2
  128.6 15.1 %backward.3 = (f32[128,1024]{1,0:T(8,128)}, f32[128,512]{1,0:T(8,128)}, f32[256,256]{1,0:T(8,128)}, f32[24,128]{1,0:T(8,128)}) custom-call(s32[1]{0:T(128)} %bitcast.which, bf16[64,2,64,128]{3,2,1,0:T(8,128)(2,1)} %bitcast.26, bf16[64,2,64,128]{3,2,1,0:T(8,128)(2,1)} %get-tuple-element.21.pair_out, bf16[2048,128]{1,0:T(8,128)(2,1)} %copy-done.2, ...), custom_call_target="tpu_custom_call" | custom-call | tf_op jit(solution)/shard_map/backward/pallas_call | solution.py:214
  143.7 1.1 copy.28
  144.9 1.0 copy.29
  145.9 1.0 slice_add_fusion
  147.0 0.8 select_maximum_fusion
  147.8 35.3 %all_to_all.26 = f32[128,16,128]{2,1,0:T(8,128)S(1)} all-to-all(f32[128,16,128]{2,1,0:T(8,128)S(1)} %bitcast.28), channel_id=1, replica_groups=mesh['row'=16,'col'=8] {'row','col'}, dimensions={0} | all-to-all | bytes 2097152 | tf_op jit(solution)/shard_map/all_to_all | solution.py:301
  183.1 0.1 reduce_sum.27
  183.3 22.9 %all_to_all.27 = f32[128,16,128]{2,1,0:T(8,128)S(1)} all-to-all(f32[128,16,128]{2,1,0:T(8,128)S(1)} %broadcast_in_dim.2), channel_id=1, replica_groups=mesh['row'=16,'col'=8] {'row','col'}, dimensions={0} | all-to-all | bytes 2097152 | tf_op jit(solution)/shard_map/all_to_all | solution.py:304
  206.4 0.8 fusion.3
  207.3 0.8 copy.26
  208.2 0.7 copy.27
  208.9 1.1 slice_bitcast_fusion
  (27 shorter events, 0.5 us)
Async XLA Ops:
  4.0 0.7 copy-start
  13.9 98.3 %collective-permute-start.2 = (bf16[2048,128]{1,0:T(8,128)(2,1)}, bf16[2048,128]{1,0:T(8,128)(2,1)S(1)}, u32[]{:S(2)}, u32[]{:S(2)}) collective-permute-start(bf16[2048,128]{1,0:T(8,128)(2,1)} %get-tuple-element.23), channel_id=1, source_target_pairs={{0,0},{1,16},{2,32},{3,48},{4,64},{5,80},{6,96},{7,112},{8,8},{9,2... | collective-permute-start | bytes 1572872 | tf_op jit(solution)/shard_map/ppermute | solution.py:271
  15.6 10.6 %copy-start.7 = (s32[8,1024]{1,0:T(8,128)S(1)}, s32[8,1024]{1,0:T(8,128)}, u32[]{:S(2)}) copy-start(s32[8,1024]{1,0:T(8,128)} %param.16) | copy-start | bytes 98308
  15.6 10.6 %copy-start.8 = (s32[8,1024]{1,0:T(8,128)S(1)}, s32[8,1024]{1,0:T(8,128)}, u32[]{:S(2)}) copy-start(s32[8,1024]{1,0:T(8,128)} %param.17) | copy-start | bytes 98308
  24.9 102.9 %collective-permute-start = (bf16[2048,128]{1,0:T(8,128)(2,1)}, bf16[2048,128]{1,0:T(8,128)(2,1)S(1)}, u32[]{:S(2)}, u32[]{:S(2)}) collective-permute-start(bf16[2048,128]{1,0:T(8,128)(2,1)} %get-tuple-element.22), channel_id=1, source_target_pairs={{0,8},{1,24},{2,40},{3,56},{4,72},{5,88},{6,104},{7,120},{8,0},{9,... | collective-permute-start | bytes 1572872 | tf_op jit(solution)/shard_map/ppermute | solution.py:278
  26.9 82.4 %all-to-all-start = ((s32[8,8,128]{2,0,1:T(8,128)}), s32[8,8,128]{2,0,1:T(8,128)S(1)}, u32[]{:S(2)}, u32[]{:S(2)}) async-start(s32[8,8,128]{2,0,1:T(8,128)} %add_bitcast_fusion), calls=%async_computation | async-start | bytes 65536 | tf_op jit(solution)/shard_map/all_to_all | solution.py:252
  109.5 2.7 %copy-start.4 = (s32[64,1,64]{2,1,0:T(1,128)}, s32[64,1,64]{2,1,0:T(1,128)S(1)}, u32[]{:S(2)}) copy-start(s32[64,1,64]{2,1,0:T(1,128)S(1)} %get-tuple-element.50) | copy-start | bytes 49156
  109.5 18.3 %copy-start.3 = (s32[64,1,64]{2,1,0:T(1,128)}, s32[64,1,64]{2,1,0:T(1,128)S(1)}, u32[]{:S(2)}) copy-start(s32[64,1,64]{2,1,0:T(1,128)S(1)} %get-tuple-element.51) | copy-start | bytes 49156
  109.5 2.7 %collective-permute-start.3 = (s32[64,64]{1,0:T(8,128)S(1)}, s32[64,64]{1,0:T(8,128)S(1)}, u32[]{:S(2)}, u32[]{:S(2)}) collective-permute-start(s32[64,64]{1,0:T(8,128)S(1)} %bitcast.37), channel_id=1, source_target_pairs={{0,0},{1,16},{2,32},{3,48},{4,64},{5,80},{6,96},{7,112},{8,8},{9,2... | collective-permute-start | bytes 49160 | tf_op jit(solution)/shard_map/ppermute | solution.py:276
  110.2 17.6 %collective-permute-start.1 = (s32[64,64]{1,0:T(8,128)S(1)}, s32[64,64]{1,0:T(8,128)S(1)}, u32[]{:S(2)}, u32[]{:S(2)}) collective-permute-start(s32[64,64]{1,0:T(8,128)S(1)} %bitcast.35), channel_id=1, source_target_pairs={{0,8},{1,24},{2,40},{3,56},{4,72},{5,88},{6,104},{7,120},{8,0},{9,... | collective-permute-start | bytes 49160 | tf_op jit(solution)/shard_map/ppermute | solution.py:276
  112.2 0.6 copy-start.6
  112.2 0.8 copy-start.1
  127.8 0.6 copy-start.5
  127.8 0.8 copy-start.2

commit v2 on v1

v2 whole, which is shorter than its diff:
```python
import jax
import jax.numpy as jnp
from jax import lax
from jax.experimental import pallas as pl
from jax.experimental.pallas import tpu as pltpu
from jax.sharding import PartitionSpec as P

EPSILON = 1e-05
F32 = jnp.float32
BF16 = jnp.bfloat16
AXES = ("row", "col")

SIDE = 64
PARTS = 2
GROUP = 8
F_COLS = 16
B_GROUPS = 2
ROWS = SIDE * GROUP // 2

ROUTES = ((0, 0, 1), (0, 0, 3), (0, 2, 0), None)


def chip_of(device):
    r, c = divmod(device, 8)
    return (c // 2, (r % 8) // 2, (c % 2) * 2 + r // 8), r % 2


def device_at(chip, core):
    x, y, z = chip
    return ((z % 2) * 8 + y * 2 + core) * 8 + x * 2 + z // 2


def mirror_of(device, turn):
    r, c = divmod(device, 8)
    return (2 * c + (r + turn) % 2) * 8 + r // 2


def shifted(device, shift):
    chip, core = chip_of(device)
    return device_at(tuple((a + b) % 4 for a, b in zip(chip, shift)), core)


def send_to_mirror(value, turn, route):
    devices = range(128)
    if route is None:
        return lax.ppermute(value, AXES, [(d, mirror_of(d, turn)) for d in devices])
    value = lax.ppermute(value, AXES, [(d, shifted(d, route)) for d in devices])
    return lax.ppermute(value, AXES, [(shifted(d, route), mirror_of(d, turn)) for d in devices])


def dot(left, right, dims=((1,), (0,))):
    return lax.dot_general(left, right, (dims, ((), ())), preferred_element_type=F32)


NT = ((1,), (1,))
TN = ((0,), (0,))


def normalize(rows_in, gain, bias):
    values = rows_in.astype(F32)
    centered = values - jnp.mean(values, axis=-1, keepdims=True)
    variance = jnp.mean(centered * centered, axis=-1, keepdims=True)
    unit_rows = centered * lax.rsqrt(variance + EPSILON)
    return unit_rows, (unit_rows * gain + bias).astype(BF16)


def sigmoid(values):
    return 0.5 * jnp.tanh(0.5 * values) + 0.5


def head_square(head_t):
    blank = jnp.zeros_like(head_t)
    return jnp.concatenate(
        [
            jnp.concatenate([head_t, blank], axis=1),
            jnp.concatenate([blank, head_t], axis=1),
        ],
        axis=0,
    )


def forward_body(which, pair, gain, bias, w_gate, w_up, w_out, head_t, *rest):
    pair_out, send, wide = rest[-3:]
    rows_in = pair[...].reshape(SIDE * F_COLS, 128)
    count = 4
    size = SIDE * F_COLS // count
    for k in range(count):
        part = rows_in[k * size : (k + 1) * size]
        _, normed = normalize(part, gain[...], bias[...])
        gate_pre = dot(normed, w_gate[...])
        up_pre = dot(normed, w_up[...])
        hidden = (gate_pre * sigmoid(gate_pre) * up_pre).astype(BF16)
        result = (part.astype(F32) + dot(hidden, w_out[...])).astype(BF16)
        pair_out[k * size // F_COLS : (k + 1) * size // F_COLS] = result.reshape(
            size // F_COLS, 1, F_COLS, 128
        )
        wide[k * size : (k + 1) * size, :] = result.astype(F32)
    head_two = head_square(head_t[...])
    for grp in range(F_COLS // GROUP):
        left, right = [
            jnp.concatenate(
                [
                    wide[pl.ds(grp * GROUP + shift + a, SIDE, stride=F_COLS), :]
                    for a in range(GROUP // 2)
                ],
                axis=0,
            )
            for shift in (0, GROUP // 2)
        ]
        both = jnp.concatenate([left, right], axis=1).astype(BF16)
        send[grp * ROWS : (grp + 1) * ROWS, :] = dot(both, head_two, NT).astype(BF16)


def whole(a):
    return pl.BlockSpec(a.shape, lambda g, w: (0,) * len(a.shape))


def forward_call(which, part, pair4, weights, partial=None, after=None):
    steps = SIDE // PARTS // F_COLS
    block = pl.BlockSpec((SIDE, 1, F_COLS, 128), lambda g, w: (0, w[0], part * steps + g, 0))
    in_specs = [block] + [whole(a) for a in weights]
    args = [pair4, *weights]
    alias = {}
    if partial is not None:
        in_specs.append(pl.BlockSpec(memory_space=pl.ANY))
        alias = {1 + len(args): 0}
        args.append(partial)
    if after is not None:
        in_specs.append(pl.BlockSpec(memory_space=pl.ANY))
        args.append(after)
    rows = ROWS * F_COLS // GROUP
    pairs = SIDE * SIDE // PARTS
    return pl.pallas_call(
        forward_body,
        out_shape=(
            jax.ShapeDtypeStruct(pair4.shape, BF16),
            jax.ShapeDtypeStruct((rows * steps, 128), BF16),
        ),
        grid_spec=pltpu.PrefetchScalarGridSpec(
            num_scalar_prefetch=1,
            grid=(steps,),
            in_specs=in_specs,
            out_specs=(block, pl.BlockSpec((rows, 128), lambda g, w: (g, 0))),
            scratch_shapes=[pltpu.VMEM((SIDE * F_COLS, 128), F32)],
        ),
        input_output_aliases=alias,
        cost_estimate=pl.CostEstimate(
            flops=pairs * 2 * 128 * 512 * 3, transcendentals=pairs * 512, bytes_accessed=pairs * 640
        ),
        compiler_params=pltpu.CompilerParams(dimension_semantics=("arbitrary",)),
        name="forward",
    )(which, *args)


def code_of(word):
    return (jnp.bitwise_and(word, 65535) + 64 * jnp.right_shift(word, 16)).astype(F32).astype(BF16)


def backward_body(first_group, first, last, which, *refs):
    pair, pair_out, mirror, own_code, mirror_code = refs[:5]
    gain, bias, w_gate, w_up, w_out, head_t = refs[5:11]
    rest = list(refs[11:])
    earlier = None
    if not first:
        earlier, rest = rest[:4], rest[4:]
    if last:
        keep, send = rest[:2]
        rest = rest[2:]
    g_in, g_out, g_head, g_small, s_normed, s_grad_in, s_hidden, s_pair = rest
    sums = (g_in, g_out, g_head, g_small)
    hid = w_out.shape[0]
    step = pl.program_id(0)

    @pl.when(step == 0)
    def _():
        for k, ref in enumerate(sums):
            ref[...] = jnp.zeros_like(ref) if first else earlier[k][...]

    lane = lax.broadcasted_iota(jnp.int32, (ROWS, 128), 1)
    wanted = (jnp.bitwise_and(lane, 63) + 64).astype(F32)
    lane_row = lax.broadcasted_iota(jnp.int32, (128, 128), 0)
    lane_col = lax.broadcasted_iota(jnp.int32, (128, 128), 1)
    same = (lane_row // 64 == lane_col // 64).astype(F32).astype(BF16)
    sum_bins = jnp.concatenate([same, same], axis=0)
    head_two = head_square(head_t[...])
    head_four = jnp.concatenate([head_two, head_two], axis=0)
    own = code_of(own_code[...])
    other = code_of(mirror_code[...])
    pick_n = lax.broadcasted_iota(jnp.int32, (SIDE, 512), 1)
    pick_k = lax.broadcasted_iota(jnp.int32, (SIDE, 512), 0)
    pick_base = pick_n // 128 + (GROUP // 2) * (jnp.bitwise_and(pick_n, 127) // 64)

    for grp in range(B_GROUPS):
        at = slice(grp * 2 * ROWS, (grp + 1) * 2 * ROWS)
        x_out = pair_out[grp * GROUP : (grp + 1) * GROUP].reshape(2 * ROWS, 128)
        both = jnp.concatenate([x_out[:ROWS], x_out[ROWS:]], axis=1)
        half = dot(both, head_two, NT).astype(BF16)
        logits = half.astype(F32) + mirror[grp * ROWS : (grp + 1) * ROWS, :].astype(F32)
        expo = 0.5 * jnp.exp(logits)
        high = expo.astype(BF16)
        low = (expo - high.astype(F32)).astype(BF16)
        total = dot(jnp.concatenate([high, low], axis=1), sum_bins)
        log_total = jnp.log(total) + 0.6931471805599453
        soft = jnp.exp(logits - log_total)
        group = first_group + step * B_GROUPS + grp
        pick = (pick_k == pick_base + GROUP * group).astype(F32).astype(BF16)
        codes = []
        for spread in (dot(own, pick, TN), dot(other, pick)):
            codes.append(
                jnp.concatenate([spread[:, 128 * a : 128 * (a + 1)] for a in range(4)], axis=0)
            )
        grads = [
            (
                (jnp.where(c >= 63.5, soft, 0.0) - jnp.where(c == wanted, 1.0, 0.0)) * (1.0 / 1024)
            ).astype(BF16)
            for c in codes
        ]
        loss_part = jnp.where(codes[0] == wanted, log_total - logits, 0.0)
        grad_both = jnp.concatenate(grads, axis=1)
        g_head[...] += dot(grad_both, both, TN)
        grad_pair = dot(grad_both, head_four).astype(BF16)
        grad_pair = jnp.concatenate([grad_pair[:, :128], grad_pair[:, 128:]], axis=0)
        s_pair[at, :] = grad_pair

        x_in = pair[grp * GROUP : (grp + 1) * GROUP].reshape(2 * ROWS, 128)
        unit_rows, normed = normalize(x_in, gain[...], bias[...])
        s_normed[at, :] = normed
        gate_pre = dot(normed, w_gate[...])
        up_pre = dot(normed, w_up[...])
        grad_hidden = dot(grad_pair, w_out[...], NT)
        squashed = sigmoid(gate_pre)
        silu_val = gate_pre * squashed
        s_hidden[at, :] = (silu_val * up_pre).astype(BF16)
        slope = squashed * (1.0 + gate_pre * (1.0 - squashed))
        s_grad_in[at, :hid] = (grad_hidden * up_pre * slope).astype(BF16)
        s_grad_in[at, hid:] = (grad_hidden * silu_val).astype(BF16)
        grad_normed = dot(s_grad_in[at, :hid], w_gate[...], NT)
        grad_normed += dot(s_grad_in[at, hid:], w_up[...], NT)
        fold = lambda v: jnp.sum(v.reshape(-1, 8, 128), axis=0)
        g_small[0:8, :] += fold(grad_normed * unit_rows)
        g_small[8:16, :] += fold(grad_normed)
        g_small[16:24, :] += fold(loss_part)
    g_in[...] += dot(s_normed[...], s_grad_in[...], TN)
    g_out[...] += dot(s_pair[...], s_hidden[...], TN)

    if not last:
        return

    def put_in(ref):
        for k in range(8):
            ref[128 * k : 128 * (k + 1), :] = g_in[:, 128 * k : 128 * (k + 1)]

    def put_rest(ref):
        for k in range(4):
            ref[128 * k : 128 * (k + 1), :] = g_out[:, 128 * k : 128 * (k + 1)].T
        ref[512:576, :] = (
            g_head[0:64, 0:128]
            + g_head[64:128, 128:256]
            + g_head[128:192, 0:128]
            + g_head[192:256, 128:256]
        )
        small = [jnp.sum(g_small[8 * k : 8 * k + 8, :], axis=0, keepdims=True) for k in range(3)]
        ref[576:584, :] = jnp.concatenate(small + [jnp.zeros((5, 128), F32)], axis=0)
        ref[584:1024, :] = jnp.zeros((440, 128), F32)

    at_end = step == pl.num_programs(0) - 1

    @pl.when(jnp.logical_and(at_end, which[1] == 0))
    def _():
        put_in(keep)
        put_rest(send)

    @pl.when(jnp.logical_and(at_end, which[1] != 0))
    def _():
        put_in(send)
        put_rest(keep)


def backward_call(
    which, part, pair4, pair_out4, mirror, own_code, mirror_code, weights, earlier, last
):
    wide, hid = 2 * weights[2].shape[1], weights[4].shape[0]
    steps = SIDE // PARTS // (GROUP * B_GROUPS)
    block = pl.BlockSpec(
        (GROUP * B_GROUPS, 1, SIDE, 128), lambda g, w: (part * steps + g, w[0], 0, 0)
    )
    rows = ROWS * B_GROUPS
    fixed = (own_code, mirror_code, *weights)
    in_specs = [block, block, pl.BlockSpec((rows, 128), lambda g, w: (g, 0))]
    in_specs += [whole(a) for a in fixed]
    args = [pair4, pair_out4, mirror, *fixed]
    sums = [(128, wide), (128, hid), (256, 256), (24, 128)]
    if earlier is not None:
        in_specs += [whole(a) for a in earlier]
        args += list(earlier)
    outs = [jax.ShapeDtypeStruct(s, F32) for s in ([(1024, 128)] * 2 if last else sums)]
    scratch = [pltpu.VMEM(s, F32) for s in sums] if last else []
    scratch += [
        pltpu.VMEM((2 * rows, 128), BF16),
        pltpu.VMEM((2 * rows, wide), BF16),
        pltpu.VMEM((2 * rows, hid), BF16),
        pltpu.VMEM((2 * rows, 128), BF16),
    ]
    pairs = SIDE * SIDE // PARTS

    def body(*refs):
        backward_body(part * steps * B_GROUPS, earlier is None, last, *refs)

    return pl.pallas_call(
        body,
        out_shape=tuple(outs),
        grid_spec=pltpu.PrefetchScalarGridSpec(
            num_scalar_prefetch=1,
            grid=(steps,),
            in_specs=in_specs,
            out_specs=tuple(whole(a) for a in outs),
            scratch_shapes=scratch,
        ),
        cost_estimate=pl.CostEstimate(
            flops=pairs * 2 * 128 * 512 * 8, transcendentals=pairs * 640, bytes_accessed=pairs * 640
        ),
        compiler_params=pltpu.CompilerParams(dimension_semantics=("arbitrary",)),
        name="backward",
    )(which, *args)


def unpack_body(core, mine, other, d_gate, d_up, d_out, d_head, d_gain, d_bias, loss):
    def fill(lower, upper):
        for k in range(4):
            d_gate[:, 128 * k : 128 * (k + 1)] = lower[128 * k : 128 * (k + 1), :]
            d_up[:, 128 * k : 128 * (k + 1)] = lower[512 + 128 * k : 640 + 128 * k, :]
        d_out[...] = upper[0:512, :]
        d_head[...] = upper[512:576, :]
        d_gain[...] = upper[576:577, :]
        d_bias[...] = upper[577:578, :]
        loss[0, 0] = jnp.sum(upper[578:579, :]) * (1.0 / 1048576)

    @pl.when(core[0] == 0)
    def _():
        fill(mine, other)

    @pl.when(core[0] != 0)
    def _():
        fill(other, mine)


def unpack_call(core, mine, other):
    shapes = [(128, 512), (128, 512), (512, 128), (64, 128), (1, 128), (1, 128), (1, 1)]
    outs = tuple(jax.ShapeDtypeStruct(s, F32) for s in shapes)
    specs = [whole(a) for a in outs[:-1]] + [pl.BlockSpec(memory_space=pltpu.SMEM)]
    return pl.pallas_call(
        unpack_body,
        out_shape=outs,
        grid_spec=pltpu.PrefetchScalarGridSpec(
            num_scalar_prefetch=1,
            grid=(1,),
            in_specs=[whole(mine), whole(other)],
            out_specs=tuple(specs),
        ),
        name="unpack",
    )(core, mine, other)


def shards(
    pair, ln_gain, ln_bias, gate_weight, up_weight, out_weight, head_weight, targets, pair_mask
):
    rows_tile, cols_tile, width = pair.shape
    row = lax.axis_index("row")
    core = lax.rem(row, 2).astype(jnp.int32)
    which = [jnp.stack([core, core]), jnp.stack([1 - core, core])]

    words = targets + 65536 * pair_mask
    with jax.named_scope("words"):
        tile_words = lax.all_to_all(words, "col", split_axis=1, concat_axis=0, tiled=True)
    blocks = tile_words.reshape(rows_tile, 2, SIDE)

    pair4 = pair.reshape(rows_tile, 2, SIDE, width)
    weights = (
        ln_gain.reshape(1, width),
        ln_bias.reshape(1, width),
        gate_weight,
        up_weight,
        out_weight,
        head_weight.T,
    )
    chunks = [(turn, part) for turn in range(2) for part in range(PARTS)]
    out4 = None
    mirrors = []
    own, theirs = [], []
    for k, (turn, part) in enumerate(chunks):
        after = tile_words if k == 1 else None
        out4, sent = forward_call(which[turn], part, pair4, weights, out4, after)
        if k == 0:
            for t in range(2):
                own.append(
                    lax.dynamic_index_in_dim(blocks, which[t][0], 1, keepdims=False)
                )
                theirs.append(send_to_mirror(own[t], t, None))
        mirrors.append(send_to_mirror(sent, turn, ROUTES[k]))
    sums = None
    for k, (turn, part) in enumerate(chunks):
        sums = backward_call(
            which[turn], part, pair4, out4, mirrors[k], own[turn], theirs[turn], weights, sums,
            k == len(chunks) - 1,
        )
    keep, send = sums
    sibling = [(d, device_at(chip_of(d)[0], 1 - chip_of(d)[1])) for d in range(128)]
    groups = [[d for d in range(128) if chip_of(d)[1] == k] for k in range(2)]
    both_cores = (keep + lax.ppermute(send, AXES, sibling)).reshape(64, 16, 128)
    pieces = lax.all_to_all(
        both_cores, AXES, split_axis=0, concat_axis=0, axis_index_groups=groups, tiled=True
    )
    mine = jnp.sum(pieces, axis=0, keepdims=True)
    mine = lax.all_to_all(
        jnp.broadcast_to(mine, pieces.shape),
        AXES,
        split_axis=0,
        concat_axis=0,
        axis_index_groups=groups,
        tiled=True,
    ).reshape(1024, 128)
    other = lax.ppermute(mine, AXES, sibling)
    d_gate, d_up, d_out, d_head, d_gain, d_bias, loss = unpack_call(core.reshape(1), mine, other)
    return (
        out4.reshape(pair.shape),
        loss.reshape(()),
        d_gain.reshape(width),
        d_bias.reshape(width),
        d_gate,
        d_up,
        d_out,
        d_head.T,
    )


def solution(mesh):
    placed = (
        P("row", "col", None),
        P(),
        P(),
        P(),
        P(),
        P(),
        P(),
        P(AXES, None),
        P(AXES, None),
    )
    return jax.shard_map(
        shards,
        mesh=mesh,
        in_specs=placed,
        out_specs=(P("row", "col", None), P(), P(), P(), P(), P(), P(), P()),
        check_vma=False,
    )
```

time: 213 us -> 162 us (0.76)
  waiting for transfers between devices: 69.1 us -> 3.31 us
  Pallas kernels: 48.3 us -> 65.5 us
  starting transfers between devices: 19 us -> 33.9 us
  blocking collectives: 58.3 us -> 48.9 us
  local copies, waits for them, and re-layouts: 10 us -> 4.44 us
    all_to_all x1, waiting for transfers between devices: 69.1 us -> 0.01 us  [shards(): lax.all_to_all(words, 'col', split_axis=1, concat_axis=0, tiled=True)]
    ppermute x4 -> x11, starting transfers between devices: 5.74 us -> 25.8 us  [the longest x3 11.3 us: send_to_mirror(): lax.ppermute(value, AXES, [(shifted(d, route), mirror_of(d, turn)) for d...]
    pallas_call x2 -> x5, Pallas kernels: 29.9 us -> 40.4 us  [the longest x4 38.1 us: backward_call(): pl.pallas_call(body, out_shape=tuple(outs), grid_spec=pltpu.PrefetchScala...]
    all_to_all x2, blocking collectives: 58.3 us -> 48.9 us  [the longest x1 33.6 us: shards(): lax.all_to_all(both_cores, AXES, split_axis=0, concat_axis=0, axis_index_...]
    pallas_call x2 -> x4, Pallas kernels: 18.4 us -> 25.1 us  [forward_call(): pl.pallas_call(forward_body, out_shape=(jax.ShapeDtypeStruct(pair4.shape,...]
    all_to_all x1, starting transfers between devices: 13.3 us -> 8.15 us  [shards(): lax.all_to_all(words, 'col', split_axis=1, concat_axis=0, tiled=True)]
    unnamed x24, local copies, waits for them, and re-layouts: 7.73 us -> 4.24 us
    ppermute x4 -> x11, waiting for transfers between devices: 0.01 us -> 3.31 us  [the longest x1 1.75 us: shards(): both_cores = (keep + lax.ppermute(send, AXES, sibling)).reshape(64, 16, 128)]
  transfers between devices with their start and end apart: 5 -> 12, of which waited for: 1 -> 2; matrix products, arithmetic and copies ran while one was open for 0% -> 1% of each run, Pallas kernels for 11% -> 33%
where the time goes in v2:
time: 162 us; the launch traced here: 161 us
  Pallas kernels  65.5 us (40%)
  blocking collectives  48.9 us (30%)
  starting transfers between devices  33.9 us (21%)
  local copies, waits for them, and re-layouts  4.44 us (3%)
  other arithmetic  3.75 us (2%)
  waiting for transfers between devices  3.31 us (2%)
    pallas_call x4, Pallas kernels, backward_call(): pl.pallas_call(body, out_shape=tuple(outs), grid_spec=pltpu.PrefetchScala...  38.1 us
    all_to_all x1, blocking collectives, shards(): lax.all_to_all(both_cores, AXES, split_axis=0, concat_axis=0, axis_index_...  33.6 us
    pallas_call x4, Pallas kernels, forward_call(): pl.pallas_call(forward_body, out_shape=(jax.ShapeDtypeStruct(pair4.shape,...  25.1 us
    all_to_all x1, blocking collectives, shards(): lax.all_to_all(jnp.broadcast_to(mine, pieces.shape), AXES, split_axis=0,...  15.3 us
    ppermute x3, starting transfers between devices, send_to_mirror(): lax.ppermute(value, AXES, [(shifted(d, route), mirror_of(d, turn)) for d...  11.3 us
    all_to_all x1, starting transfers between devices, shards(): lax.all_to_all(words, 'col', split_axis=1, concat_axis=0, tiled=True)  8.15 us
    ppermute x3, starting transfers between devices, send_to_mirror(): value = lax.ppermute(value, AXES, [(d, shifted(d, route)) for d in devices])  6.05 us
    unnamed x24, local copies, waits for them, and re-layouts  4.24 us
  transfers between devices with their start and end apart: 12, of which 2 were waited for; matrix products, arithmetic and copies ran while one was open for 1% of the time, Pallas kernels for 33%

profile of v2, /device:TPU:1, one launch (start us, length us, event | category | flops | bytes accessed | tf_op | source)
XLA Modules:
  0.0 160.8 jit_solution(7141511838510009220)
XLA Ops:
  0.6 1.4 add_bitcast_fusion
  2.0 8.2 %all-to-all-start = ((s32[8,8,128]{2,0,1:T(8,128)}), s32[8,8,128]{2,0,1:T(8,128)S(1)}, u32[]{:S(2)}, u32[]{:S(2)}) async-start(s32[8,8,128]{2,0,1:T(8,128)} %add_bitcast_fusion), calls=%async_computation | async-start | bytes 65536 | tf_op jit(solution)/shard_map/words/all_to_all | solution.py:374
  10.8 6.3 %forward.4 = (bf16[64,2,64,128]{3,2,1,0:T(8,128)(2,1)}, bf16[1024,128]{1,0:T(8,128)(2,1)}) custom-call(s32[2]{0:T(128)} %pad_add_fusion.1.which.refs_0_, bf16[64,2,64,128]{3,2,1,0:T(8,128)(2,1)} %bitcast.20, f32[1,128]{1,0:T(1,128)} %bitcast.48, f32[1,128]{1,0:T(1,128)} %bitcast.56, bf16[128,512]{1,0:T(8,128)(2,1)} %refs_8_.7, bf16[128,512]{1,0:T(8,128)(2,1)} %refs_9_.7, ...), custom_call_target="tpu_custom_call" | custom-call | flops 805306368 | bytes 1310720 | tf_op jit(solution)/shard_map/forward/pallas_call | solution.py:133
  17.0 0.7 collective-permute-start.7
  17.7 0.6 copy-done.2
  18.4 6.2 %forward.5 = (bf16[64,2,64,128]{3,2,1,0:T(8,128)(2,1)}, bf16[1024,128]{1,0:T(8,128)(2,1)}) custom-call(s32[2]{0:T(128)} %pad_add_fusion.1.which.refs_0_, bf16[64,2,64,128]{3,2,1,0:T(8,128)(2,1)} %bitcast.21, f32[1,128]{1,0:T(1,128)} %bitcast.49, f32[1,128]{1,0:T(1,128)} %bitcast.57, bf16[128,512]{1,0:T(8,128)(2,1)} %refs_8_.7, ...), custom_call_target="tpu_custom_call", output_to_operand_aliasing={{0}: (8, {})} | custom-call | flops 805306368 | bytes 1310720 | tf_op jit(solution)/shard_map/forward/pallas_call | solution.py:133
  24.6 2.4 %collective-permute-start.4 = (bf16[1024,128]{1,0:T(8,128)(2,1)}, bf16[1024,128]{1,0:T(8,128)(2,1)S(1)}, u32[]{:S(2)}, u32[]{:S(2)}) collective-permute-start(bf16[1024,128]{1,0:T(8,128)(2,1)} %get-tuple-element.43), channel_id=1, source_target_pairs={{0,65},{1,64},{2,67},{3,66},{4,69},{5,68},{6,71},{7,70},{8,73},{9,... | collective-permute-start | bytes 786440 | tf_op jit(solution)/shard_map/ppermute | solution.py:47
  27.0 0.6 pad_add_fusion.which.refs_0_
  27.6 6.4 %forward.6 = (bf16[64,2,64,128]{3,2,1,0:T(8,128)(2,1)}, bf16[1024,128]{1,0:T(8,128)(2,1)}) custom-call(s32[2]{0:T(128)} %pad_add_fusion.which.refs_0_, bf16[64,2,64,128]{3,2,1,0:T(8,128)(2,1)} %bitcast.22, f32[1,128]{1,0:T(1,128)} %bitcast.50, f32[1,128]{1,0:T(1,128)} %bitcast.58, bf16[128,512]{1,0:T(8,128)(2,1)} %refs_8_.7, ...), custom_call_target="tpu_custom_call", output_to_operand_aliasing={{0}: (8, {})} | custom-call | flops 805306368 | bytes 1310720 | tf_op jit(solution)/shard_map/forward/pallas_call | solution.py:133
  33.9 2.9 %collective-permute-start.2 = (bf16[1024,128]{1,0:T(8,128)(2,1)}, bf16[1024,128]{1,0:T(8,128)(2,1)S(1)}, u32[]{:S(2)}, u32[]{:S(2)}) collective-permute-start(bf16[1024,128]{1,0:T(8,128)(2,1)} %get-tuple-element.42), channel_id=1, source_target_pairs={{0,32},{1,33},{2,34},{3,35},{4,36},{5,37},{6,38},{7,39},{8,40},{9,... | collective-permute-start | bytes 786440 | tf_op jit(solution)/shard_map/ppermute | solution.py:47
  36.9 2.8 %collective-permute-start.8 = (bf16[1024,128]{1,0:T(8,128)(2,1)S(1)}, bf16[1024,128]{1,0:T(8,128)(2,1)S(1)}, u32[]{:S(2)}, u32[]{:S(2)}) collective-permute-start(bf16[1024,128]{1,0:T(8,128)(2,1)S(1)} %collective-permute-done.7), channel_id=1, source_target_pairs={{64,0},{65,16},{66,32},{67,48},{68,64},{69,80},{70,96},{71,112},{7... | collective-permute-start | bytes 786440 | tf_op jit(solution)/shard_map/ppermute | solution.py:48
  39.9 0.7 collective-permute-start.6
  40.5 2.7 %collective-permute-start.5 = (bf16[1024,128]{1,0:T(8,128)(2,1)S(1)}, bf16[1024,128]{1,0:T(8,128)(2,1)S(1)}, u32[]{:S(2)}, u32[]{:S(2)}) collective-permute-start(bf16[1024,128]{1,0:T(8,128)(2,1)S(1)} %collective-permute-done.4), channel_id=1, source_target_pairs={{65,0},{64,16},{67,32},{66,48},{69,64},{68,80},{71,96},{70,112},{7... | collective-permute-start | bytes 786440 | tf_op jit(solution)/shard_map/ppermute | solution.py:48
  43.2 6.2 %forward.7 = (bf16[64,2,64,128]{3,2,1,0:T(8,128)(2,1)}, bf16[1024,128]{1,0:T(8,128)(2,1)}) custom-call(s32[2]{0:T(128)} %pad_add_fusion.which.refs_0_, bf16[64,2,64,128]{3,2,1,0:T(8,128)(2,1)} %bitcast.23, f32[1,128]{1,0:T(1,128)} %bitcast.51, f32[1,128]{1,0:T(1,128)} %bitcast.59, bf16[128,512]{1,0:T(8,128)(2,1)} %refs_8_.7, ...), custom_call_target="tpu_custom_call", output_to_operand_aliasing={{0}: (8, {})} | custom-call | flops 805306368 | bytes 1310720 | tf_op jit(solution)/shard_map/forward/pallas_call | solution.py:133
  49.5 2.7 %collective-permute-start.1 = (s32[64,64]{1,0:T(8,128)S(1)}, s32[64,64]{1,0:T(8,128)S(1)}, u32[]{:S(2)}, u32[]{:S(2)}) collective-permute-start(s32[64,64]{1,0:T(8,128)S(1)} %bitcast.42), channel_id=1, source_target_pairs={{0,8},{1,24},{2,40},{3,56},{4,72},{5,88},{6,104},{7,120},{8,0},{9,... | collective-permute-start | bytes 49160 | tf_op jit(solution)/shard_map/ppermute | solution.py:46
  52.3 5.8 %collective-permute-start.3 = (bf16[1024,128]{1,0:T(8,128)(2,1)S(1)}, bf16[1024,128]{1,0:T(8,128)(2,1)S(1)}, u32[]{:S(2)}, u32[]{:S(2)}) collective-permute-start(bf16[1024,128]{1,0:T(8,128)(2,1)S(1)} %collective-permute-done.2), channel_id=1, source_target_pairs={{32,8},{33,24},{34,40},{35,56},{36,72},{37,88},{38,104},{39,120},{... | collective-permute-start | bytes 786440 | tf_op jit(solution)/shard_map/ppermute | solution.py:48
  58.1 0.7 copy-done.6
  58.8 9.2 %backward.4 = (f32[128,1024]{1,0:T(8,128)}, f32[128,512]{1,0:T(8,128)}, f32[256,256]{1,0:T(8,128)}, f32[24,128]{1,0:T(8,128)}) custom-call(s32[2]{0:T(128)} %pad_add_fusion.1.which.refs_0_, bf16[64,2,64,128]{3,2,1,0:T(8,128)(2,1)} %bitcast.24, bf16[64,2,64,128]{3,2,1,0:T(8,128)(2,1)} %get-tuple-element.40.refs_2_, bf16[1024,128]{1,0:T(8,128)(2,1)} %copy-done.6, ...), custom_call_target="tpu_custom_call" | custom-call | flops 2147483648 | bytes 1310720 | tf_op jit(solution)/shard_map/backward/pallas_call | solution.py:309
  68.0 0.7 copy-done.8
  68.6 9.5 %backward.5 = (f32[128,1024]{1,0:T(8,128)}, f32[128,512]{1,0:T(8,128)}, f32[256,256]{1,0:T(8,128)}, f32[24,128]{1,0:T(8,128)}) custom-call(s32[2]{0:T(128)} %pad_add_fusion.1.which.refs_0_, bf16[64,2,64,128]{3,2,1,0:T(8,128)(2,1)} %bitcast.25, bf16[64,2,64,128]{3,2,1,0:T(8,128)(2,1)} %get-tuple-element.40.refs_2_, bf16[1024,128]{1,0:T(8,128)(2,1)} %copy-done.8, ...), custom_call_target="tpu_custom_call" | custom-call | flops 2147483648 | bytes 1310720 | tf_op jit(solution)/shard_map/backward/pallas_call | solution.py:309
  78.9 9.5 %backward.6 = (f32[128,1024]{1,0:T(8,128)}, f32[128,512]{1,0:T(8,128)}, f32[256,256]{1,0:T(8,128)}, f32[24,128]{1,0:T(8,128)}) custom-call(s32[2]{0:T(128)} %pad_add_fusion.which.refs_0_, bf16[64,2,64,128]{3,2,1,0:T(8,128)(2,1)} %bitcast.26, bf16[64,2,64,128]{3,2,1,0:T(8,128)(2,1)} %get-tuple-element.40.refs_2_, bf16[1024,128]{1,0:T(8,128)(2,1)} %copy-done.9, ...), custom_call_target="tpu_custom_call" | custom-call | flops 2147483648 | bytes 1310720 | tf_op jit(solution)/shard_map/backward/pallas_call | solution.py:309
  88.4 0.7 copy-done.7
  89.1 9.9 %backward.7 = (f32[1024,128]{1,0:T(8,128)}, f32[1024,128]{1,0:T(8,128)}) custom-call(s32[2]{0:T(128)} %pad_add_fusion.which.refs_0_, bf16[64,2,64,128]{3,2,1,0:T(8,128)(2,1)} %bitcast.27, bf16[64,2,64,128]{3,2,1,0:T(8,128)(2,1)} %get-tuple-element.40.refs_2_, bf16[1024,128]{1,0:T(8,128)(2,1)} %copy-done.7, s32[64,64]{1,0:T(8,128)} %bitcast.44, ...), custom_call_target="tpu_custom_call" | custom-call | flops 2147483648 | bytes 1310720 | tf_op jit(solution)/shard_map/backward/pallas_call | solution.py:309
  99.1 1.6 %collective-permute-start.9 = (f32[1024,128]{1,0:T(8,128)}, f32[1024,128]{1,0:T(8,128)S(1)}, u32[]{:S(2)}, u32[]{:S(2)}) collective-permute-start(f32[1024,128]{1,0:T(8,128)} %get-tuple-element.58), channel_id=1, source_target_pairs={{0,8},{1,9},{2,10},{3,11},{4,12},{5,13},{6,14},{7,15},{8,0},{9,1},... | collective-permute-start | bytes 1572872 | tf_op jit(solution)/shard_map/ppermute | solution.py:409
  100.7 1.7 %collective-permute-done.9 = f32[1024,128]{1,0:T(8,128)S(1)} collective-permute-done((f32[1024,128]{1,0:T(8,128)}, f32[1024,128]{1,0:T(8,128)S(1)}, u32[]{:S(2)}, u32[]{:S(2)}) %collective-permute-start.9) | collective-permute-done | bytes 524320 | tf_op jit(solution)/shard_map/ppermute | solution.py:409
  102.4 1.1 add.17
  103.6 33.6 %all_to_all.29 = f32[64,16,128]{2,1,0:T(8,128)S(1)} all-to-all(f32[64,16,128]{2,1,0:T(8,128)S(1)} %bitcast.29), channel_id=1, replica_groups={{0,1,2,3,4,5,6,7,16,17,18,19,20,21,22,23,32,33,34,35,36,37,38,39,48,49,..., dimensions={0} | all-to-all | bytes 1048576 | tf_op jit(solution)/shard_map/all_to_all | solution.py:410
  137.3 15.3 %all_to_all.30 = f32[64,16,128]{2,1,0:T(8,128)S(1)} all-to-all(f32[64,16,128]{2,1,0:T(8,128)S(1)} %broadcast_in_dim.2), channel_id=1, replica_groups={{0,1,2,3,4,5,6,7,16,17,18,19,20,21,22,23,32,33,34,35,36,37,38,39,48,49,..., dimensions={0} | all-to-all | bytes 1048576 | tf_op jit(solution)/shard_map/all_to_all | solution.py:414
  152.6 3.4 %collective-permute-start.10 = (f32[1024,128]{1,0:T(8,128)S(1)}, f32[1024,128]{1,0:T(8,128)S(1)}, u32[]{:S(2)}, u32[]{:S(2)}) collective-permute-start(f32[1024,128]{1,0:T(8,128)S(1)} %bitcast.30), channel_id=1, source_target_pairs={{0,8},{1,9},{2,10},{3,11},{4,12},{5,13},{6,14},{7,15},{8,0},{9,1},... | collective-permute-start | bytes 1572872 | tf_op jit(solution)/shard_map/ppermute | solution.py:422
  156.0 1.5 collective-permute-done.10.other
  157.5 0.8 copy-done.1
  158.3 2.3 %unpack.1 = (f32[128,512]{1,0:T(8,128)}, f32[128,512]{1,0:T(8,128)}, f32[512,128]{1,0:T(8,128)}, f32[64,128]{1,0:T(8,128)}, f32[1,128]{1,0:T(1,128)}, /*index=5*/f32[1,128]{1,0:T(1,128)}, f32[1,1]{1,0:T(1,128)}) custom-call(s32[1]{0:T(128)} %bitcast.1.core, f32[1024,128]{1,0:T(8,128)} %bitcast.31, f32[1024,128]{1,0:T(8,128)} %copy-done.1), custom_call_target="tpu_custom_call" | custom-call | tf_op jit(solution)/shard_map/unpack/pallas_call | solution.py:351
  (35 shorter events, 1.7 us)
Async XLA Ops:
  2.0 15.7 %all-to-all-start = ((s32[8,8,128]{2,0,1:T(8,128)}), s32[8,8,128]{2,0,1:T(8,128)S(1)}, u32[]{:S(2)}, u32[]{:S(2)}) async-start(s32[8,8,128]{2,0,1:T(8,128)} %add_bitcast_fusion), calls=%async_computation | async-start | bytes 65536 | tf_op jit(solution)/shard_map/words/all_to_all | solution.py:374
  17.0 19.8 %collective-permute-start.7 = (bf16[1024,128]{1,0:T(8,128)(2,1)}, bf16[1024,128]{1,0:T(8,128)(2,1)S(1)}, u32[]{:S(2)}, u32[]{:S(2)}) collective-permute-start(bf16[1024,128]{1,0:T(8,128)(2,1)} %get-tuple-element.44), channel_id=1, source_target_pairs={{0,64},{1,65},{2,66},{3,67},{4,68},{5,69},{6,70},{7,71},{8,72},{9,... | collective-permute-start | bytes 786440 | tf_op jit(solution)/shard_map/ppermute | solution.py:47
  17.7 0.6 copy-start.2
  24.6 16.0 %collective-permute-start.4 = (bf16[1024,128]{1,0:T(8,128)(2,1)}, bf16[1024,128]{1,0:T(8,128)(2,1)S(1)}, u32[]{:S(2)}, u32[]{:S(2)}) collective-permute-start(bf16[1024,128]{1,0:T(8,128)(2,1)} %get-tuple-element.43), channel_id=1, source_target_pairs={{0,65},{1,64},{2,67},{3,66},{4,69},{5,68},{6,71},{7,70},{8,73},{9,... | collective-permute-start | bytes 786440 | tf_op jit(solution)/shard_map/ppermute | solution.py:47
  27.6 12.1 %copy-start.3 = (s32[8,8,128]{2,0,1:T(8,128)S(1)}, s32[8,8,128]{2,0,1:T(8,128)}, u32[]{:S(2)}) copy-start(s32[8,8,128]{2,0,1:T(8,128)} %copy-done.2) | copy-start | bytes 98308
  33.9 18.4 %collective-permute-start.2 = (bf16[1024,128]{1,0:T(8,128)(2,1)}, bf16[1024,128]{1,0:T(8,128)(2,1)S(1)}, u32[]{:S(2)}, u32[]{:S(2)}) collective-permute-start(bf16[1024,128]{1,0:T(8,128)(2,1)} %get-tuple-element.42), channel_id=1, source_target_pairs={{0,32},{1,33},{2,34},{3,35},{4,36},{5,37},{6,38},{7,39},{8,40},{9,... | collective-permute-start | bytes 786440 | tf_op jit(solution)/shard_map/ppermute | solution.py:47
  36.9 21.2 %collective-permute-start.8 = (bf16[1024,128]{1,0:T(8,128)(2,1)S(1)}, bf16[1024,128]{1,0:T(8,128)(2,1)S(1)}, u32[]{:S(2)}, u32[]{:S(2)}) collective-permute-start(bf16[1024,128]{1,0:T(8,128)(2,1)S(1)} %collective-permute-done.7), channel_id=1, source_target_pairs={{64,0},{65,16},{66,32},{67,48},{68,64},{69,80},{70,96},{71,112},{7... | collective-permute-start | bytes 786440 | tf_op jit(solution)/shard_map/ppermute | solution.py:48
  39.8 9.6 %copy-start.5 = (s32[64,1,64]{2,1,0:T(1,128)}, s32[64,1,64]{2,1,0:T(1,128)S(1)}, u32[]{:S(2)}) copy-start(s32[64,1,64]{2,1,0:T(1,128)S(1)} %get-tuple-element.66) | copy-start | bytes 49156
  39.9 9.6 %copy-start.4 = (s32[64,1,64]{2,1,0:T(1,128)}, s32[64,1,64]{2,1,0:T(1,128)S(1)}, u32[]{:S(2)}) copy-start(s32[64,1,64]{2,1,0:T(1,128)S(1)} %get-tuple-element.67) | copy-start | bytes 49156
  39.9 12.3 %collective-permute-start.6 = (s32[64,64]{1,0:T(8,128)S(1)}, s32[64,64]{1,0:T(8,128)S(1)}, u32[]{:S(2)}, u32[]{:S(2)}) collective-permute-start(s32[64,64]{1,0:T(8,128)S(1)} %bitcast.45), channel_id=1, source_target_pairs={{0,0},{1,16},{2,32},{3,48},{4,64},{5,80},{6,96},{7,112},{8,8},{9,2... | collective-permute-start | bytes 49160 | tf_op jit(solution)/shard_map/ppermute | solution.py:46
  40.5 27.4 %collective-permute-start.5 = (bf16[1024,128]{1,0:T(8,128)(2,1)S(1)}, bf16[1024,128]{1,0:T(8,128)(2,1)S(1)}, u32[]{:S(2)}, u32[]{:S(2)}) collective-permute-start(bf16[1024,128]{1,0:T(8,128)(2,1)S(1)} %collective-permute-done.4), channel_id=1, source_target_pairs={{65,0},{64,16},{67,32},{66,48},{69,64},{68,80},{71,96},{70,112},{7... | collective-permute-start | bytes 786440 | tf_op jit(solution)/shard_map/ppermute | solution.py:48
  49.5 28.7 %collective-permute-start.1 = (s32[64,64]{1,0:T(8,128)S(1)}, s32[64,64]{1,0:T(8,128)S(1)}, u32[]{:S(2)}, u32[]{:S(2)}) collective-permute-start(s32[64,64]{1,0:T(8,128)S(1)} %bitcast.42), channel_id=1, source_target_pairs={{0,8},{1,24},{2,40},{3,56},{4,72},{5,88},{6,104},{7,120},{8,0},{9,... | collective-permute-start | bytes 49160 | tf_op jit(solution)/shard_map/ppermute | solution.py:46
  52.2 5.9 %copy-start.11 = (s32[64,64]{1,0:T(8,128)}, s32[64,64]{1,0:T(8,128)S(1)}, u32[]{:S(2)}) copy-start(s32[64,64]{1,0:T(8,128)S(1)} %collective-permute-done.6.refs_5_) | copy-start | bytes 49156
  52.2 36.3 %collective-permute-start = (bf16[1024,128]{1,0:T(8,128)(2,1)}, bf16[1024,128]{1,0:T(8,128)(2,1)S(1)}, u32[]{:S(2)}, u32[]{:S(2)}) collective-permute-start(bf16[1024,128]{1,0:T(8,128)(2,1)} %get-tuple-element.41), channel_id=1, source_target_pairs={{0,8},{1,24},{2,40},{3,56},{4,72},{5,88},{6,104},{7,120},{8,0},{9,... | collective-permute-start | bytes 786440 | tf_op jit(solution)/shard_map/ppermute | solution.py:46
  52.3 25.9 %collective-permute-start.3 = (bf16[1024,128]{1,0:T(8,128)(2,1)S(1)}, bf16[1024,128]{1,0:T(8,128)(2,1)S(1)}, u32[]{:S(2)}, u32[]{:S(2)}) collective-permute-start(bf16[1024,128]{1,0:T(8,128)(2,1)S(1)} %collective-permute-done.2), channel_id=1, source_target_pairs={{32,8},{33,24},{34,40},{35,56},{36,72},{37,88},{38,104},{39,120},{... | collective-permute-start | bytes 786440 | tf_op jit(solution)/shard_map/ppermute | solution.py:48
  58.1 0.7 copy-start.6
  67.9 0.7 copy-start.8
  78.2 0.6 copy-start.10
  78.2 0.7 copy-start.9
  88.4 0.7 copy-start.7
  99.1 3.4 %collective-permute-start.9 = (f32[1024,128]{1,0:T(8,128)}, f32[1024,128]{1,0:T(8,128)S(1)}, u32[]{:S(2)}, u32[]{:S(2)}) collective-permute-start(f32[1024,128]{1,0:T(8,128)} %get-tuple-element.58), channel_id=1, source_target_pairs={{0,8},{1,9},{2,10},{3,11},{4,12},{5,13},{6,14},{7,15},{8,0},{9,1},... | collective-permute-start | bytes 1572872 | tf_op jit(solution)/shard_map/ppermute | solution.py:409
  152.6 4.9 %copy-start = (f32[64,16,128]{2,1,0:T(8,128)}, f32[64,16,128]{2,1,0:T(8,128)S(1)}, u32[]{:S(2)}) copy-start(f32[64,16,128]{2,1,0:T(8,128)S(1)} %all_to_all.30) | copy-start | bytes 1572868
  152.6 4.9 %collective-permute-start.10 = (f32[1024,128]{1,0:T(8,128)S(1)}, f32[1024,128]{1,0:T(8,128)S(1)}, u32[]{:S(2)}, u32[]{:S(2)}) collective-permute-start(f32[1024,128]{1,0:T(8,128)S(1)} %bitcast.30), channel_id=1, source_target_pairs={{0,8},{1,9},{2,10},{3,11},{4,12},{5,13},{6,14},{7,15},{8,0},{9,1},... | collective-permute-start | bytes 1572872 | tf_op jit(solution)/shard_map/ppermute | solution.py:422
  157.5 0.8 copy-start.1

commit v3 on v2

--- a/solution.py
+++ b/solution.py
@@ -5,19 +5,20 @@
 from jax.experimental.pallas import tpu as pltpu
 from jax.sharding import PartitionSpec as P
 
+
 EPSILON = 1e-05
 F32 = jnp.float32
 BF16 = jnp.bfloat16
 AXES = ("row", "col")
 
 SIDE = 64
-PARTS = 2
 GROUP = 8
 F_COLS = 16
 B_GROUPS = 2
 ROWS = SIDE * GROUP // 2
-
-ROUTES = ((0, 0, 1), (0, 0, 3), (0, 2, 0), None)
+CHUNK_ROWS = SIDE * SIDE // 4
+
+ROUTES = (((0, 0, 1), None), ((0, 0, 3), (0, 2, 0)))
 
 
 def chip_of(device):
@@ -79,10 +80,17 @@
     )
 
 
-def forward_body(which, pair, gain, bias, w_gate, w_up, w_out, head_t, *rest):
-    pair_out, send, wide = rest[-3:]
+def block_words(words, block):
+    tile = words[...]
+    return jnp.where(block == 0, tile[:, :SIDE], tile[:, SIDE:])
+
+
+def forward_body(turn, core, pair, gain, bias, w_gate, w_up, w_out, head_t, *rest):
+    pair_out, send_a, send_b, wide = rest[-4:]
+    words = rest[:-4]
+    step = pl.program_id(0)
     rows_in = pair[...].reshape(SIDE * F_COLS, 128)
-    count = 4
+    count = 2
     size = SIDE * F_COLS // count
     for k in range(count):
         part = rows_in[k * size : (k + 1) * size]
@@ -96,6 +104,7 @@
         )
         wide[k * size : (k + 1) * size, :] = result.astype(F32)
     head_two = head_square(head_t[...])
+    halves = []
     for grp in range(F_COLS // GROUP):
         left, right = [
             jnp.concatenate(
@@ -108,58 +117,85 @@
             for shift in (0, GROUP // 2)
         ]
         both = jnp.concatenate([left, right], axis=1).astype(BF16)
-        send[grp * ROWS : (grp + 1) * ROWS, :] = dot(both, head_two, NT).astype(BF16)
+        halves.append(dot(both, head_two, NT).astype(BF16))
+    rows = ROWS * F_COLS // GROUP
+    per_chunk = CHUNK_ROWS // rows
+    first_row = pl.multiple_of(lax.rem(step, per_chunk) * rows, rows)
+
+    @pl.when(step < per_chunk)
+    def _():
+        send_a[pl.ds(first_row, rows), :] = jnp.concatenate(halves, axis=0)
+
+    @pl.when(step >= per_chunk)
+    def _():
+        send_b[pl.ds(first_row, rows), :] = jnp.concatenate(halves, axis=0)
+
+    if turn == 0:
+        return
+
+    @pl.when(step == 0)
+    def _():
+        own = block_words(words[0], lax.rem(core[0] + turn, 2))
+        target = jnp.bitwise_and(own, 65535).astype(F32)
+        mask = jnp.right_shift(own, 16).astype(F32)
+        send_b[CHUNK_ROWS:, :] = jnp.concatenate([target, mask], axis=1).astype(BF16)
 
 
 def whole(a):
     return pl.BlockSpec(a.shape, lambda g, w: (0,) * len(a.shape))
 
 
-def forward_call(which, part, pair4, weights, partial=None, after=None):
-    steps = SIDE // PARTS // F_COLS
-    block = pl.BlockSpec((SIDE, 1, F_COLS, 128), lambda g, w: (0, w[0], part * steps + g, 0))
+def block_of(turn, core):
+    return core[0] if turn == 0 else 1 - core[0]
+
+
+def forward_call(core, turn, pair4, weights, words=None, partial=None):
+    steps = SIDE // F_COLS
+    block = pl.BlockSpec((SIDE, 1, F_COLS, 128), lambda g, w: (0, block_of(turn, w), g, 0))
     in_specs = [block] + [whole(a) for a in weights]
     args = [pair4, *weights]
     alias = {}
-    if partial is not None:
+    if turn == 1:
+        in_specs.append(whole(words))
+        args.append(words)
         in_specs.append(pl.BlockSpec(memory_space=pl.ANY))
         alias = {1 + len(args): 0}
         args.append(partial)
-    if after is not None:
-        in_specs.append(pl.BlockSpec(memory_space=pl.ANY))
-        args.append(after)
-    rows = ROWS * F_COLS // GROUP
-    pairs = SIDE * SIDE // PARTS
+    outs = (
+        jax.ShapeDtypeStruct(pair4.shape, BF16),
+        jax.ShapeDtypeStruct((CHUNK_ROWS, 128), BF16),
+        jax.ShapeDtypeStruct((CHUNK_ROWS + turn * SIDE, 128), BF16),
+    )
+    pairs = SIDE * SIDE
+
+    def body(*refs):
+        forward_body(turn, *refs)
+
     return pl.pallas_call(
-        forward_body,
-        out_shape=(
-            jax.ShapeDtypeStruct(pair4.shape, BF16),
-            jax.ShapeDtypeStruct((rows * steps, 128), BF16),
-        ),
+        body,
+        out_shape=outs,
         grid_spec=pltpu.PrefetchScalarGridSpec(
             num_scalar_prefetch=1,
             grid=(steps,),
             in_specs=in_specs,
-            out_specs=(block, pl.BlockSpec((rows, 128), lambda g, w: (g, 0))),
+            out_specs=(block, whole(outs[1]), whole(outs[2])),
             scratch_shapes=[pltpu.VMEM((SIDE * F_COLS, 128), F32)],
         ),
         input_output_aliases=alias,
         cost_estimate=pl.CostEstimate(
             flops=pairs * 2 * 128 * 512 * 3, transcendentals=pairs * 512, bytes_accessed=pairs * 640
         ),
-        compiler_params=pltpu.CompilerParams(dimension_semantics=("arbitrary",)),
+        compiler_params=pltpu.CompilerParams(
+            dimension_semantics=("arbitrary",), vmem_limit_bytes=16 * 1024 * 1024
+        ),
         name="forward",
-    )(which, *args)
-
-
-def code_of(word):
-    return (jnp.bitwise_and(word, 65535) + 64 * jnp.right_shift(word, 16)).astype(F32).astype(BF16)
-
-
-def backward_body(first_group, first, last, which, *refs):
-    pair, pair_out, mirror, own_code, mirror_code = refs[:5]
-    gain, bias, w_gate, w_up, w_out, head_t = refs[5:11]
-    rest = list(refs[11:])
+    )(core, *args)
+
+
+def backward_body(turn, first, last, core, *refs):
+    pair, pair_out, mirror_a, mirror_b, mirror_words, words = refs[:6]
+    gain, bias, w_gate, w_up, w_out, head_t = refs[6:12]
+    rest = list(refs[12:])
     earlier = None
     if not first:
         earlier, rest = rest[:4], rest[4:]
@@ -184,8 +220,17 @@
     sum_bins = jnp.concatenate([same, same], axis=0)
     head_two = head_square(head_t[...])
     head_four = jnp.concatenate([head_two, head_two], axis=0)
-    own = code_of(own_code[...])
-    other = code_of(mirror_code[...])
+    own = block_words(words, lax.rem(core[0] + turn, 2))
+    own = jnp.bitwise_and(own, 65535) + 64 * jnp.right_shift(own, 16)
+    own = own.astype(F32).astype(BF16)
+    if turn == 0:
+        other = block_words(mirror_words, core[0])
+        other = jnp.bitwise_and(other, 65535) + 64 * jnp.right_shift(other, 16)
+        other = other.astype(F32).astype(BF16)
+    else:
+        other = mirror_words[...].astype(F32)
+        other = (other[:, :SIDE] + 64.0 * other[:, SIDE:]).astype(BF16)
+    early = step < CHUNK_ROWS // (B_GROUPS * ROWS)
     pick_n = lax.broadcasted_iota(jnp.int32, (SIDE, 512), 1)
     pick_k = lax.broadcasted_iota(jnp.int32, (SIDE, 512), 0)
     pick_base = pick_n // 128 + (GROUP // 2) * (jnp.bitwise_and(pick_n, 127) // 64)
@@ -195,14 +240,16 @@
         x_out = pair_out[grp * GROUP : (grp + 1) * GROUP].reshape(2 * ROWS, 128)
         both = jnp.concatenate([x_out[:ROWS], x_out[ROWS:]], axis=1)
         half = dot(both, head_two, NT).astype(BF16)
-        logits = half.astype(F32) + mirror[grp * ROWS : (grp + 1) * ROWS, :].astype(F32)
+        rows = slice(grp * ROWS, (grp + 1) * ROWS)
+        mirror = jnp.where(early, mirror_a[rows, :].astype(F32), mirror_b[rows, :].astype(F32))
+        logits = half.astype(F32) + mirror
         expo = 0.5 * jnp.exp(logits)
         high = expo.astype(BF16)
         low = (expo - high.astype(F32)).astype(BF16)
         total = dot(jnp.concatenate([high, low], axis=1), sum_bins)
         log_total = jnp.log(total) + 0.6931471805599453
         soft = jnp.exp(logits - log_total)
-        group = first_group + step * B_GROUPS + grp
+        group = step * B_GROUPS + grp
         pick = (pick_k == pick_base + GROUP * group).astype(F32).astype(BF16)
         codes = []
         for spread in (dot(own, pick, TN), dot(other, pick)):
@@ -265,30 +312,37 @@
 
     at_end = step == pl.num_programs(0) - 1
 
-    @pl.when(jnp.logical_and(at_end, which[1] == 0))
+    @pl.when(jnp.logical_and(at_end, core[0] == 0))
     def _():
         put_in(keep)
         put_rest(send)
 
-    @pl.when(jnp.logical_and(at_end, which[1] != 0))
+    @pl.when(jnp.logical_and(at_end, core[0] != 0))
     def _():
         put_in(send)
         put_rest(keep)
 
 
 def backward_call(
-    which, part, pair4, pair_out4, mirror, own_code, mirror_code, weights, earlier, last
+    core, turn, pair4, pair_out4, mirror_a, mirror_b, mirror_words, words, weights, earlier, last
 ):
     wide, hid = 2 * weights[2].shape[1], weights[4].shape[0]
-    steps = SIDE // PARTS // (GROUP * B_GROUPS)
+    steps = SIDE // (GROUP * B_GROUPS)
     block = pl.BlockSpec(
-        (GROUP * B_GROUPS, 1, SIDE, 128), lambda g, w: (part * steps + g, w[0], 0, 0)
+        (GROUP * B_GROUPS, 1, SIDE, 128), lambda g, w: (g, block_of(turn, w), 0, 0)
     )
     rows = ROWS * B_GROUPS
-    fixed = (own_code, mirror_code, *weights)
-    in_specs = [block, block, pl.BlockSpec((rows, 128), lambda g, w: (g, 0))]
+    half_way = CHUNK_ROWS // rows
+    fixed = (words, *weights)
+    in_specs = [
+        block,
+        block,
+        pl.BlockSpec((rows, 128), lambda g, w: (jnp.minimum(g, half_way - 1), 0)),
+        pl.BlockSpec((rows, 128), lambda g, w: (jnp.maximum(g - half_way, 0), 0)),
+        pl.BlockSpec((SIDE, 128), lambda g, w: (turn * CHUNK_ROWS // SIDE, 0)),
+    ]
     in_specs += [whole(a) for a in fixed]
-    args = [pair4, pair_out4, mirror, *fixed]
+    args = [pair4, pair_out4, mirror_a, mirror_b, mirror_words, *fixed]
     sums = [(128, wide), (128, hid), (256, 256), (24, 128)]
     if earlier is not None:
         in_specs += [whole(a) for a in earlier]
@@ -301,10 +355,10 @@
         pltpu.VMEM((2 * rows, hid), BF16),
         pltpu.VMEM((2 * rows, 128), BF16),
     ]
-    pairs = SIDE * SIDE // PARTS
+    pairs = SIDE * SIDE
 
     def body(*refs):
-        backward_body(part * steps * B_GROUPS, earlier is None, last, *refs)
+        backward_body(turn, earlier is None, last, *refs)
 
     return pl.pallas_call(
         body,
@@ -319,9 +373,11 @@
         cost_estimate=pl.CostEstimate(
             flops=pairs * 2 * 128 * 512 * 8, transcendentals=pairs * 640, bytes_accessed=pairs * 640
         ),
-        compiler_params=pltpu.CompilerParams(dimension_semantics=("arbitrary",)),
+        compiler_params=pltpu.CompilerParams(
+            dimension_semantics=("arbitrary",), vmem_limit_bytes=28 * 1024 * 1024
+        ),
         name="backward",
-    )(which, *args)
+    )(core, *args)
 
 
 def unpack_body(core, mine, other, d_gate, d_up, d_out, d_head, d_gain, d_bias, loss):
@@ -357,6 +413,7 @@
             in_specs=[whole(mine), whole(other)],
             out_specs=tuple(specs),
         ),
+        compiler_params=pltpu.CompilerParams(vmem_limit_bytes=8 * 1024 * 1024),
         name="unpack",
     )(core, mine, other)
 
@@ -364,15 +421,11 @@
 def shards(
     pair, ln_gain, ln_bias, gate_weight, up_weight, out_weight, head_weight, targets, pair_mask
 ):
-    rows_tile, cols_tile, width = pair.shape
-    row = lax.axis_index("row")
-    core = lax.rem(row, 2).astype(jnp.int32)
-    which = [jnp.stack([core, core]), jnp.stack([1 - core, core])]
+    rows_tile, _, width = pair.shape
+    core = lax.rem(lax.axis_index("row"), 2).astype(jnp.int32).reshape(1)
 
     words = targets + 65536 * pair_mask
-    with jax.named_scope("words"):
-        tile_words = lax.all_to_all(words, "col", split_axis=1, concat_axis=0, tiled=True)
-    blocks = tile_words.reshape(rows_tile, 2, SIDE)
+    tile_words = lax.all_to_all(words, "col", split_axis=1, concat_axis=0, tiled=True)
 
     pair4 = pair.reshape(rows_tile, 2, SIDE, width)
     weights = (
@@ -383,27 +436,15 @@
         out_weight,
         head_weight.T,
     )
-    chunks = [(turn, part) for turn in range(2) for part in range(PARTS)]
-    out4 = None
-    mirrors = []
-    own, theirs = [], []
-    for k, (turn, part) in enumerate(chunks):
-        after = tile_words if k == 1 else None
-        out4, sent = forward_call(which[turn], part, pair4, weights, out4, after)
-        if k == 0:
-            for t in range(2):
-                own.append(
-                    lax.dynamic_index_in_dim(blocks, which[t][0], 1, keepdims=False)
-                )
-                theirs.append(send_to_mirror(own[t], t, None))
-        mirrors.append(send_to_mirror(sent, turn, ROUTES[k]))
-    sums = None
-    for k, (turn, part) in enumerate(chunks):
-        sums = backward_call(
-            which[turn], part, pair4, out4, mirrors[k], own[turn], theirs[turn], weights, sums,
-            k == len(chunks) - 1,
-        )
-    keep, send = sums
+    out4, *sent0 = forward_call(core, 0, pair4, weights)
+    words0 = send_to_mirror(tile_words, 0, None)
+    mirror0 = [send_to_mirror(v, 0, route) for v, route in zip(sent0, ROUTES[0])]
+    out4, *sent1 = forward_call(core, 1, pair4, weights, tile_words, out4)
+    mirror1 = [send_to_mirror(v, 1, route) for v, route in zip(sent1, ROUTES[1])]
+    sums = backward_call(core, 0, pair4, out4, *mirror0, words0, tile_words, weights, None, False)
+    keep, send = backward_call(
+        core, 1, pair4, out4, *mirror1, mirror1[1], tile_words, weights, sums, True
+    )
     sibling = [(d, device_at(chip_of(d)[0], 1 - chip_of(d)[1])) for d in range(128)]
     groups = [[d for d in range(128) if chip_of(d)[1] == k] for k in range(2)]
     both_cores = (keep + lax.ppermute(send, AXES, sibling)).reshape(64, 16, 128)
@@ -420,7 +461,7 @@
         tiled=True,
     ).reshape(1024, 128)
     other = lax.ppermute(mine, AXES, sibling)
-    d_gate, d_up, d_out, d_head, d_gain, d_bias, loss = unpack_call(core.reshape(1), mine, other)
+    d_gate, d_up, d_out, d_head, d_gain, d_bias, loss = unpack_call(core, mine, other)
     return (
         out4.reshape(pair.shape),
         loss.reshape(()),

time: 162 us -> 146 us (0.901)
  Pallas kernels: 65.5 us -> 42.1 us
  starting transfers between devices: 33.9 us -> 43.4 us
  other arithmetic: 3.75 us -> 0.13 us
  local copies, waits for them, and re-layouts: 4.44 us -> 7.99 us
    ppermute x3, starting transfers between devices: 11.3 us -> 31.8 us  [send_to_mirror(): lax.ppermute(value, AXES, [(shifted(d, route), mirror_of(d, turn)) for d...]
    all_to_all x1, blocking collectives: 33.6 us -> 19.5 us  [shards(): lax.all_to_all(both_cores, AXES, split_axis=0, concat_axis=0, axis_index_...]
    all_to_all x0 -> x1, blocking collectives: none -> 13.4 us  [shards(): lax.all_to_all(words, 'col', split_axis=1, concat_axis=0, tiled=True)]
    pallas_call x4 -> x2, Pallas kernels: 38.1 us -> 26.2 us  [backward_call(): pl.pallas_call(body, out_shape=tuple(outs), grid_spec=pltpu.PrefetchScala...]
    pallas_call x4 -> x2, Pallas kernels: 25.1 us -> 14.8 us  [forward_call(): pl.pallas_call(body, out_shape=outs, grid_spec=pltpu.PrefetchScalarGridSp...]
    all_to_all x1 -> x0, starting transfers between devices: 8.15 us -> none  [shards(): lax.all_to_all(words, 'col', split_axis=1, concat_axis=0, tiled=True)]
    unnamed x24 -> x34, local copies, waits for them, and re-layouts: 4.24 us -> 7.95 us
    ppermute x3 -> x2, starting transfers between devices: 3.48 us -> 1.32 us  [send_to_mirror(): return lax.ppermute(value, AXES, [(d, mirror_of(d, turn)) for d in devices])]
  transfers between devices with their start and end apart: 12 -> 10, of which waited for: 2 -> 2; matrix products, arithmetic and copies ran while one was open for 1% -> 0% of each run, Pallas kernels for 33% -> 14%
where the time goes in v3:
time: 146 us
  blocking collectives  48.3 us (33%)
  starting transfers between devices  43.4 us (30%)
  Pallas kernels  42.1 us (29%)
  local copies, waits for them, and re-layouts  7.99 us (5%)
  waiting for transfers between devices  3.09 us (2%)
    ppermute x3, starting transfers between devices, send_to_mirror(): lax.ppermute(value, AXES, [(shifted(d, route), mirror_of(d, turn)) for d...  31.8 us
    pallas_call x2, Pallas kernels, backward_call(): pl.pallas_call(body, out_shape=tuple(outs), grid_spec=pltpu.PrefetchScala...  26.2 us
    all_to_all x1, blocking collectives, shards(): lax.all_to_all(both_cores, AXES, split_axis=0, concat_axis=0, axis_index_...  19.5 us
    all_to_all x1, blocking collectives, shards(): lax.all_to_all(jnp.broadcast_to(mine, pieces.shape), AXES, split_axis=0,...  15.3 us
    pallas_call x2, Pallas kernels, forward_call(): pl.pallas_call(body, out_shape=outs, grid_spec=pltpu.PrefetchScalarGridSp...  14.8 us
    all_to_all x1, blocking collectives, shards(): lax.all_to_all(words, 'col', split_axis=1, concat_axis=0, tiled=True)  13.4 us
    unnamed x34, local copies, waits for them, and re-layouts  7.95 us
    ppermute x3, starting transfers between devices, send_to_mirror(): value = lax.ppermute(value, AXES, [(d, shifted(d, route)) for d in devices])  5.38 us
  transfers between devices with their start and end apart: 10, of which 2 were waited for; matrix products, arithmetic and copies ran while one was open for 0% of the time, Pallas kernels for 14%

profile of v3, /device:TPU:1, one launch (start us, length us, event | category | flops | bytes accessed | tf_op | source)
XLA Modules:
  0.0 146.0 jit_solution(13414782740350913872)
XLA Ops:
  0.6 0.0 copy-start
  0.7 1.6 %copy-done = bf16[64,128,128]{2,1,0:T(8,128)(2,1)S(1)} copy-done((bf16[64,128,128]{2,1,0:T(8,128)(2,1)S(1)}, bf16[64,128,128]{2,1,0:T(8,128)(2,1)}, u32[]{:S(2)}) %copy-start) | copy-done | bytes 2097176
  2.2 0.9 copy-done.2
  3.1 0.9 copy-done.4
  4.0 0.9 copy-done.6
  4.9 0.7 copy-done.8
  5.7 0.7 copy-done.10
  6.3 0.7 copy-done.12
  7.0 7.3 %forward.2 = (bf16[64,2,64,128]{3,2,1,0:T(8,128)(2,1)}, bf16[1024,128]{1,0:T(8,128)(2,1)S(1)}, bf16[1024,128]{1,0:T(8,128)(2,1)S(1)}) custom-call(s32[1]{0:T(128)} %bitcast.refs_0_.core, bf16[64,2,64,128]{3,2,1,0:T(8,128)(2,1)S(1)} %bitcast.23, f32[1,128]{1,0:T(1,128)S(1)} %bitcast.31, f32[1,128]{1,0:T(1,128)S(1)} %bitcast.35, ...), custom_call_target="tpu_custom_call" | custom-call | flops 1610612736 | bytes 2621440 | tf_op jit(solution)/shard_map/forward/pallas_call | solution.py:174
  14.3 2.5 %collective-permute-start.4 = (bf16[1024,128]{1,0:T(8,128)(2,1)S(1)}, bf16[1024,128]{1,0:T(8,128)(2,1)S(1)}, u32[]{:S(2)}, u32[]{:S(2)}) collective-permute-start(bf16[1024,128]{1,0:T(8,128)(2,1)S(1)} %get-tuple-element.31), channel_id=1, source_target_pairs={{0,64},{1,65},{2,66},{3,67},{4,68},{5,69},{6,70},{7,71},{8,72},{9,... | collective-permute-start | bytes 786440 | tf_op jit(solution)/shard_map/ppermute | solution.py:48
  16.8 13.4 %all_to_all.29 = s32[8,8,128]{2,0,1:T(8,128)S(1)} all-to-all(s32[8,8,128]{2,0,1:T(8,128)S(1)} %add_bitcast_fusion), channel_id=1, replica_groups=mesh['row'=16,'col'=8] {'col'}, dimensions={1} | all-to-all | bytes 65536 | tf_op jit(solution)/shard_map/all_to_all | solution.py:428
  30.2 0.0 copy-start.11
  30.2 0.0 copy-start.13
  30.2 7.5 %forward.3 = (bf16[64,2,64,128]{3,2,1,0:T(8,128)(2,1)}, bf16[1024,128]{1,0:T(8,128)(2,1)S(1)}, bf16[1088,128]{1,0:T(8,128)(2,1)S(1)}) custom-call(s32[1]{0:T(128)} %bitcast.refs_0_.core, bf16[64,2,64,128]{3,2,1,0:T(8,128)(2,1)S(1)} %bitcast.24, f32[1,128]{1,0:T(1,128)S(1)} %bitcast.32, f32[1,128]{1,0:T(1,128)S(1)} %bitcast.36, ...), custom_call_target="tpu_custom_call", output_to_operand_aliasing={{0}: (9, {})} | custom-call | flops 1610612736 | bytes 2621440 | tf_op jit(solution)/shard_map/forward/pallas_call | solution.py:174
  37.8 2.9 %collective-permute-start.2 = (bf16[1088,128]{1,0:T(8,128)(2,1)S(1)}, bf16[1088,128]{1,0:T(8,128)(2,1)S(1)}, u32[]{:S(2)}, u32[]{:S(2)}) collective-permute-start(bf16[1088,128]{1,0:T(8,128)(2,1)S(1)} %get-tuple-element.30), channel_id=1, source_target_pairs={{0,32},{1,33},{2,34},{3,35},{4,36},{5,37},{6,38},{7,39},{8,40},{9,... | collective-permute-start | bytes 835592 | tf_op jit(solution)/shard_map/ppermute | solution.py:48
  40.7 0.7 collective-permute-start.6
  41.4 5.6 %collective-permute-start.5 = (bf16[1024,128]{1,0:T(8,128)(2,1)S(1)}, bf16[1024,128]{1,0:T(8,128)(2,1)S(1)}, u32[]{:S(2)}, u32[]{:S(2)}) collective-permute-start(bf16[1024,128]{1,0:T(8,128)(2,1)S(1)} %collective-permute-done.4), channel_id=1, source_target_pairs={{64,0},{65,16},{66,32},{67,48},{68,64},{69,80},{70,96},{71,112},{7... | collective-permute-start | bytes 786440 | tf_op jit(solution)/shard_map/ppermute | solution.py:49
  46.9 0.7 collective-permute-start.7
  47.6 15.4 %collective-permute-start.1 = (bf16[1024,128]{1,0:T(8,128)(2,1)S(1)}, bf16[1024,128]{1,0:T(8,128)(2,1)S(1)}, u32[]{:S(2)}, u32[]{:S(2)}) collective-permute-start(bf16[1024,128]{1,0:T(8,128)(2,1)S(1)} %collective-permute-done), channel_id=1, source_target_pairs={{65,8},{64,24},{67,40},{66,56},{69,72},{68,88},{71,104},{70,120},{... | collective-permute-start | bytes 786440 | tf_op jit(solution)/shard_map/ppermute | solution.py:49
  63.0 10.8 %collective-permute-start.3 = (bf16[1088,128]{1,0:T(8,128)(2,1)S(1)}, bf16[1088,128]{1,0:T(8,128)(2,1)S(1)}, u32[]{:S(2)}, u32[]{:S(2)}) collective-permute-start(bf16[1088,128]{1,0:T(8,128)(2,1)S(1)} %collective-permute-done.2), channel_id=1, source_target_pairs={{32,8},{33,24},{34,40},{35,56},{36,72},{37,88},{38,104},{39,120},{... | collective-permute-start | bytes 835592 | tf_op jit(solution)/shard_map/ppermute | solution.py:49
  73.9 1.6 %copy-done.14 = bf16[64,2,64,128]{3,2,1,0:T(8,128)(2,1)S(1)} copy-done((bf16[64,2,64,128]{3,2,1,0:T(8,128)(2,1)S(1)}, bf16[64,2,64,128]{3,2,1,0:T(8,128)(2,1)}, u32[]{:S(2)}) %copy-start.14) | copy-done | bytes 2097176
  75.5 13.0 %backward.2 = (f32[128,1024]{1,0:T(8,128)S(1)}, f32[128,512]{1,0:T(8,128)S(1)}, f32[256,256]{1,0:T(8,128)S(1)}, f32[24,128]{1,0:T(8,128)S(1)}) custom-call(s32[1]{0:T(128)} %bitcast.refs_0_.core, bf16[64,2,64,128]{3,2,1,0:T(8,128)(2,1)S(1)} %bitcast.25, bf16[64,2,64,128]{3,2,1,0:T(8,128)(2,1)S(1)} %copy-done.14, ...), custom_call_target="tpu_custom_call" | custom-call | flops 4294967296 | bytes 2621440 | tf_op jit(solution)/shard_map/backward/pallas_call | solution.py:363
  88.5 13.2 %backward.3 = (f32[1024,128]{1,0:T(8,128)S(1)}, f32[1024,128]{1,0:T(8,128)S(1)}) custom-call(s32[1]{0:T(128)} %bitcast.refs_0_.core, bf16[64,2,64,128]{3,2,1,0:T(8,128)(2,1)S(1)} %bitcast.26, bf16[64,2,64,128]{3,2,1,0:T(8,128)(2,1)S(1)} %copy-done.14, bf16[1024,128]{1,0:T(8,128)(2,1)S(1)} %collective-permute-done.1.refs_3_, ...), custom_call_target="tpu_custom_call" | custom-call | flops 4294967296 | bytes 2621440 | tf_op jit(solution)/shard_map/backward/pallas_call | solution.py:363
  101.7 1.6 %collective-permute-start.8 = (f32[1024,128]{1,0:T(8,128)S(1)}, f32[1024,128]{1,0:T(8,128)S(1)}, u32[]{:S(2)}, u32[]{:S(2)}) collective-permute-start(f32[1024,128]{1,0:T(8,128)S(1)} %get-tuple-element.38), channel_id=1, source_target_pairs={{0,8},{1,9},{2,10},{3,11},{4,12},{5,13},{6,14},{7,15},{8,0},{9,1},... | collective-permute-start | bytes 1572872 | tf_op jit(solution)/shard_map/ppermute | solution.py:450
  103.3 1.5 %collective-permute-done.8 = f32[1024,128]{1,0:T(8,128)S(1)} collective-permute-done((f32[1024,128]{1,0:T(8,128)S(1)}, f32[1024,128]{1,0:T(8,128)S(1)}, u32[]{:S(2)}, u32[]{:S(2)}) %collective-permute-start.8) | collective-permute-done | bytes 524320 | tf_op jit(solution)/shard_map/ppermute | solution.py:450
  104.8 0.1 add.7
  104.9 19.5 %all_to_all.30 = f32[64,16,128]{2,1,0:T(8,128)S(1)} all-to-all(f32[64,16,128]{2,1,0:T(8,128)S(1)} %bitcast.40), channel_id=1, replica_groups={{0,1,2,3,4,5,6,7,16,17,18,19,20,21,22,23,32,33,34,35,36,37,38,39,48,49,..., dimensions={0} | all-to-all | bytes 1048576 | tf_op jit(solution)/shard_map/all_to_all | solution.py:451
  124.4 0.1 reduce_sum.9
  124.5 15.3 %all_to_all.31 = f32[64,16,128]{2,1,0:T(8,128)S(1)} all-to-all(f32[64,16,128]{2,1,0:T(8,128)S(1)} %broadcast_in_dim.2), channel_id=1, replica_groups={{0,1,2,3,4,5,6,7,16,17,18,19,20,21,22,23,32,33,34,35,36,37,38,39,48,49,..., dimensions={0} | all-to-all | bytes 1048576 | tf_op jit(solution)/shard_map/all_to_all | solution.py:455
  139.8 3.3 %collective-permute-start.9 = (f32[1024,128]{1,0:T(8,128)S(1)}, f32[1024,128]{1,0:T(8,128)S(1)}, u32[]{:S(2)}, u32[]{:S(2)}) collective-permute-start(f32[1024,128]{1,0:T(8,128)S(1)} %bitcast.17), channel_id=1, source_target_pairs={{0,8},{1,9},{2,10},{3,11},{4,12},{5,13},{6,14},{7,15},{8,0},{9,1},... | collective-permute-start | bytes 1572872 | tf_op jit(solution)/shard_map/ppermute | solution.py:463
  143.2 1.5 %collective-permute-done.9.other = f32[1024,128]{1,0:T(8,128)S(1)} collective-permute-done((f32[1024,128]{1,0:T(8,128)S(1)}, f32[1024,128]{1,0:T(8,128)S(1)}, u32[]{:S(2)}, u32[]{:S(2)}) %collective-permute-start.9) | collective-permute-done | bytes 524320 | tf_op jit(solution)/shard_map/ppermute | solution.py:463
  144.7 1.1 unpack.1
  (34 shorter events, 0.1 us)
Async XLA Ops:
  0.6 1.6 %copy-start = (bf16[64,128,128]{2,1,0:T(8,128)(2,1)S(1)}, bf16[64,128,128]{2,1,0:T(8,128)(2,1)}, u32[]{:S(2)}) copy-start(bf16[64,128,128]{2,1,0:T(8,128)(2,1)} %param.9) | copy-start | bytes 6291460
  2.2 0.9 copy-start.2
  3.1 0.9 copy-start.4
  4.0 0.9 copy-start.6
  4.9 0.7 copy-start.8
  5.7 0.7 copy-start.10
  6.3 0.7 copy-start.12
  7.0 9.8 %copy-start.15 = (s32[8,1024]{1,0:T(8,128)S(1)}, s32[8,1024]{1,0:T(8,128)}, u32[]{:S(2)}) copy-start(s32[8,1024]{1,0:T(8,128)} %param.16) | copy-start | bytes 98308
  7.0 9.8 %copy-start.16 = (s32[8,1024]{1,0:T(8,128)S(1)}, s32[8,1024]{1,0:T(8,128)}, u32[]{:S(2)}) copy-start(s32[8,1024]{1,0:T(8,128)} %param.17) | copy-start | bytes 98308
  14.3 27.0 %collective-permute-start.4 = (bf16[1024,128]{1,0:T(8,128)(2,1)S(1)}, bf16[1024,128]{1,0:T(8,128)(2,1)S(1)}, u32[]{:S(2)}, u32[]{:S(2)}) collective-permute-start(bf16[1024,128]{1,0:T(8,128)(2,1)S(1)} %get-tuple-element.31), channel_id=1, source_target_pairs={{0,64},{1,65},{2,66},{3,67},{4,68},{5,69},{6,70},{7,71},{8,72},{9,... | collective-permute-start | bytes 786440 | tf_op jit(solution)/shard_map/ppermute | solution.py:48
  30.2 43.6 %copy-start.1 = (bf16[64,128,128]{2,1,0:T(8,128)(2,1)S(1)}, bf16[64,128,128]{2,1,0:T(8,128)(2,1)}, u32[]{:S(2)}) copy-start(bf16[64,128,128]{2,1,0:T(8,128)(2,1)} %param.9) | copy-start | bytes 6291460
  30.2 43.6 %copy-start.3 = (bf16[128,512]{1,0:T(8,128)(2,1)S(1)}, bf16[128,512]{1,0:T(8,128)(2,1)}, u32[]{:S(2)}) copy-start(bf16[128,512]{1,0:T(8,128)(2,1)} %refs_9_.3) | copy-start | bytes 393220
  30.2 43.6 %copy-start.5 = (bf16[128,512]{1,0:T(8,128)(2,1)S(1)}, bf16[128,512]{1,0:T(8,128)(2,1)}, u32[]{:S(2)}) copy-start(bf16[128,512]{1,0:T(8,128)(2,1)} %refs_10_.3) | copy-start | bytes 393220
  30.2 43.6 %copy-start.7 = (bf16[512,128]{1,0:T(8,128)(2,1)S(1)}, bf16[512,128]{1,0:T(8,128)(2,1)}, u32[]{:S(2)}) copy-start(bf16[512,128]{1,0:T(8,128)(2,1)} %refs_11_.3) | copy-start | bytes 393220
  30.2 43.6 %copy-start.9 = (bf16[128,64]{0,1:T(8,128)(2,1)S(1)}, bf16[128,64]{0,1:T(8,128)(2,1)}, u32[]{:S(2)}) copy-start(bf16[128,64]{0,1:T(8,128)(2,1)} %param.15) | copy-start | bytes 49156
  30.2 43.6 %copy-start.11 = (f32[128]{0:T(128)S(1)}, f32[128]{0:T(128)}, u32[]{:S(2)}) copy-start(f32[128]{0:T(128)} %param.10) | copy-start | bytes 1540
  30.2 43.6 %copy-start.13 = (f32[128]{0:T(128)S(1)}, f32[128]{0:T(128)}, u32[]{:S(2)}) copy-start(f32[128]{0:T(128)} %param.11) | copy-start | bytes 1540
  37.8 25.3 %collective-permute-start.2 = (bf16[1088,128]{1,0:T(8,128)(2,1)S(1)}, bf16[1088,128]{1,0:T(8,128)(2,1)S(1)}, u32[]{:S(2)}, u32[]{:S(2)}) collective-permute-start(bf16[1088,128]{1,0:T(8,128)(2,1)S(1)} %get-tuple-element.30), channel_id=1, source_target_pairs={{0,32},{1,33},{2,34},{3,35},{4,36},{5,37},{6,38},{7,39},{8,40},{9,... | collective-permute-start | bytes 835592 | tf_op jit(solution)/shard_map/ppermute | solution.py:48
  40.7 6.9 %collective-permute-start = (bf16[1024,128]{1,0:T(8,128)(2,1)S(1)}, bf16[1024,128]{1,0:T(8,128)(2,1)S(1)}, u32[]{:S(2)}, u32[]{:S(2)}) collective-permute-start(bf16[1024,128]{1,0:T(8,128)(2,1)S(1)} %get-tuple-element.29), channel_id=1, source_target_pairs={{0,65},{1,64},{2,67},{3,66},{4,69},{5,68},{6,71},{7,70},{8,73},{9,... | collective-permute-start | bytes 786440 | tf_op jit(solution)/shard_map/ppermute | solution.py:48
  40.7 33.1 %collective-permute-start.6 = (bf16[1024,128]{1,0:T(8,128)(2,1)S(1)}, bf16[1024,128]{1,0:T(8,128)(2,1)S(1)}, u32[]{:S(2)}, u32[]{:S(2)}) collective-permute-start(bf16[1024,128]{1,0:T(8,128)(2,1)S(1)} %get-tuple-element.32), channel_id=1, source_target_pairs={{0,0},{1,16},{2,32},{3,48},{4,64},{5,80},{6,96},{7,112},{8,8},{9,2... | collective-permute-start | bytes 786440 | tf_op jit(solution)/shard_map/ppermute | solution.py:47
  41.4 32.4 %collective-permute-start.5 = (bf16[1024,128]{1,0:T(8,128)(2,1)S(1)}, bf16[1024,128]{1,0:T(8,128)(2,1)S(1)}, u32[]{:S(2)}, u32[]{:S(2)}) collective-permute-start(bf16[1024,128]{1,0:T(8,128)(2,1)S(1)} %collective-permute-done.4), channel_id=1, source_target_pairs={{64,0},{65,16},{66,32},{67,48},{68,64},{69,80},{70,96},{71,112},{7... | collective-permute-start | bytes 786440 | tf_op jit(solution)/shard_map/ppermute | solution.py:49
  46.9 26.9 %collective-permute-start.7 = (s32[64,128]{1,0:T(8,128)S(1)}, s32[64,128]{1,0:T(8,128)S(1)}, u32[]{:S(2)}, u32[]{:S(2)}) collective-permute-start(s32[64,128]{1,0:T(8,128)S(1)} %bitcast.20), channel_id=1, source_target_pairs={{0,0},{1,16},{2,32},{3,48},{4,64},{5,80},{6,96},{7,112},{8,8},{9,2... | collective-permute-start | bytes 98312 | tf_op jit(solution)/shard_map/ppermute | solution.py:47
  47.6 40.9 %collective-permute-start.1 = (bf16[1024,128]{1,0:T(8,128)(2,1)S(1)}, bf16[1024,128]{1,0:T(8,128)(2,1)S(1)}, u32[]{:S(2)}, u32[]{:S(2)}) collective-permute-start(bf16[1024,128]{1,0:T(8,128)(2,1)S(1)} %collective-permute-done), channel_id=1, source_target_pairs={{65,8},{64,24},{67,40},{66,56},{69,72},{68,88},{71,104},{70,120},{... | collective-permute-start | bytes 786440 | tf_op jit(solution)/shard_map/ppermute | solution.py:49
  63.0 25.5 %collective-permute-start.3 = (bf16[1088,128]{1,0:T(8,128)(2,1)S(1)}, bf16[1088,128]{1,0:T(8,128)(2,1)S(1)}, u32[]{:S(2)}, u32[]{:S(2)}) collective-permute-start(bf16[1088,128]{1,0:T(8,128)(2,1)S(1)} %collective-permute-done.2), channel_id=1, source_target_pairs={{32,8},{33,24},{34,40},{35,56},{36,72},{37,88},{38,104},{39,120},{... | collective-permute-start | bytes 835592 | tf_op jit(solution)/shard_map/ppermute | solution.py:49
  73.9 1.6 %copy-start.14 = (bf16[64,2,64,128]{3,2,1,0:T(8,128)(2,1)S(1)}, bf16[64,2,64,128]{3,2,1,0:T(8,128)(2,1)}, u32[]{:S(2)}) copy-start(bf16[64,2,64,128]{3,2,1,0:T(8,128)(2,1)} %get-tuple-element.28.refs_2_) | copy-start | bytes 6291460
  101.7 3.1 %collective-permute-start.8 = (f32[1024,128]{1,0:T(8,128)S(1)}, f32[1024,128]{1,0:T(8,128)S(1)}, u32[]{:S(2)}, u32[]{:S(2)}) collective-permute-start(f32[1024,128]{1,0:T(8,128)S(1)} %get-tuple-element.38), channel_id=1, source_target_pairs={{0,8},{1,9},{2,10},{3,11},{4,12},{5,13},{6,14},{7,15},{8,0},{9,1},... | collective-permute-start | bytes 1572872 | tf_op jit(solution)/shard_map/ppermute | solution.py:450
  139.8 4.9 %collective-permute-start.9 = (f32[1024,128]{1,0:T(8,128)S(1)}, f32[1024,128]{1,0:T(8,128)S(1)}, u32[]{:S(2)}, u32[]{:S(2)}) collective-permute-start(f32[1024,128]{1,0:T(8,128)S(1)} %bitcast.17), channel_id=1, source_target_pairs={{0,8},{1,9},{2,10},{3,11},{4,12},{5,13},{6,14},{7,15},{8,0},{9,1},... | collective-permute-start | bytes 1572872 | tf_op jit(solution)/shard_map/ppermute | solution.py:463

commit v4 on v3

--- a/solution.py
+++ b/solution.py
@@ -18,7 +18,7 @@
 ROWS = SIDE * GROUP // 2
 CHUNK_ROWS = SIDE * SIDE // 4
 
-ROUTES = (((0, 0, 1), None), ((0, 0, 3), (0, 2, 0)))
+ROUTES = (((0, 0, 1), (0, 0, 3)), ((0, 2, 0), None))
 
 
 def chip_of(device):
@@ -62,7 +62,8 @@
     centered = values - jnp.mean(values, axis=-1, keepdims=True)
     variance = jnp.mean(centered * centered, axis=-1, keepdims=True)
     unit_rows = centered * lax.rsqrt(variance + EPSILON)
-    return unit_rows, (unit_rows * gain + bias).astype(BF16)
+    scaled = unit_rows * gain + bias
+    return scaled, scaled.astype(BF16)
 
 
 def sigmoid(values):
@@ -192,18 +193,74 @@
     )(core, *args)
 
 
+def prepare_body(core, pair, gain, bias, w_gate, w_up, left, silu, up_slope, hidden):
+    rows_in = pair[...].reshape(-1, 128)
+    count = 2
+    size = rows_in.shape[0] // count
+    for k in range(count):
+        at = slice(k * size, (k + 1) * size)
+        scaled, normed = normalize(rows_in[at], gain[...], bias[...])
+        left[at, :128] = normed
+        left[at, 128:] = (normed.astype(F32) - scaled).astype(BF16)
+        gate_pre = dot(normed, w_gate[...])
+        up_pre = dot(normed, w_up[...])
+        squashed = sigmoid(gate_pre)
+        silu_val = gate_pre * squashed
+        silu[at, :] = silu_val
+        hidden[at, :] = (silu_val * up_pre).astype(BF16)
+        up_slope[at, :] = up_pre * (squashed * (1.0 + gate_pre * (1.0 - squashed)))
+
+
+def prepare_call(core, pair4, gain, bias, w_gate, w_up):
+    hid = w_gate.shape[1]
+    steps = SIDE // (GROUP * B_GROUPS)
+    first = GROUP * B_GROUPS
+    rows = first * SIDE
+    pairs = 2 * SIDE * SIDE
+    outs = (
+        jax.ShapeDtypeStruct((pairs, 256), BF16),
+        jax.ShapeDtypeStruct((pairs, hid), F32),
+        jax.ShapeDtypeStruct((pairs, hid), F32),
+        jax.ShapeDtypeStruct((pairs, hid), BF16),
+    )
+    args = (pair4, gain, bias, w_gate, w_up)
+    return pl.pallas_call(
+        prepare_body,
+        out_shape=outs,
+        grid_spec=pltpu.PrefetchScalarGridSpec(
+            num_scalar_prefetch=1,
+            grid=(2 * steps,),
+            in_specs=[
+                pl.BlockSpec(
+                    (first, 1, SIDE, 128),
+                    lambda g, w: (lax.rem(g, steps), lax.rem(w[0] + g // steps, 2), 0, 0),
+                )
+            ]
+            + [whole(a) for a in args[1:]],
+            out_specs=tuple(pl.BlockSpec((rows, a.shape[1]), lambda g, w: (g, 0)) for a in outs),
+        ),
+        cost_estimate=pl.CostEstimate(
+            flops=pairs * 2 * 128 * 512 * 2, transcendentals=pairs * 512, bytes_accessed=pairs * 5888
+        ),
+        compiler_params=pltpu.CompilerParams(
+            dimension_semantics=("arbitrary",), vmem_limit_bytes=28 * 1024 * 1024
+        ),
+        name="prepare",
+    )(core, *args)
+
+
 def backward_body(turn, first, last, core, *refs):
-    pair, pair_out, mirror_a, mirror_b, mirror_words, words = refs[:6]
-    gain, bias, w_gate, w_up, w_out, head_t = refs[6:12]
-    rest = list(refs[12:])
+    left, silu, up_slope, hidden, pair_out, mirror_a, mirror_b, mirror_words, words = refs[:9]
+    gain, bias, w_gate, w_up, w_out, head_t = refs[9:15]
+    rest = list(refs[15:])
     earlier = None
     if not first:
-        earlier, rest = rest[:4], rest[4:]
+        earlier, rest = rest[:5], rest[5:]
     if last:
         keep, send = rest[:2]
         rest = rest[2:]
-    g_in, g_out, g_head, g_small, s_normed, s_grad_in, s_hidden, s_pair = rest
-    sums = (g_in, g_out, g_head, g_small)
+    g_in, g_out, g_head, g_cols, g_loss, s_grad_in, s_pair = rest
+    sums = (g_in, g_out, g_head, g_cols, g_loss)
     hid = w_out.shape[0]
     step = pl.program_id(0)
 
@@ -269,33 +326,24 @@
         grad_pair = jnp.concatenate([grad_pair[:, :128], grad_pair[:, 128:]], axis=0)
         s_pair[at, :] = grad_pair
 
-        x_in = pair[grp * GROUP : (grp + 1) * GROUP].reshape(2 * ROWS, 128)
-        unit_rows, normed = normalize(x_in, gain[...], bias[...])
-        s_normed[at, :] = normed
-        gate_pre = dot(normed, w_gate[...])
-        up_pre = dot(normed, w_up[...])
         grad_hidden = dot(grad_pair, w_out[...], NT)
-        squashed = sigmoid(gate_pre)
-        silu_val = gate_pre * squashed
-        s_hidden[at, :] = (silu_val * up_pre).astype(BF16)
-        slope = squashed * (1.0 + gate_pre * (1.0 - squashed))
-        s_grad_in[at, :hid] = (grad_hidden * up_pre * slope).astype(BF16)
-        s_grad_in[at, hid:] = (grad_hidden * silu_val).astype(BF16)
-        grad_normed = dot(s_grad_in[at, :hid], w_gate[...], NT)
-        grad_normed += dot(s_grad_in[at, hid:], w_up[...], NT)
-        fold = lambda v: jnp.sum(v.reshape(-1, 8, 128), axis=0)
-        g_small[0:8, :] += fold(grad_normed * unit_rows)
-        g_small[8:16, :] += fold(grad_normed)
-        g_small[16:24, :] += fold(loss_part)
-    g_in[...] += dot(s_normed[...], s_grad_in[...], TN)
-    g_out[...] += dot(s_pair[...], s_hidden[...], TN)
+        fold = lambda v: jnp.sum(v.astype(F32).reshape(-1, 8, v.shape[1]), axis=0)
+        grad_gate_pre = (grad_hidden * up_slope[at, :]).astype(BF16)
+        grad_up_pre = (grad_hidden * silu[at, :]).astype(BF16)
+        s_grad_in[at, :hid] = grad_gate_pre
+        s_grad_in[at, hid:] = grad_up_pre
+        g_cols[:, :hid] += fold(grad_gate_pre)
+        g_cols[:, hid:] += fold(grad_up_pre)
+        g_loss[...] += fold(loss_part)
+    g_in[...] += dot(left[...], s_grad_in[...], TN)
+    g_out[...] += dot(s_pair[...], hidden[...], TN)
 
     if not last:
         return
 
     def put_in(ref):
         for k in range(8):
-            ref[128 * k : 128 * (k + 1), :] = g_in[:, 128 * k : 128 * (k + 1)]
+            ref[128 * k : 128 * (k + 1), :] = g_in[0:128, 128 * k : 128 * (k + 1)]
 
     def put_rest(ref):
         for k in range(4):
@@ -306,8 +354,18 @@
             + g_head[128:192, 0:128]
             + g_head[192:256, 128:256]
         )
-        small = [jnp.sum(g_small[8 * k : 8 * k + 8, :], axis=0, keepdims=True) for k in range(3)]
-        ref[576:584, :] = jnp.concatenate(small + [jnp.zeros((5, 128), F32)], axis=0)
+        through, along = jnp.zeros((128, 128), F32), jnp.zeros((128, 128), F32)
+        cols = jnp.sum(g_cols[...], axis=0, keepdims=True)
+        for k in range(8):
+            lanes = slice(128 * k, 128 * (k + 1))
+            w = w_gate[:, lanes] if k < 4 else w_up[:, 128 * (k - 4) : 128 * (k - 3)]
+            w = w.astype(F32)
+            through += w * cols[:, lanes]
+            along += w * (g_in[0:128, lanes] - g_in[128:256, lanes])
+        d_bias = jnp.sum(through.T, axis=0, keepdims=True)
+        d_gain = (jnp.sum(along.T, axis=0, keepdims=True) - bias[...] * d_bias) / gain[...]
+        loss = jnp.sum(g_loss[...], axis=0, keepdims=True)
+        ref[576:584, :] = jnp.concatenate([d_gain, d_bias, loss, jnp.zeros((5, 128), F32)], axis=0)
         ref[584:1024, :] = jnp.zeros((440, 128), F32)
 
     at_end = step == pl.num_programs(0) - 1
@@ -324,7 +382,7 @@
 
 
 def backward_call(
-    core, turn, pair4, pair_out4, mirror_a, mirror_b, mirror_words, words, weights, earlier, last
+    core, turn, ready, pair_out4, mirror_a, mirror_b, mirror_words, words, weights, earlier, last
 ):
     wide, hid = 2 * weights[2].shape[1], weights[4].shape[0]
     steps = SIDE // (GROUP * B_GROUPS)
@@ -333,26 +391,24 @@
     )
     rows = ROWS * B_GROUPS
     half_way = CHUNK_ROWS // rows
+    wide_rows = lambda a: pl.BlockSpec((2 * rows, a.shape[1]), lambda g, w: (turn * steps + g, 0))
     fixed = (words, *weights)
-    in_specs = [
-        block,
+    in_specs = [wide_rows(a) for a in ready] + [
         block,
         pl.BlockSpec((rows, 128), lambda g, w: (jnp.minimum(g, half_way - 1), 0)),
         pl.BlockSpec((rows, 128), lambda g, w: (jnp.maximum(g - half_way, 0), 0)),
         pl.BlockSpec((SIDE, 128), lambda g, w: (turn * CHUNK_ROWS // SIDE, 0)),
     ]
     in_specs += [whole(a) for a in fixed]
-    args = [pair4, pair_out4, mirror_a, mirror_b, mirror_words, *fixed]
-    sums = [(128, wide), (128, hid), (256, 256), (24, 128)]
+    args = [*ready, pair_out4, mirror_a, mirror_b, mirror_words, *fixed]
+    sums = [(256, wide), (128, hid), (256, 256), (8, wide), (8, 128)]
     if earlier is not None:
         in_specs += [whole(a) for a in earlier]
         args += list(earlier)
     outs = [jax.ShapeDtypeStruct(s, F32) for s in ([(1024, 128)] * 2 if last else sums)]
     scratch = [pltpu.VMEM(s, F32) for s in sums] if last else []
     scratch += [
-        pltpu.VMEM((2 * rows, 128), BF16),
         pltpu.VMEM((2 * rows, wide), BF16),
-        pltpu.VMEM((2 * rows, hid), BF16),
         pltpu.VMEM((2 * rows, 128), BF16),
     ]
     pairs = SIDE * SIDE
@@ -371,10 +427,12 @@
             scratch_shapes=scratch,
         ),
         cost_estimate=pl.CostEstimate(
-            flops=pairs * 2 * 128 * 512 * 8, transcendentals=pairs * 640, bytes_accessed=pairs * 640
+            flops=pairs * 2 * 128 * 512 * 6,
+            transcendentals=pairs * 192,
+            bytes_accessed=pairs * 6400,
         ),
         compiler_params=pltpu.CompilerParams(
-            dimension_semantics=("arbitrary",), vmem_limit_bytes=28 * 1024 * 1024
+            dimension_semantics=("arbitrary",), vmem_limit_bytes=32 * 1024 * 1024
         ),
         name="backward",
     )(core, *args)
@@ -436,14 +494,17 @@
         out_weight,
         head_weight.T,
     )
-    out4, *sent0 = forward_call(core, 0, pair4, weights)
+    in_hbm = lambda a: pltpu.with_memory_space_constraint(a, pltpu.HBM)
+    out4, *sent0 = forward_call(core, 0, in_hbm(pair4), [in_hbm(a) for a in weights])
     words0 = send_to_mirror(tile_words, 0, None)
     mirror0 = [send_to_mirror(v, 0, route) for v, route in zip(sent0, ROUTES[0])]
     out4, *sent1 = forward_call(core, 1, pair4, weights, tile_words, out4)
     mirror1 = [send_to_mirror(v, 1, route) for v, route in zip(sent1, ROUTES[1])]
-    sums = backward_call(core, 0, pair4, out4, *mirror0, words0, tile_words, weights, None, False)
+    held = in_hbm(out4)
+    ready = prepare_call(core, pair4, *weights[:4])
+    sums = backward_call(core, 0, ready, held, *mirror0, words0, tile_words, weights, None, False)
     keep, send = backward_call(
-        core, 1, pair4, out4, *mirror1, mirror1[1], tile_words, weights, sums, True
+        core, 1, ready, held, *mirror1, mirror1[1], tile_words, weights, sums, True
     )
     sibling = [(d, device_at(chip_of(d)[0], 1 - chip_of(d)[1])) for d in range(128)]
     groups = [[d for d in range(128) if chip_of(d)[1] == k] for k in range(2)]

time: 146 us -> 147 us (level)
  starting transfers between devices: 43.4 us -> 24.7 us
  Pallas kernels: 42.1 us -> 56.1 us
  blocking collectives: 48.3 us -> 61.3 us
  local copies, waits for them, and re-layouts: 7.99 us -> 0.07 us
    ppermute x3, starting transfers between devices: 31.8 us -> 7.54 us  [send_to_mirror(): lax.ppermute(value, AXES, [(shifted(d, route), mirror_of(d, turn)) for d...]
    pallas_call x0 -> x1, Pallas kernels: none -> 16.4 us  [prepare_call(): pl.pallas_call(prepare_body, out_shape=outs, grid_spec=pltpu.PrefetchScal...]
    all_to_all x1, blocking collectives: 19.5 us -> 34.5 us  [shards(): lax.all_to_all(both_cores, AXES, split_axis=0, concat_axis=0, axis_index_...]
    unnamed x34 -> x18, local copies, waits for them, and re-layouts: 7.95 us -> 0.04 us
    pallas_call x2, Pallas kernels: 26.2 us -> 22.7 us  [backward_call(): pl.pallas_call(body, out_shape=tuple(outs), grid_spec=pltpu.PrefetchScala...]
    ppermute x2, starting transfers between devices: 1.32 us -> 4.15 us  [send_to_mirror(): return lax.ppermute(value, AXES, [(d, mirror_of(d, turn)) for d in devices])]
    ppermute x3, starting transfers between devices: 5.38 us -> 7.5 us  [send_to_mirror(): value = lax.ppermute(value, AXES, [(d, shifted(d, route)) for d in devices])]
    all_to_all x1, blocking collectives: 13.4 us -> 11.4 us  [shards(): lax.all_to_all(words, 'col', split_axis=1, concat_axis=0, tiled=True)]
  transfers between devices with their start and end apart: 10 -> 10, of which waited for: 2 -> 2; matrix products, arithmetic and copies ran while one was open for 0% -> 0% of each run, Pallas kernels for 14% -> 24%
where the time goes in v4:
time: 147 us; the launch traced here: 146 us
  blocking collectives  61.3 us (42%)
  Pallas kernels  56.1 us (38%)
  starting transfers between devices  24.7 us (17%)
  waiting for transfers between devices  3.09 us (2%)
    all_to_all x1, blocking collectives, shards(): lax.all_to_all(both_cores, AXES, split_axis=0, concat_axis=0, axis_index_...  34.5 us
    pallas_call x2, Pallas kernels, backward_call(): pl.pallas_call(body, out_shape=tuple(outs), grid_spec=pltpu.PrefetchScala...  22.7 us
    pallas_call x1, Pallas kernels, prepare_call(): pl.pallas_call(prepare_body, out_shape=outs, grid_spec=pltpu.PrefetchScal...  16.4 us
    pallas_call x2, Pallas kernels, forward_call(): pl.pallas_call(body, out_shape=outs, grid_spec=pltpu.PrefetchScalarGridSp...  15.9 us
    all_to_all x1, blocking collectives, shards(): lax.all_to_all(jnp.broadcast_to(mine, pieces.shape), AXES, split_axis=0,...  15.3 us
    all_to_all x1, blocking collectives, shards(): lax.all_to_all(words, 'col', split_axis=1, concat_axis=0, tiled=True)  11.4 us
    ppermute x3, starting transfers between devices, send_to_mirror(): lax.ppermute(value, AXES, [(shifted(d, route), mirror_of(d, turn)) for d...  7.54 us
    ppermute x3, starting transfers between devices, send_to_mirror(): value = lax.ppermute(value, AXES, [(d, shifted(d, route)) for d in devices])  7.5 us
  transfers between devices with their start and end apart: 10, of which 2 were waited for; matrix products, arithmetic and copies ran while one was open for 0% of the time, Pallas kernels for 24%

profile of v4, /device:TPU:1, one launch (start us, length us, event | category | flops | bytes accessed | tf_op | source)
XLA Modules:
  0.0 146.3 jit_solution(16696800054311037127)
XLA Ops:
  0.7 8.5 %forward.2 = (bf16[64,2,64,128]{3,2,1,0:T(8,128)(2,1)}, bf16[1024,128]{1,0:T(8,128)(2,1)S(1)}, bf16[1024,128]{1,0:T(8,128)(2,1)S(1)}) custom-call(s32[1]{0:T(128)} %bitcast.refs_0_.core, bf16[64,2,64,128]{3,2,1,0:T(8,128)(2,1)} %bitcast.37, f32[1,128]{1,0:T(1,128)} %bitcast.27, f32[1,128]{1,0:T(1,128)} %bitcast.32, bf16[128,512]{1,0:T(8,128)(2,1)} %refs_12_.3, ...), custom_call_target="tpu_custom_call" | custom-call | flops 1610612736 | bytes 2621440 | tf_op jit(solution)/shard_map/forward/pallas_call | solution.py:175
  9.2 2.5 %collective-permute-start.3 = (bf16[1024,128]{1,0:T(8,128)(2,1)S(1)}, bf16[1024,128]{1,0:T(8,128)(2,1)S(1)}, u32[]{:S(2)}, u32[]{:S(2)}) collective-permute-start(bf16[1024,128]{1,0:T(8,128)(2,1)S(1)} %get-tuple-element.40), channel_id=1, source_target_pairs={{0,64},{1,65},{2,66},{3,67},{4,68},{5,69},{6,70},{7,71},{8,72},{9,... | collective-permute-start | bytes 786440 | tf_op jit(solution)/shard_map/ppermute | solution.py:48
  11.7 2.1 %collective-permute-start.5 = (bf16[1024,128]{1,0:T(8,128)(2,1)S(1)}, bf16[1024,128]{1,0:T(8,128)(2,1)S(1)}, u32[]{:S(2)}, u32[]{:S(2)}) collective-permute-start(bf16[1024,128]{1,0:T(8,128)(2,1)S(1)} %get-tuple-element.41), channel_id=1, source_target_pairs={{0,65},{1,64},{2,67},{3,66},{4,69},{5,68},{6,71},{7,70},{8,73},{9,... | collective-permute-start | bytes 786440 | tf_op jit(solution)/shard_map/ppermute | solution.py:48
  13.8 0.0 copy-done.7
  13.8 11.4 %all_to_all.29 = s32[8,8,128]{2,0,1:T(8,128)S(1)} all-to-all(s32[8,8,128]{2,0,1:T(8,128)S(1)} %add_bitcast_fusion), channel_id=1, replica_groups=mesh['row'=16,'col'=8] {'col'}, dimensions={1} | all-to-all | bytes 65536 | tf_op jit(solution)/shard_map/all_to_all | solution.py:486
  25.3 7.4 %forward.3 = (bf16[64,2,64,128]{3,2,1,0:T(8,128)(2,1)}, bf16[1024,128]{1,0:T(8,128)(2,1)S(1)}, bf16[1088,128]{1,0:T(8,128)(2,1)S(1)}) custom-call(s32[1]{0:T(128)} %bitcast.refs_0_.core, bf16[64,2,64,128]{3,2,1,0:T(8,128)(2,1)S(1)} %bitcast.38, f32[1,128]{1,0:T(1,128)S(1)} %bitcast.28, f32[1,128]{1,0:T(1,128)S(1)} %bitcast.33, ...), custom_call_target="tpu_custom_call", output_to_operand_aliasing={{0}: (9, {})} | custom-call | flops 1610612736 | bytes 2621440 | tf_op jit(solution)/shard_map/forward/pallas_call | solution.py:175
  32.7 2.9 %collective-permute-start = (bf16[1024,128]{1,0:T(8,128)(2,1)S(1)}, bf16[1024,128]{1,0:T(8,128)(2,1)S(1)}, u32[]{:S(2)}, u32[]{:S(2)}) collective-permute-start(bf16[1024,128]{1,0:T(8,128)(2,1)S(1)} %get-tuple-element.38), channel_id=1, source_target_pairs={{0,32},{1,33},{2,34},{3,35},{4,36},{5,37},{6,38},{7,39},{8,40},{9,... | collective-permute-start | bytes 786440 | tf_op jit(solution)/shard_map/ppermute | solution.py:48
  35.6 0.0 collective-permute-done.3
  35.6 1.1 collective-permute-start.4
  36.7 0.0 collective-permute-done.5
  36.7 0.8 collective-permute-start.6
  37.5 0.7 collective-permute-start.7
  38.1 16.4 %prepare.1 = (bf16[8192,256]{1,0:T(8,128)(2,1)S(1)}, f32[8192,512]{1,0:T(8,128)}, f32[8192,512]{1,0:T(8,128)}, bf16[8192,512]{1,0:T(8,128)(2,1)S(1)}) custom-call(s32[1]{0:T(128)} %bitcast.refs_0_.core, bf16[64,2,64,128]{3,2,1,0:T(8,128)(2,1)S(1)} %bitcast.39, f32[1,128]{1,0:T(1,128)S(1)} %bitcast.29, f32[1,128]{1,0:T(1,128)S(1)} %bitcast.34, ...), custom_call_target="tpu_custom_call" | custom-call | flops 2147483648 | bytes 48234496 | tf_op jit(solution)/shard_map/prepare/pallas_call | solution.py:227
  54.5 3.5 %collective-permute-start.2 = (bf16[1088,128]{1,0:T(8,128)(2,1)S(1)}, bf16[1088,128]{1,0:T(8,128)(2,1)S(1)}, u32[]{:S(2)}, u32[]{:S(2)}) collective-permute-start(bf16[1088,128]{1,0:T(8,128)(2,1)S(1)} %get-tuple-element.39), channel_id=1, source_target_pairs={{0,8},{1,24},{2,40},{3,56},{4,72},{5,88},{6,104},{7,120},{8,0},{9,... | collective-permute-start | bytes 835592 | tf_op jit(solution)/shard_map/ppermute | solution.py:47
  58.0 0.0 collective-permute-done
  58.0 5.7 %collective-permute-start.1 = (bf16[1024,128]{1,0:T(8,128)(2,1)S(1)}, bf16[1024,128]{1,0:T(8,128)(2,1)S(1)}, u32[]{:S(2)}, u32[]{:S(2)}) collective-permute-start(bf16[1024,128]{1,0:T(8,128)(2,1)S(1)} %collective-permute-done), channel_id=1, source_target_pairs={{32,8},{33,24},{34,40},{35,56},{36,72},{37,88},{38,104},{39,120},{... | collective-permute-start | bytes 786440 | tf_op jit(solution)/shard_map/ppermute | solution.py:49
  63.7 0.0 collective-permute-done.7.refs_8_
  63.7 0.0 collective-permute-done.4.refs_6_
  63.7 0.0 collective-permute-done.6.refs_7_
  63.7 11.2 %backward.2 = (f32[256,1024]{1,0:T(8,128)S(1)}, f32[128,512]{1,0:T(8,128)S(1)}, f32[256,256]{1,0:T(8,128)S(1)}, f32[8,1024]{1,0:T(8,128)S(1)}, f32[8,128]{1,0:T(8,128)S(1)}) custom-call(s32[1]{0:T(128)} %bitcast.refs_0_.core, bf16[8192,256]{1,0:T(8,128)(2,1)S(1)} %get-tuple-element.34.refs_1_, f32[8192,512]{1,0:T(8,128)} %get-tuple-element.35.refs_2_, ...), custom_call_target="tpu_custom_call" | custom-call | flops 3221225472 | bytes 26214400 | tf_op jit(solution)/shard_map/backward/pallas_call | solution.py:419
  74.9 0.0 collective-permute-done.2.refs_7_.refs_8_
  75.0 0.0 collective-permute-done.1.refs_6_
  75.0 11.5 %backward.3 = (f32[1024,128]{1,0:T(8,128)S(1)}, f32[1024,128]{1,0:T(8,128)S(1)}) custom-call(s32[1]{0:T(128)} %bitcast.refs_0_.core, bf16[8192,256]{1,0:T(8,128)(2,1)S(1)} %get-tuple-element.34.refs_1_, f32[8192,512]{1,0:T(8,128)} %get-tuple-element.35.refs_2_, f32[8192,512]{1,0:T(8,128)} %get-tuple-element.36.refs_3_, ...), custom_call_target="tpu_custom_call" | custom-call | flops 3221225472 | bytes 26214400 | tf_op jit(solution)/shard_map/backward/pallas_call | solution.py:419
  86.5 2.1 %collective-permute-start.8 = (f32[1024,128]{1,0:T(8,128)S(1)}, f32[1024,128]{1,0:T(8,128)S(1)}, u32[]{:S(2)}, u32[]{:S(2)}) collective-permute-start(f32[1024,128]{1,0:T(8,128)S(1)} %get-tuple-element.48), channel_id=1, source_target_pairs={{0,8},{1,9},{2,10},{3,11},{4,12},{5,13},{6,14},{7,15},{8,0},{9,1},... | collective-permute-start | bytes 1572872 | tf_op jit(solution)/shard_map/ppermute | solution.py:511
  88.5 1.5 %collective-permute-done.8 = f32[1024,128]{1,0:T(8,128)S(1)} collective-permute-done((f32[1024,128]{1,0:T(8,128)S(1)}, f32[1024,128]{1,0:T(8,128)S(1)}, u32[]{:S(2)}, u32[]{:S(2)}) %collective-permute-start.8) | collective-permute-done | bytes 524320 | tf_op jit(solution)/shard_map/ppermute | solution.py:511
  90.1 0.1 add.7
  90.2 34.5 %all_to_all.30 = f32[64,16,128]{2,1,0:T(8,128)S(1)} all-to-all(f32[64,16,128]{2,1,0:T(8,128)S(1)} %bitcast.41), channel_id=1, replica_groups={{0,1,2,3,4,5,6,7,16,17,18,19,20,21,22,23,32,33,34,35,36,37,38,39,48,49,..., dimensions={0} | all-to-all | bytes 1048576 | tf_op jit(solution)/shard_map/all_to_all | solution.py:512
  124.7 0.1 reduce_sum.9
  124.8 15.3 %all_to_all.31 = f32[64,16,128]{2,1,0:T(8,128)S(1)} all-to-all(f32[64,16,128]{2,1,0:T(8,128)S(1)} %broadcast_in_dim.2), channel_id=1, replica_groups={{0,1,2,3,4,5,6,7,16,17,18,19,20,21,22,23,32,33,34,35,36,37,38,39,48,49,..., dimensions={0} | all-to-all | bytes 1048576 | tf_op jit(solution)/shard_map/all_to_all | solution.py:516
  140.1 3.4 %collective-permute-start.9 = (f32[1024,128]{1,0:T(8,128)S(1)}, f32[1024,128]{1,0:T(8,128)S(1)}, u32[]{:S(2)}, u32[]{:S(2)}) collective-permute-start(f32[1024,128]{1,0:T(8,128)S(1)} %bitcast.17), channel_id=1, source_target_pairs={{0,8},{1,9},{2,10},{3,11},{4,12},{5,13},{6,14},{7,15},{8,0},{9,1},... | collective-permute-start | bytes 1572872 | tf_op jit(solution)/shard_map/ppermute | solution.py:524
  143.5 1.5 %collective-permute-done.9.other = f32[1024,128]{1,0:T(8,128)S(1)} collective-permute-done((f32[1024,128]{1,0:T(8,128)S(1)}, f32[1024,128]{1,0:T(8,128)S(1)}, u32[]{:S(2)}, u32[]{:S(2)}) %collective-permute-start.9) | collective-permute-done | bytes 524320 | tf_op jit(solution)/shard_map/ppermute | solution.py:524
  145.0 1.1 unpack.1
  (19 shorter events, 0.1 us)
Async XLA Ops:
  0.6 24.6 %copy-start.1 = (bf16[128,512]{1,0:T(8,128)(2,1)S(1)}, bf16[128,512]{1,0:T(8,128)(2,1)}, u32[]{:S(2)}) copy-start(bf16[128,512]{1,0:T(8,128)(2,1)} %refs_13_.3) | copy-start | bytes 393220
  0.6 24.6 %copy-start = (bf16[128,512]{1,0:T(8,128)(2,1)S(1)}, bf16[128,512]{1,0:T(8,128)(2,1)}, u32[]{:S(2)}) copy-start(bf16[128,512]{1,0:T(8,128)(2,1)} %refs_12_.3) | copy-start | bytes 393220
  0.7 24.6 %copy-start.2 = (bf16[512,128]{1,0:T(8,128)(2,1)S(1)}, bf16[512,128]{1,0:T(8,128)(2,1)}, u32[]{:S(2)}) copy-start(bf16[512,128]{1,0:T(8,128)(2,1)} %refs_14_.3) | copy-start | bytes 393220
  0.7 24.6 %copy-start.3 = (bf16[128,64]{0,1:T(8,128)(2,1)S(1)}, bf16[128,64]{0,1:T(8,128)(2,1)}, u32[]{:S(2)}) copy-start(bf16[128,64]{0,1:T(8,128)(2,1)} %param.15) | copy-start | bytes 49156
  0.7 24.6 %copy-start.5 = (f32[128]{0:T(128)S(1)}, f32[128]{0:T(128)}, u32[]{:S(2)}) copy-start(f32[128]{0:T(128)} %param.11) | copy-start | bytes 1540
  0.7 24.6 %copy-start.4 = (f32[128]{0:T(128)S(1)}, f32[128]{0:T(128)}, u32[]{:S(2)}) copy-start(f32[128]{0:T(128)} %param.10) | copy-start | bytes 1540
  0.7 24.6 %copy-start.6 = (bf16[64,128,128]{2,1,0:T(8,128)(2,1)S(1)}, bf16[64,128,128]{2,1,0:T(8,128)(2,1)}, u32[]{:S(2)}) copy-start(bf16[64,128,128]{2,1,0:T(8,128)(2,1)} %param.9) | copy-start | bytes 6291460
  0.7 13.1 %copy-start.8 = (s32[8,1024]{1,0:T(8,128)S(1)}, s32[8,1024]{1,0:T(8,128)}, u32[]{:S(2)}) copy-start(s32[8,1024]{1,0:T(8,128)} %param.17) | copy-start | bytes 98308
  0.7 13.1 %copy-start.7 = (s32[8,1024]{1,0:T(8,128)S(1)}, s32[8,1024]{1,0:T(8,128)}, u32[]{:S(2)}) copy-start(s32[8,1024]{1,0:T(8,128)} %param.16) | copy-start | bytes 98308
  9.2 26.4 %collective-permute-start.3 = (bf16[1024,128]{1,0:T(8,128)(2,1)S(1)}, bf16[1024,128]{1,0:T(8,128)(2,1)S(1)}, u32[]{:S(2)}, u32[]{:S(2)}) collective-permute-start(bf16[1024,128]{1,0:T(8,128)(2,1)S(1)} %get-tuple-element.40), channel_id=1, source_target_pairs={{0,64},{1,65},{2,66},{3,67},{4,68},{5,69},{6,70},{7,71},{8,72},{9,... | collective-permute-start | bytes 786440 | tf_op jit(solution)/shard_map/ppermute | solution.py:48
  11.7 25.0 %collective-permute-start.5 = (bf16[1024,128]{1,0:T(8,128)(2,1)S(1)}, bf16[1024,128]{1,0:T(8,128)(2,1)S(1)}, u32[]{:S(2)}, u32[]{:S(2)}) collective-permute-start(bf16[1024,128]{1,0:T(8,128)(2,1)S(1)} %get-tuple-element.41), channel_id=1, source_target_pairs={{0,65},{1,64},{2,67},{3,66},{4,69},{5,68},{6,71},{7,70},{8,73},{9,... | collective-permute-start | bytes 786440 | tf_op jit(solution)/shard_map/ppermute | solution.py:48
  32.7 25.3 %collective-permute-start = (bf16[1024,128]{1,0:T(8,128)(2,1)S(1)}, bf16[1024,128]{1,0:T(8,128)(2,1)S(1)}, u32[]{:S(2)}, u32[]{:S(2)}) collective-permute-start(bf16[1024,128]{1,0:T(8,128)(2,1)S(1)} %get-tuple-element.38), channel_id=1, source_target_pairs={{0,32},{1,33},{2,34},{3,35},{4,36},{5,37},{6,38},{7,39},{8,40},{9,... | collective-permute-start | bytes 786440 | tf_op jit(solution)/shard_map/ppermute | solution.py:48
  35.6 28.1 %collective-permute-start.4 = (bf16[1024,128]{1,0:T(8,128)(2,1)S(1)}, bf16[1024,128]{1,0:T(8,128)(2,1)S(1)}, u32[]{:S(2)}, u32[]{:S(2)}) collective-permute-start(bf16[1024,128]{1,0:T(8,128)(2,1)S(1)} %collective-permute-done.3), channel_id=1, source_target_pairs={{64,0},{65,16},{66,32},{67,48},{68,64},{69,80},{70,96},{71,112},{7... | collective-permute-start | bytes 786440 | tf_op jit(solution)/shard_map/ppermute | solution.py:49
  36.7 27.0 %collective-permute-start.6 = (bf16[1024,128]{1,0:T(8,128)(2,1)S(1)}, bf16[1024,128]{1,0:T(8,128)(2,1)S(1)}, u32[]{:S(2)}, u32[]{:S(2)}) collective-permute-start(bf16[1024,128]{1,0:T(8,128)(2,1)S(1)} %collective-permute-done.5), channel_id=1, source_target_pairs={{65,0},{64,16},{67,32},{66,48},{69,64},{68,80},{71,96},{70,112},{7... | collective-permute-start | bytes 786440 | tf_op jit(solution)/shard_map/ppermute | solution.py:49
  37.5 26.2 %collective-permute-start.7 = (s32[64,128]{1,0:T(8,128)S(1)}, s32[64,128]{1,0:T(8,128)S(1)}, u32[]{:S(2)}, u32[]{:S(2)}) collective-permute-start(s32[64,128]{1,0:T(8,128)S(1)} %bitcast.20), channel_id=1, source_target_pairs={{0,0},{1,16},{2,32},{3,48},{4,64},{5,80},{6,96},{7,112},{8,8},{9,2... | collective-permute-start | bytes 98312 | tf_op jit(solution)/shard_map/ppermute | solution.py:47
  54.5 20.4 %collective-permute-start.2 = (bf16[1088,128]{1,0:T(8,128)(2,1)S(1)}, bf16[1088,128]{1,0:T(8,128)(2,1)S(1)}, u32[]{:S(2)}, u32[]{:S(2)}) collective-permute-start(bf16[1088,128]{1,0:T(8,128)(2,1)S(1)} %get-tuple-element.39), channel_id=1, source_target_pairs={{0,8},{1,24},{2,40},{3,56},{4,72},{5,88},{6,104},{7,120},{8,0},{9,... | collective-permute-start | bytes 835592 | tf_op jit(solution)/shard_map/ppermute | solution.py:47
  58.0 16.9 %collective-permute-start.1 = (bf16[1024,128]{1,0:T(8,128)(2,1)S(1)}, bf16[1024,128]{1,0:T(8,128)(2,1)S(1)}, u32[]{:S(2)}, u32[]{:S(2)}) collective-permute-start(bf16[1024,128]{1,0:T(8,128)(2,1)S(1)} %collective-permute-done), channel_id=1, source_target_pairs={{32,8},{33,24},{34,40},{35,56},{36,72},{37,88},{38,104},{39,120},{... | collective-permute-start | bytes 786440 | tf_op jit(solution)/shard_map/ppermute | solution.py:49
  86.5 3.6 %collective-permute-start.8 = (f32[1024,128]{1,0:T(8,128)S(1)}, f32[1024,128]{1,0:T(8,128)S(1)}, u32[]{:S(2)}, u32[]{:S(2)}) collective-permute-start(f32[1024,128]{1,0:T(8,128)S(1)} %get-tuple-element.48), channel_id=1, source_target_pairs={{0,8},{1,9},{2,10},{3,11},{4,12},{5,13},{6,14},{7,15},{8,0},{9,1},... | collective-permute-start | bytes 1572872 | tf_op jit(solution)/shard_map/ppermute | solution.py:511
  140.1 4.9 %collective-permute-start.9 = (f32[1024,128]{1,0:T(8,128)S(1)}, f32[1024,128]{1,0:T(8,128)S(1)}, u32[]{:S(2)}, u32[]{:S(2)}) collective-permute-start(f32[1024,128]{1,0:T(8,128)S(1)} %bitcast.17), channel_id=1, source_target_pairs={{0,8},{1,9},{2,10},{3,11},{4,12},{5,13},{6,14},{7,15},{8,0},{9,1},... | collective-permute-start | bytes 1572872 | tf_op jit(solution)/shard_map/ppermute | solution.py:524

commit v5 on v3

--- a/solution.py
+++ b/solution.py
@@ -13,12 +13,12 @@
 
 SIDE = 64
 GROUP = 8
-F_COLS = 16
+F_COLS = 32
 B_GROUPS = 2
 ROWS = SIDE * GROUP // 2
 CHUNK_ROWS = SIDE * SIDE // 4
 
-ROUTES = (((0, 0, 1), None), ((0, 0, 3), (0, 2, 0)))
+ROUTES = (((0, 0, 1), (0, 0, 3)), ((0, 2, 0), None))
 
 
 def chip_of(device):
@@ -90,7 +90,7 @@
     words = rest[:-4]
     step = pl.program_id(0)
     rows_in = pair[...].reshape(SIDE * F_COLS, 128)
-    count = 2
+    count = 4
     size = SIDE * F_COLS // count
     for k in range(count):
         part = rows_in[k * size : (k + 1) * size]
@@ -436,14 +436,16 @@
         out_weight,
         head_weight.T,
     )
-    out4, *sent0 = forward_call(core, 0, pair4, weights)
+    in_hbm = lambda a: pltpu.with_memory_space_constraint(a, pltpu.HBM)
+    out4, *sent0 = forward_call(core, 0, in_hbm(pair4), [in_hbm(a) for a in weights])
     words0 = send_to_mirror(tile_words, 0, None)
     mirror0 = [send_to_mirror(v, 0, route) for v, route in zip(sent0, ROUTES[0])]
     out4, *sent1 = forward_call(core, 1, pair4, weights, tile_words, out4)
     mirror1 = [send_to_mirror(v, 1, route) for v, route in zip(sent1, ROUTES[1])]
-    sums = backward_call(core, 0, pair4, out4, *mirror0, words0, tile_words, weights, None, False)
+    held = in_hbm(out4)
+    sums = backward_call(core, 0, pair4, held, *mirror0, words0, tile_words, weights, None, False)
     keep, send = backward_call(
-        core, 1, pair4, out4, *mirror1, mirror1[1], tile_words, weights, sums, True
+        core, 1, pair4, held, *mirror1, mirror1[1], tile_words, weights, sums, True
     )
     sibling = [(d, device_at(chip_of(d)[0], 1 - chip_of(d)[1])) for d in range(128)]
     groups = [[d for d in range(128) if chip_of(d)[1] == k] for k in range(2)]

time: 146 us -> 144 us (0.986)
  blocking collectives: 48.3 us -> 70.4 us
  starting transfers between devices: 43.4 us -> 25.5 us
  local copies, waits for them, and re-layouts: 7.99 us -> 0.07 us
  Pallas kernels: 42.1 us -> 43.9 us
    all_to_all x1, blocking collectives: 19.5 us -> 43.7 us  [shards(): lax.all_to_all(both_cores, AXES, split_axis=0, concat_axis=0, axis_index_...]
    ppermute x3, starting transfers between devices: 31.8 us -> 7.77 us  [send_to_mirror(): lax.ppermute(value, AXES, [(shifted(d, route), mirror_of(d, turn)) for d...]
    unnamed x34 -> x18, local copies, waits for them, and re-layouts: 7.95 us -> 0.04 us
    ppermute x2, starting transfers between devices: 1.32 us -> 4.24 us  [send_to_mirror(): return lax.ppermute(value, AXES, [(d, mirror_of(d, turn)) for d in devices])]
    ppermute x3, starting transfers between devices: 5.38 us -> 7.49 us  [send_to_mirror(): value = lax.ppermute(value, AXES, [(d, shifted(d, route)) for d in devices])]
    all_to_all x1, blocking collectives: 13.4 us -> 11.4 us  [shards(): lax.all_to_all(words, 'col', split_axis=1, concat_axis=0, tiled=True)]
    pallas_call x2, Pallas kernels: 26.2 us -> 27.9 us  [backward_call(): pl.pallas_call(body, out_shape=tuple(outs), grid_spec=pltpu.PrefetchScala...]
where the time goes in v5:
time: 144 us
  blocking collectives  70.4 us (49%)
  Pallas kernels  43.9 us (30%)
  starting transfers between devices  25.5 us (18%)
  waiting for transfers between devices  3.09 us (2%)
    all_to_all x1, blocking collectives, shards(): lax.all_to_all(both_cores, AXES, split_axis=0, concat_axis=0, axis_index_...  43.7 us
    pallas_call x2, Pallas kernels, backward_call(): pl.pallas_call(body, out_shape=tuple(outs), grid_spec=pltpu.PrefetchScala...  27.9 us
    all_to_all x1, blocking collectives, shards(): lax.all_to_all(jnp.broadcast_to(mine, pieces.shape), AXES, split_axis=0,...  15.3 us
    pallas_call x2, Pallas kernels, forward_call(): pl.pallas_call(body, out_shape=outs, grid_spec=pltpu.PrefetchScalarGridSp...  14.9 us
    all_to_all x1, blocking collectives, shards(): lax.all_to_all(words, 'col', split_axis=1, concat_axis=0, tiled=True)  11.4 us
    ppermute x3, starting transfers between devices, send_to_mirror(): lax.ppermute(value, AXES, [(shifted(d, route), mirror_of(d, turn)) for d...  7.77 us
    ppermute x3, starting transfers between devices, send_to_mirror(): value = lax.ppermute(value, AXES, [(d, shifted(d, route)) for d in devices])  7.49 us
    ppermute x2, starting transfers between devices, send_to_mirror(): return lax.ppermute(value, AXES, [(d, mirror_of(d, turn)) for d in devices])  4.24 us
  transfers between devices with their start and end apart: 10, of which 2 were waited for; matrix products, arithmetic and copies ran while one was open for 0% of the time, Pallas kernels for 14%

profile of v5, /device:TPU:1, one launch (start us, length us, event | category | flops | bytes accessed | tf_op | source)
XLA Modules:
  0.0 144.1 jit_solution(11646625694841903287)
XLA Ops:
  0.6 0.0 copy-start.7
  0.7 0.0 copy-start.8
  0.7 8.0 %forward.2 = (bf16[64,2,64,128]{3,2,1,0:T(8,128)(2,1)}, bf16[1024,128]{1,0:T(8,128)(2,1)S(1)}, bf16[1024,128]{1,0:T(8,128)(2,1)S(1)}) custom-call(s32[1]{0:T(128)} %bitcast.refs_0_.core, bf16[64,2,64,128]{3,2,1,0:T(8,128)(2,1)} %bitcast.23, f32[1,128]{1,0:T(1,128)} %bitcast.31, f32[1,128]{1,0:T(1,128)} %bitcast.35, bf16[128,512]{1,0:T(8,128)(2,1)} %refs_9_.3, ...), custom_call_target="tpu_custom_call" | custom-call | flops 1610612736 | bytes 2621440 | tf_op jit(solution)/shard_map/forward/pallas_call | solution.py:174
  8.7 2.5 %collective-permute-start.3 = (bf16[1024,128]{1,0:T(8,128)(2,1)S(1)}, bf16[1024,128]{1,0:T(8,128)(2,1)S(1)}, u32[]{:S(2)}, u32[]{:S(2)}) collective-permute-start(bf16[1024,128]{1,0:T(8,128)(2,1)S(1)} %get-tuple-element.31), channel_id=1, source_target_pairs={{0,64},{1,65},{2,66},{3,67},{4,68},{5,69},{6,70},{7,71},{8,72},{9,... | collective-permute-start | bytes 786440 | tf_op jit(solution)/shard_map/ppermute | solution.py:48
  11.1 2.1 %collective-permute-start.5 = (bf16[1024,128]{1,0:T(8,128)(2,1)S(1)}, bf16[1024,128]{1,0:T(8,128)(2,1)S(1)}, u32[]{:S(2)}, u32[]{:S(2)}) collective-permute-start(bf16[1024,128]{1,0:T(8,128)(2,1)S(1)} %get-tuple-element.32), channel_id=1, source_target_pairs={{0,65},{1,64},{2,67},{3,66},{4,69},{5,68},{6,71},{7,70},{8,73},{9,... | collective-permute-start | bytes 786440 | tf_op jit(solution)/shard_map/ppermute | solution.py:48
  13.3 11.4 %all_to_all.29 = s32[8,8,128]{2,0,1:T(8,128)S(1)} all-to-all(s32[8,8,128]{2,0,1:T(8,128)S(1)} %add_bitcast_fusion), channel_id=1, replica_groups=mesh['row'=16,'col'=8] {'col'}, dimensions={1} | all-to-all | bytes 65536 | tf_op jit(solution)/shard_map/all_to_all | solution.py:428
  24.7 7.0 %forward.3 = (bf16[64,2,64,128]{3,2,1,0:T(8,128)(2,1)}, bf16[1024,128]{1,0:T(8,128)(2,1)S(1)}, bf16[1088,128]{1,0:T(8,128)(2,1)S(1)}) custom-call(s32[1]{0:T(128)} %bitcast.refs_0_.core, bf16[64,2,64,128]{3,2,1,0:T(8,128)(2,1)S(1)} %bitcast.24, f32[1,128]{1,0:T(1,128)S(1)} %bitcast.32, f32[1,128]{1,0:T(1,128)S(1)} %bitcast.36, ...), custom_call_target="tpu_custom_call", output_to_operand_aliasing={{0}: (9, {})} | custom-call | flops 1610612736 | bytes 2621440 | tf_op jit(solution)/shard_map/forward/pallas_call | solution.py:174
  31.7 2.9 %collective-permute-start = (bf16[1024,128]{1,0:T(8,128)(2,1)S(1)}, bf16[1024,128]{1,0:T(8,128)(2,1)S(1)}, u32[]{:S(2)}, u32[]{:S(2)}) collective-permute-start(bf16[1024,128]{1,0:T(8,128)(2,1)S(1)} %get-tuple-element.29), channel_id=1, source_target_pairs={{0,32},{1,33},{2,34},{3,35},{4,36},{5,37},{6,38},{7,39},{8,40},{9,... | collective-permute-start | bytes 786440 | tf_op jit(solution)/shard_map/ppermute | solution.py:48
  34.6 0.0 collective-permute-done.3
  34.6 1.1 collective-permute-start.4
  35.7 0.0 collective-permute-done.5
  35.7 0.8 collective-permute-start.6
  36.5 0.7 collective-permute-start.7
  37.1 3.6 %collective-permute-start.2 = (bf16[1088,128]{1,0:T(8,128)(2,1)S(1)}, bf16[1088,128]{1,0:T(8,128)(2,1)S(1)}, u32[]{:S(2)}, u32[]{:S(2)}) collective-permute-start(bf16[1088,128]{1,0:T(8,128)(2,1)S(1)} %get-tuple-element.30), channel_id=1, source_target_pairs={{0,8},{1,24},{2,40},{3,56},{4,72},{5,88},{6,104},{7,120},{8,0},{9,... | collective-permute-start | bytes 835592 | tf_op jit(solution)/shard_map/ppermute | solution.py:47
  40.7 0.0 collective-permute-done
  40.7 5.9 %collective-permute-start.1 = (bf16[1024,128]{1,0:T(8,128)(2,1)S(1)}, bf16[1024,128]{1,0:T(8,128)(2,1)S(1)}, u32[]{:S(2)}, u32[]{:S(2)}) collective-permute-start(bf16[1024,128]{1,0:T(8,128)(2,1)S(1)} %collective-permute-done), channel_id=1, source_target_pairs={{32,8},{33,24},{34,40},{35,56},{36,72},{37,88},{38,104},{39,120},{... | collective-permute-start | bytes 786440 | tf_op jit(solution)/shard_map/ppermute | solution.py:49
  46.6 0.0 collective-permute-done.7.refs_5_
  46.6 0.0 collective-permute-done.4.refs_3_
  46.6 0.0 collective-permute-done.6.refs_4_
  46.7 13.9 %backward.2 = (f32[128,1024]{1,0:T(8,128)S(1)}, f32[128,512]{1,0:T(8,128)S(1)}, f32[256,256]{1,0:T(8,128)S(1)}, f32[24,128]{1,0:T(8,128)S(1)}) custom-call(s32[1]{0:T(128)} %bitcast.refs_0_.core, bf16[64,2,64,128]{3,2,1,0:T(8,128)(2,1)S(1)} %bitcast.25, bf16[64,2,64,128]{3,2,1,0:T(8,128)(2,1)} %get-tuple-element.28.refs_2_, ...), custom_call_target="tpu_custom_call" | custom-call | flops 4294967296 | bytes 2621440 | tf_op jit(solution)/shard_map/backward/pallas_call | solution.py:363
  60.5 0.0 collective-permute-done.2.refs_4_.refs_5_
  60.5 0.0 collective-permute-done.1.refs_3_
  60.5 14.0 %backward.3 = (f32[1024,128]{1,0:T(8,128)S(1)}, f32[1024,128]{1,0:T(8,128)S(1)}) custom-call(s32[1]{0:T(128)} %bitcast.refs_0_.core, bf16[64,2,64,128]{3,2,1,0:T(8,128)(2,1)S(1)} %bitcast.26, bf16[64,2,64,128]{3,2,1,0:T(8,128)(2,1)} %get-tuple-element.28.refs_2_, bf16[1024,128]{1,0:T(8,128)(2,1)S(1)} %collective-permute-done.1.refs_3_, ...), custom_call_target="tpu_custom_call" | custom-call | flops 4294967296 | bytes 2621440 | tf_op jit(solution)/shard_map/backward/pallas_call | solution.py:363
  74.6 2.7 %collective-permute-start.8 = (f32[1024,128]{1,0:T(8,128)S(1)}, f32[1024,128]{1,0:T(8,128)S(1)}, u32[]{:S(2)}, u32[]{:S(2)}) collective-permute-start(f32[1024,128]{1,0:T(8,128)S(1)} %get-tuple-element.38), channel_id=1, source_target_pairs={{0,8},{1,9},{2,10},{3,11},{4,12},{5,13},{6,14},{7,15},{8,0},{9,1},... | collective-permute-start | bytes 1572872 | tf_op jit(solution)/shard_map/ppermute | solution.py:452
  77.2 1.5 %collective-permute-done.8 = f32[1024,128]{1,0:T(8,128)S(1)} collective-permute-done((f32[1024,128]{1,0:T(8,128)S(1)}, f32[1024,128]{1,0:T(8,128)S(1)}, u32[]{:S(2)}, u32[]{:S(2)}) %collective-permute-start.8) | collective-permute-done | bytes 524320 | tf_op jit(solution)/shard_map/ppermute | solution.py:452
  78.8 0.1 add.7
  78.8 43.7 %all_to_all.30 = f32[64,16,128]{2,1,0:T(8,128)S(1)} all-to-all(f32[64,16,128]{2,1,0:T(8,128)S(1)} %bitcast.39), channel_id=1, replica_groups={{0,1,2,3,4,5,6,7,16,17,18,19,20,21,22,23,32,33,34,35,36,37,38,39,48,49,..., dimensions={0} | all-to-all | bytes 1048576 | tf_op jit(solution)/shard_map/all_to_all | solution.py:453
  122.5 0.1 reduce_sum.9
  122.7 15.3 %all_to_all.31 = f32[64,16,128]{2,1,0:T(8,128)S(1)} all-to-all(f32[64,16,128]{2,1,0:T(8,128)S(1)} %broadcast_in_dim.2), channel_id=1, replica_groups={{0,1,2,3,4,5,6,7,16,17,18,19,20,21,22,23,32,33,34,35,36,37,38,39,48,49,..., dimensions={0} | all-to-all | bytes 1048576 | tf_op jit(solution)/shard_map/all_to_all | solution.py:457
  138.0 3.3 %collective-permute-start.9 = (f32[1024,128]{1,0:T(8,128)S(1)}, f32[1024,128]{1,0:T(8,128)S(1)}, u32[]{:S(2)}, u32[]{:S(2)}) collective-permute-start(f32[1024,128]{1,0:T(8,128)S(1)} %bitcast.17), channel_id=1, source_target_pairs={{0,8},{1,9},{2,10},{3,11},{4,12},{5,13},{6,14},{7,15},{8,0},{9,1},... | collective-permute-start | bytes 1572872 | tf_op jit(solution)/shard_map/ppermute | solution.py:465
  141.3 1.5 %collective-permute-done.9.other = f32[1024,128]{1,0:T(8,128)S(1)} collective-permute-done((f32[1024,128]{1,0:T(8,128)S(1)}, f32[1024,128]{1,0:T(8,128)S(1)}, u32[]{:S(2)}, u32[]{:S(2)}) %collective-permute-start.9) | collective-permute-done | bytes 524320 | tf_op jit(solution)/shard_map/ppermute | solution.py:465
  142.8 1.1 unpack.1
  (18 shorter events, 0.1 us)
Async XLA Ops:
  0.6 12.6 %copy-start.7 = (s32[8,1024]{1,0:T(8,128)S(1)}, s32[8,1024]{1,0:T(8,128)}, u32[]{:S(2)}) copy-start(s32[8,1024]{1,0:T(8,128)} %param.16) | copy-start | bytes 98308
  0.7 12.6 %copy-start.8 = (s32[8,1024]{1,0:T(8,128)S(1)}, s32[8,1024]{1,0:T(8,128)}, u32[]{:S(2)}) copy-start(s32[8,1024]{1,0:T(8,128)} %param.17) | copy-start | bytes 98308
  0.7 24.0 %copy-start = (bf16[64,128,128]{2,1,0:T(8,128)(2,1)S(1)}, bf16[64,128,128]{2,1,0:T(8,128)(2,1)}, u32[]{:S(2)}) copy-start(bf16[64,128,128]{2,1,0:T(8,128)(2,1)} %param.9) | copy-start | bytes 6291460
  0.7 24.0 %copy-start.1 = (bf16[128,512]{1,0:T(8,128)(2,1)S(1)}, bf16[128,512]{1,0:T(8,128)(2,1)}, u32[]{:S(2)}) copy-start(bf16[128,512]{1,0:T(8,128)(2,1)} %refs_9_.3) | copy-start | bytes 393220
  0.7 24.0 %copy-start.2 = (bf16[128,512]{1,0:T(8,128)(2,1)S(1)}, bf16[128,512]{1,0:T(8,128)(2,1)}, u32[]{:S(2)}) copy-start(bf16[128,512]{1,0:T(8,128)(2,1)} %refs_10_.3) | copy-start | bytes 393220
  0.7 24.0 %copy-start.3 = (bf16[512,128]{1,0:T(8,128)(2,1)S(1)}, bf16[512,128]{1,0:T(8,128)(2,1)}, u32[]{:S(2)}) copy-start(bf16[512,128]{1,0:T(8,128)(2,1)} %refs_11_.3) | copy-start | bytes 393220
  0.7 24.0 %copy-start.4 = (bf16[128,64]{0,1:T(8,128)(2,1)S(1)}, bf16[128,64]{0,1:T(8,128)(2,1)}, u32[]{:S(2)}) copy-start(bf16[128,64]{0,1:T(8,128)(2,1)} %param.15) | copy-start | bytes 49156
  0.7 24.0 %copy-start.5 = (f32[128]{0:T(128)S(1)}, f32[128]{0:T(128)}, u32[]{:S(2)}) copy-start(f32[128]{0:T(128)} %param.10) | copy-start | bytes 1540
  0.7 24.0 %copy-start.6 = (f32[128]{0:T(128)S(1)}, f32[128]{0:T(128)}, u32[]{:S(2)}) copy-start(f32[128]{0:T(128)} %param.11) | copy-start | bytes 1540
  8.7 25.9 %collective-permute-start.3 = (bf16[1024,128]{1,0:T(8,128)(2,1)S(1)}, bf16[1024,128]{1,0:T(8,128)(2,1)S(1)}, u32[]{:S(2)}, u32[]{:S(2)}) collective-permute-start(bf16[1024,128]{1,0:T(8,128)(2,1)S(1)} %get-tuple-element.31), channel_id=1, source_target_pairs={{0,64},{1,65},{2,66},{3,67},{4,68},{5,69},{6,70},{7,71},{8,72},{9,... | collective-permute-start | bytes 786440 | tf_op jit(solution)/shard_map/ppermute | solution.py:48
  11.1 24.6 %collective-permute-start.5 = (bf16[1024,128]{1,0:T(8,128)(2,1)S(1)}, bf16[1024,128]{1,0:T(8,128)(2,1)S(1)}, u32[]{:S(2)}, u32[]{:S(2)}) collective-permute-start(bf16[1024,128]{1,0:T(8,128)(2,1)S(1)} %get-tuple-element.32), channel_id=1, source_target_pairs={{0,65},{1,64},{2,67},{3,66},{4,69},{5,68},{6,71},{7,70},{8,73},{9,... | collective-permute-start | bytes 786440 | tf_op jit(solution)/shard_map/ppermute | solution.py:48
  31.7 9.0 %collective-permute-start = (bf16[1024,128]{1,0:T(8,128)(2,1)S(1)}, bf16[1024,128]{1,0:T(8,128)(2,1)S(1)}, u32[]{:S(2)}, u32[]{:S(2)}) collective-permute-start(bf16[1024,128]{1,0:T(8,128)(2,1)S(1)} %get-tuple-element.29), channel_id=1, source_target_pairs={{0,32},{1,33},{2,34},{3,35},{4,36},{5,37},{6,38},{7,39},{8,40},{9,... | collective-permute-start | bytes 786440 | tf_op jit(solution)/shard_map/ppermute | solution.py:48
  34.6 12.0 %collective-permute-start.4 = (bf16[1024,128]{1,0:T(8,128)(2,1)S(1)}, bf16[1024,128]{1,0:T(8,128)(2,1)S(1)}, u32[]{:S(2)}, u32[]{:S(2)}) collective-permute-start(bf16[1024,128]{1,0:T(8,128)(2,1)S(1)} %collective-permute-done.3), channel_id=1, source_target_pairs={{64,0},{65,16},{66,32},{67,48},{68,64},{69,80},{70,96},{71,112},{7... | collective-permute-start | bytes 786440 | tf_op jit(solution)/shard_map/ppermute | solution.py:49
  35.7 10.9 %collective-permute-start.6 = (bf16[1024,128]{1,0:T(8,128)(2,1)S(1)}, bf16[1024,128]{1,0:T(8,128)(2,1)S(1)}, u32[]{:S(2)}, u32[]{:S(2)}) collective-permute-start(bf16[1024,128]{1,0:T(8,128)(2,1)S(1)} %collective-permute-done.5), channel_id=1, source_target_pairs={{65,0},{64,16},{67,32},{66,48},{69,64},{68,80},{71,96},{70,112},{7... | collective-permute-start | bytes 786440 | tf_op jit(solution)/shard_map/ppermute | solution.py:49
  36.5 10.2 %collective-permute-start.7 = (s32[64,128]{1,0:T(8,128)S(1)}, s32[64,128]{1,0:T(8,128)S(1)}, u32[]{:S(2)}, u32[]{:S(2)}) collective-permute-start(s32[64,128]{1,0:T(8,128)S(1)} %bitcast.20), channel_id=1, source_target_pairs={{0,0},{1,16},{2,32},{3,48},{4,64},{5,80},{6,96},{7,112},{8,8},{9,2... | collective-permute-start | bytes 98312 | tf_op jit(solution)/shard_map/ppermute | solution.py:47
  37.1 23.4 %collective-permute-start.2 = (bf16[1088,128]{1,0:T(8,128)(2,1)S(1)}, bf16[1088,128]{1,0:T(8,128)(2,1)S(1)}, u32[]{:S(2)}, u32[]{:S(2)}) collective-permute-start(bf16[1088,128]{1,0:T(8,128)(2,1)S(1)} %get-tuple-element.30), channel_id=1, source_target_pairs={{0,8},{1,24},{2,40},{3,56},{4,72},{5,88},{6,104},{7,120},{8,0},{9,... | collective-permute-start | bytes 835592 | tf_op jit(solution)/shard_map/ppermute | solution.py:47
  40.7 19.8 %collective-permute-start.1 = (bf16[1024,128]{1,0:T(8,128)(2,1)S(1)}, bf16[1024,128]{1,0:T(8,128)(2,1)S(1)}, u32[]{:S(2)}, u32[]{:S(2)}) collective-permute-start(bf16[1024,128]{1,0:T(8,128)(2,1)S(1)} %collective-permute-done), channel_id=1, source_target_pairs={{32,8},{33,24},{34,40},{35,56},{36,72},{37,88},{38,104},{39,120},{... | collective-permute-start | bytes 786440 | tf_op jit(solution)/shard_map/ppermute | solution.py:49
  74.6 4.2 %collective-permute-start.8 = (f32[1024,128]{1,0:T(8,128)S(1)}, f32[1024,128]{1,0:T(8,128)S(1)}, u32[]{:S(2)}, u32[]{:S(2)}) collective-permute-start(f32[1024,128]{1,0:T(8,128)S(1)} %get-tuple-element.38), channel_id=1, source_target_pairs={{0,8},{1,9},{2,10},{3,11},{4,12},{5,13},{6,14},{7,15},{8,0},{9,1},... | collective-permute-start | bytes 1572872 | tf_op jit(solution)/shard_map/ppermute | solution.py:452
  138.0 4.9 %collective-permute-start.9 = (f32[1024,128]{1,0:T(8,128)S(1)}, f32[1024,128]{1,0:T(8,128)S(1)}, u32[]{:S(2)}, u32[]{:S(2)}) collective-permute-start(f32[1024,128]{1,0:T(8,128)S(1)} %bitcast.17), channel_id=1, source_target_pairs={{0,8},{1,9},{2,10},{3,11},{4,12},{5,13},{6,14},{7,15},{8,0},{9,1},... | collective-permute-start | bytes 1572872 | tf_op jit(solution)/shard_map/ppermute | solution.py:465
